TPU v7x, 512 devices: a whole 4x8x8 slice. The times are simulated.
512 devices in a mesh: pts: 128 (over z, y, core), ch: 4 (over x).
Axes of the slice: x: 4, y: 8, z: 8, core: 2. Of those that a mesh axis runs over, the one named last changes fastest.
Arguments:
- points_in: bfloat16 [65536, 256], P('pts'), may hold values from -6 to 6
- neighbor_offsets: int32 [65536, 16], P('pts'), may hold values from -128 to 128, as said below
- kernel_ids: int32 [65536, 16], P('pts'), may hold values from 0 to 26
- cluster_ids: int32 [65536], P('pts'), may hold values from 0 to 16383, as said below
- owners: int32 [65536], P('pts'), may hold values from 0 to 127, as said below
- conv_weight: bfloat16 [27, 256], replicated, may hold values from -1.5 to 1.5
- norm_gain: float32 [256], replicated, may hold values from 0.1 to 1.9
- norm_bias: float32 [256], replicated, may hold values from -3 to 3
- qkv_weight: bfloat16 [3, 256, 256], P(None, None, 'ch'), may hold values from -20 to 20
- proj_weight: bfloat16 [256, 256], replicated, may hold values from -1.5 to 1.5
- pool_weight: bfloat16 [256, 512], P(None, 'ch'), may hold values from -0.375 to 0.375
Outputs:
- block_out: bfloat16 [65536, 256], P('pts', 'ch')
- pooled: bfloat16 [16384, 512], P('pts', 'ch')
Inputs may be any that keep to these rules, and one draw needn't show every extreme that they name: `owners`: each device's points name every owner at most 8 times; in every draw one owner is named exactly 8 times by the points of every device. `cluster_ids`: cluster ids never fall along the points, every cluster holds one or more points, the points of device i belong to clusters i * 128 - 1 .. i * 128 + 127, and only the first 1 to 3 points of a device (none on device 0) lie in cluster i * 128 - 1; some device has exactly 3 such points. `neighbor_offsets`: offsets -128 and 128 both occur.
All inputs are finite; a program needn't handle non-finite values.
Results may differ from a plain program's by a relative error of at most 0.017.
Values may be sent and summed in bfloat16 or wider, within the bound.
No kernel may reach another device: no remote copies, remote signals or barrier semaphores. Data moves between devices by JAX's collectives and lax.ppermute only.
A program may use at most 64 MiB of HBM per device.

v0:
```python
import math

import jax
import jax.numpy as jnp
from jax import lax
from jax.sharding import PartitionSpec as P

HD = 32
PATCH = 1024
G = 128


def padded_2(value, sides, width):
    for axis, dim in sides:
        devices, length = (lax.axis_size(axis), value.shape[dim])
        up = [(i, (i + 1) % devices) for i in range(devices - 1)]
        down = [(j, i) for i, j in up]
        last = lax.slice_in_dim(value, length - width, length, axis=dim)
        initial = lax.slice_in_dim(value, 0, width, axis=dim)
        before = lax.ppermute(last, axis, up)
        after = lax.ppermute(initial, axis, down)
        value = jnp.concatenate([before, value, after], axis=dim)
    return value


def from_behind(value, axis, by):
    devices = lax.axis_size(axis)
    pairs = [(i, i + by) for i in range(devices) if 0 <= i + by < devices]
    return lax.ppermute(value, axis, pairs)


def attend_patches(packed_rows, live_slots, heads_here):
    slot_total = packed_rows.shape[0]
    patch_count = slot_total // PATCH
    head_cols = packed_rows.shape[1] // 3
    head_size = head_cols // heads_here
    score_scale = 1.0 / math.sqrt(head_size)
    patch_cube = packed_rows.reshape(patch_count, PATCH, 3, heads_here, head_size)
    key_alive = live_slots.reshape(patch_count, PATCH)

    def one_patch(operands):
        patch_rows, alive_keys = operands
        queries = patch_rows[:, 0]
        key_rows = patch_rows[:, 1]
        value_rows = patch_rows[:, 2]
        scores = (
            jnp.einsum("qhd,khd->hqk", queries, key_rows, preferred_element_type=jnp.float32)
            * score_scale
        )
        scores = jnp.where(alive_keys[None, None, :], scores, -1e30)
        row_max = jnp.max(scores, axis=-1, keepdims=True)
        exponent = jnp.exp(scores - row_max)
        denominator = jnp.sum(exponent, axis=-1)
        summed = jnp.einsum(
            "hqk,khd->qhd",
            exponent.astype(jnp.bfloat16),
            value_rows,
            preferred_element_type=jnp.float32,
        )
        return (summed / jnp.transpose(denominator)[:, :, None]).astype(jnp.bfloat16)

    attended = lax.map(one_patch, (patch_cube, key_alive))
    return attended.reshape(slot_total, head_cols)


def shards(
    points_in,
    neighbor_offsets,
    kernel_ids,
    cluster_ids,
    owners,
    conv_weight,
    norm_gain,
    norm_bias,
    qkv_weight,
    proj_weight,
    pool_weight,
):
    point_rows = points_in.shape[0]
    feature_count = points_in.shape[1]
    node_count = lax.axis_size("pts")
    my_index = lax.axis_index("pts")
    channel_index = lax.axis_index("ch")
    capacity = 2 * point_rows // node_count
    slot_total = capacity * node_count
    head_cols = qkv_weight.shape[2]
    heads_here = head_cols // HD
    padded = padded_2(points_in, (("pts", 0),), G)
    offsets_base = jnp.arange(point_rows, dtype=jnp.int32) + G
    kind_ids = jnp.arange(conv_weight.shape[0], dtype=jnp.int32)
    conv = jnp.zeros((point_rows, feature_count), jnp.float32)
    for neighbor_slot in range(neighbor_offsets.shape[1]):
        selector = (kernel_ids[:, neighbor_slot][:, None] == kind_ids[None, :]).astype(jnp.bfloat16)
        weights_here = jnp.dot(selector, conv_weight, preferred_element_type=jnp.float32)
        picked = padded[offsets_base + neighbor_offsets[:, neighbor_slot]]
        conv = conv + weights_here * picked.astype(jnp.float32)
    residual_rows = (points_in.astype(jnp.float32) + conv).astype(jnp.bfloat16)
    features = residual_rows.astype(jnp.float32)
    average = jnp.mean(features, axis=1, keepdims=True)
    centered = features - average
    variance = jnp.mean(centered * centered, axis=1, keepdims=True)
    normed_rows = (centered / jnp.sqrt(variance + 1e-05) * norm_gain + norm_bias).astype(
        jnp.bfloat16
    )
    flat_weight = jnp.transpose(qkv_weight, (1, 0, 2)).reshape(feature_count, 3 * head_cols)
    peer_ids = jnp.arange(node_count, dtype=jnp.int32)
    dest_marks = (owners[:, None] == peer_ids[None, :]).astype(jnp.int32)
    earlier_count = jnp.cumsum(dest_marks, axis=0) - dest_marks
    slot_index = jnp.sum(earlier_count * dest_marks, axis=1)
    send_counts = jnp.sum(dest_marks, axis=0).reshape(node_count, 1)
    position = owners * capacity + slot_index
    projected = jnp.dot(normed_rows, flat_weight, preferred_element_type=jnp.float32).astype(
        jnp.bfloat16
    )
    outgoing = (
        jnp.zeros((slot_total, projected.shape[1]), projected.dtype)
        .at[position]
        .set(projected)
        .reshape(node_count, capacity * 3 * head_cols)
    )
    arrived, incoming_counts = (
        lax.all_to_all(outgoing, "pts", split_axis=0, concat_axis=0, tiled=True),
        lax.all_to_all(send_counts, "pts", split_axis=0, concat_axis=0, tiled=True),
    )
    packed_rows = arrived.reshape(slot_total, 3 * head_cols)
    live_slots = (jnp.arange(capacity, dtype=jnp.int32)[None, :] < incoming_counts).reshape(
        slot_total
    )
    attended = attend_patches(packed_rows, live_slots, heads_here)
    returned_rows = lax.all_to_all(
        attended.reshape(node_count, capacity * head_cols),
        "pts",
        split_axis=0,
        concat_axis=0,
        tiled=True,
    )
    returned = returned_rows.reshape(slot_total, head_cols)[position]
    projected_sum = jnp.dot(
        lax.all_gather(returned, "ch", axis=1, tiled=True),
        proj_weight,
        preferred_element_type=jnp.float32,
    )
    full_out = (residual_rows.astype(jnp.float32) + projected_sum).astype(jnp.bfloat16)
    block_out = lax.dynamic_slice_in_dim(full_out, channel_index * head_cols, head_cols, 1)
    lifted_rows = jnp.dot(full_out, pool_weight, preferred_element_type=jnp.float32)
    cluster_count = point_rows // 4
    local_cluster = cluster_ids - my_index * cluster_count + 1
    cluster_sums = jax.ops.segment_sum(lifted_rows, local_cluster, num_segments=cluster_count + 1)
    point_counts = jax.ops.segment_sum(
        jnp.ones((point_rows,), jnp.float32), local_cluster, num_segments=cluster_count + 1
    )
    spill_sum, spill_count = from_behind((cluster_sums[:1], point_counts[:1]), "pts", -1)
    own_sums = cluster_sums[1:].at[cluster_count - 1].add(spill_sum[0])
    own_counts = point_counts[1:].at[cluster_count - 1].add(spill_count[0])
    pooled = jax.nn.gelu(own_sums / own_counts[:, None], approximate=False).astype(jnp.bfloat16)
    return (block_out, pooled)


def solution(mesh):
    return jax.shard_map(
        shards,
        mesh=mesh,
        in_specs=(
            P("pts", None),
            P("pts", None),
            P("pts", None),
            P("pts"),
            P("pts"),
            P(),
            P(),
            P(),
            P(None, None, "ch"),
            P(),
            P(None, "ch"),
        ),
        out_specs=(P("pts", "ch"), P("pts", "ch")),
        check_vma=False,
    )
```

profile of v0, /device:TPU:1, one launch (start us, length us, event | category | flops | bytes accessed | tf_op | source)
XLA Modules:
  0.0 208.5 jit_solution(9440661710691054107)
XLA Ops:
  0.7 0.9 fusion.87
  1.6 4.6 %collective-permute-start = (bf16[128,256]{1,0:T(8,128)(2,1)S(1)}, bf16[128,256]{1,0:T(8,128)(2,1)S(1)}, u32[]{:S(2)}, u32[]{:S(2)}) collective-permute-start(bf16[128,256]{1,0:T(8,128)(2,1)S(1)} %get-tuple-element.46), channel_id=1, source_target_pairs={{0,4},{4,8},{8,12},{12,16},{16,20},{20,24},{24,28},{28,32},{32,36}... | collective-permute-start | bytes 196616 | tf_op jit(solution)/shard_map/ppermute | solution.py:20
  6.2 5.5 %collective-permute-start.1 = (bf16[128,256]{1,0:T(8,128)(2,1)S(1)}, bf16[128,256]{1,0:T(8,128)(2,1)S(1)}, u32[]{:S(2)}, u32[]{:S(2)}) collective-permute-start(bf16[128,256]{1,0:T(8,128)(2,1)S(1)} %get-tuple-element.45), channel_id=1, source_target_pairs={{4,0},{8,4},{12,8},{16,12},{20,16},{24,20},{28,24},{32,28},{36,32}... | collective-permute-start | bytes 196616 | tf_op jit(solution)/shard_map/ppermute | solution.py:21
  12.8 0.9 convert_reduce_fusion.1
  14.4 15.5 %all-to-all-start.1 = ((s32[128,1,1]{2,1,0:T(1,128)}), s32[128,1,1]{2,1,0:T(1,128)S(1)}, u32[]{:S(2)}, u32[]{:S(2)}) async-start(s32[128,1,1]{2,1,0:T(1,128)} %copy.107), calls=%async_computation.1 | async-start | bytes 131072 | tf_op jit(solution)/shard_map/all_to_all | solution.py:123
  29.9 1.8 copy.85
  31.7 1.2 compare_select_fusion.15
  32.9 1.1 fusion.88
  34.0 1.1 fusion.33
  35.1 1.1 fusion.34
  36.1 1.1 fusion.35
  37.2 1.1 fusion.36
  38.3 1.1 fusion.37
  39.4 1.9 fusion.38
  41.2 1.9 fusion.39
  43.1 1.9 fusion.40
  45.0 1.9 fusion.41
  46.8 1.9 fusion.42
  48.7 1.9 fusion.43
  50.6 1.1 fusion.44
  51.7 1.2 fusion.45
  52.9 1.2 fusion.46
  54.0 1.2 fusion.47
  55.2 1.1 fusion.48
  60.6 2.1 %gather_fusion.14 = bf16[512,256]{1,0:T(8,128)(2,1)S(1)} fusion(bf16[768,256]{1,0:T(8,128)(2,1)S(1)} %constant_dynamic-update-slice_fusion, s32[1024]{0:T(1024)} %get-tuple-element.82), kind=kCustom, calls=%fused_computation.14 | custom fusion | bytes 526336 | tf_op jit(solution)/shard_map/gather | solution.py:95
  63.6 2.2 %gather_fusion.15 = bf16[512,256]{1,0:T(8,128)(2,1)S(1)} fusion(bf16[768,256]{1,0:T(8,128)(2,1)S(1)} %constant_dynamic-update-slice_fusion, s32[1024]{0:T(1024)} %get-tuple-element.81), kind=kCustom, calls=%fused_computation.15 | custom fusion | bytes 526336 | tf_op jit(solution)/shard_map/gather | solution.py:95
  66.7 2.2 %gather_fusion = bf16[512,256]{1,0:T(8,128)(2,1)S(1)} fusion(bf16[768,256]{1,0:T(8,128)(2,1)S(1)} %constant_dynamic-update-slice_fusion, s32[1024]{0:T(1024)} %get-tuple-element.96), kind=kCustom, calls=%fused_computation | custom fusion | bytes 526336 | tf_op jit(solution)/shard_map/gather | solution.py:95
  69.7 1.9 gather_fusion.1
  72.5 1.9 gather_fusion.2
  75.4 1.9 gather_fusion.3
  78.2 1.9 gather_fusion.4
  81.0 1.9 gather_fusion.5
  83.7 1.9 gather_fusion.6
  86.6 2.4 %gather_fusion.7 = bf16[512,256]{1,0:T(8,128)(2,1)S(1)} fusion(bf16[768,256]{1,0:T(8,128)(2,1)S(1)} %constant_dynamic-update-slice_fusion, s32[1024]{0:T(1024)S(1)} %copy-done.7), kind=kCustom, calls=%fused_computation.7 | custom fusion | bytes 526336 | tf_op jit(solution)/shard_map/gather | solution.py:95
  89.8 1.9 gather_fusion.8
  92.6 1.9 gather_fusion.9
  95.4 1.9 gather_fusion.10
  98.2 1.9 gather_fusion.11
  100.2 0.9 copy.97
  101.1 1.9 gather_fusion.12
  103.9 1.9 gather_fusion.13
  106.0 5.0 %convert_reduce_fusion = (f32[512]{0:T(512)S(1)}, bf16[512,256]{0,1:T(8,128)(2,1)S(1)}) fusion(f32[512,256]{0,1:T(8,128)} %fusion.48, bf16[512,256]{0,1:T(8,128)(2,1)} %copy.101, f32[512,256]{0,1:T(8,128)} %fusion.47, bf16[512,256]{0,1:T(8,128)(2,1)} %copy.100, f32[512,256]{0,1:T(8,128)} %fusion.46, bf16[512,256]{0,1:T(8,128)(2,1)S(1)} %copy.99, ...), kind=kLoop, calls=%fused_computation.34 | loop fusion | flops 6815232 | bytes 13109248 | tf_op jit(solution)/shard_map/reduce_sum | solution.py:99
  111.6 2.5 %scatter_custom_fusion = bf16[1024,192]{1,0:T(8,128)(2,1)S(1)} fusion(s32[512]{0:T(512)S(1)} %copy-done.14, bf16[512,192]{1,0:T(8,128)(2,1)S(1)} %copy.104, bf16[]{:T(256)} %constant.131.clone.1), kind=kCustom, calls=%fused_computation.54 | custom fusion | bytes 393218 | tf_op jit(solution)/shard_map/scatter | solution.py:118
  115.3 3.0 %reduce.7 = bf16[128,1536]{1,0:T(8,128)(2,1)S(1)} reduce(bf16[128,1,1536]{2,1,0:T(2,128)(2,1)S(1)} %all_to_all.24, bf16[]{:T(256)} %broadcast.271), dimensions={1}, to_apply=%all_to_all.24.reduce_sub_computation | reduce | bytes 786434 | tf_op jit(solution)/shard_map/all_to_all | solution.py:122
  119.2 14.0 %all-to-all-start = ((bf16[128,2,768]{2,1,0:T(2,128)(2,1)}), bf16[128,2,768]{2,1,0:T(2,128)(2,1)S(1)}, u32[]{:S(2)}, u32[]{:S(2)}) async-start(bf16[128,2,768]{2,1,0:T(2,128)(2,1)} %reshape.325), calls=%async_computation | async-start | bytes 786432 | tf_op jit(solution)/shard_map/all_to_all | solution.py:122
  133.2 2.4 %reduce.5 = s32[128]{0:T(128)S(1)} reduce(s32[128,1,1]{2,1,0:T(1,128)S(1)} %all-to-all-done.1, s32[]{:T(128)} %constant.129.clone.1), dimensions={1,2}, to_apply=%all_to_all.21.reduce_sub_computation | reduce | bytes 1028 | tf_op jit(solution)/shard_map/all_to_all | solution.py:123
  135.8 15.2 %all-to-all-done = bf16[128,2,768]{2,1,0:T(2,128)(2,1)S(1)} async-done(((bf16[128,2,768]{2,1,0:T(2,128)(2,1)}), bf16[128,2,768]{2,1,0:T(2,128)(2,1)S(1)}, u32[]{:S(2)}, u32[]{:S(2)}) %all-to-all-start) | async-done | bytes 393248 | tf_op jit(solution)/shard_map/all_to_all | solution.py:122
  151.2 2.4 %reduce.4 = bf16[128,1536]{1,0:T(8,128)(2,1)S(1)} reduce(bf16[128,1,1536]{2,1,0:T(2,128)(2,1)S(1)} %reshape.326, bf16[]{:T(256)} %constant.176), dimensions={1}, to_apply=%all_to_all.19.reduce_sub_computation | reduce | bytes 786434 | tf_op jit(solution)/shard_map/all_to_all | solution.py:122
  153.6 1.0 squeeze.15
  154.6 1.1 fusion.86
  156.8 1.7 fusion
  158.5 2.4 %fusion.1 = f32[2,1024]{1,0:T(2,128)S(1)} fusion(f32[2,1024,1024]{1,2,0:T(8,128)S(1)} %get-tuple-element.80, f32[2,1024]{1,0:T(2,128)S(1)} %get-tuple-element.79, pred[1024]{0:T(1024)(128)(4,1)S(1)} %lt.115), kind=kLoop, calls=%fused_computation.23 | loop fusion | flops 8386560 | bytes 8406016 | tf_op jit(solution)/shard_map/while/body/eval_jaxpr/reduce_sum | solution.py:53
  160.9 1.9 fusion.13
  163.8 1.4 reduce.8
  165.9 5.5 %all-to-all-start.2 = ((bf16[128,2,256]{2,1,0:T(2,128)(2,1)}), bf16[128,2,256]{2,1,0:T(2,128)(2,1)S(1)}, u32[]{:S(2)}, u32[]{:S(2)}) async-start(bf16[128,2,256]{2,1,0:T(2,128)(2,1)} %reshape.327), calls=%async_computation.2 | async-start | bytes 262144 | tf_op jit(solution)/shard_map/all_to_all | solution.py:130
  171.4 4.1 %scatter_custom_fusion.2 = f32[129]{0:T(256)S(1)} fusion(s32[512]{0:T(512)S(1)} %subtract_add_fusion, f32[512]{0:T(512)S(1)} %broadcast.149, f32[]{:T(128)} %constant.134.clone.1), kind=kCustom, calls=%fused_computation.176 | custom fusion | flops 512 | bytes 520 | tf_op jit(solution)/shard_map/scatter-add | solution.py:149
  176.0 2.9 %collective-permute-start.3 = (f32[1]{0:T(128)}, f32[1]{0:T(128)}, u32[]{:S(2)}, u32[]{:S(2)}) collective-permute-start(f32[1]{0:T(128)} %slice.207), channel_id=1, source_target_pairs={{4,0},{8,4},{12,8},{16,12},{20,16},{24,20},{28,24},{32,28},{36,32}... | collective-permute-start | bytes 20 | tf_op jit(solution)/shard_map/ppermute | solution.py:29
  179.0 2.0 collective-permute-done.3
  181.6 2.6 %all-to-all-done.2 = bf16[128,2,256]{2,1,0:T(2,128)(2,1)S(1)} async-done(((bf16[128,2,256]{2,1,0:T(2,128)(2,1)}), bf16[128,2,256]{2,1,0:T(2,128)(2,1)S(1)}, u32[]{:S(2)}, u32[]{:S(2)}) %all-to-all-start.2) | async-done | bytes 131104 | tf_op jit(solution)/shard_map/all_to_all | solution.py:130
  185.2 1.3 gather_fusion.16
  186.7 10.2 %all-gather = bf16[512,256]{0,1:T(8,128)(2,1)S(1)} all-gather(bf16[512,64]{0,1:T(8,128)(2,1)S(1)} %copy.113), channel_id=2, replica_groups=mesh['pts'=128,'ch'=4] {'ch'}, dimensions={1}, use_global_device_ids=true | all-gather | bytes 327680 | tf_op jit(solution)/shard_map/all_gather | solution.py:139
  197.5 3.5 %scatter_custom_fusion.1 = f32[129,128]{1,0:T(8,128)S(1)} fusion(s32[512]{0:T(512)S(1)} %subtract_add_fusion, f32[512,128]{1,0:T(8,128)S(1)} %fusion.89, f32[]{:T(128)} %constant.134.clone.1), kind=kCustom, calls=%fused_computation.130 | custom fusion | flops 65536 | bytes 66052 | tf_op jit(solution)/shard_map/scatter-add | solution.py:148
  201.0 4.7 %collective-permute-start.2 = (f32[1,128]{1,0:T(1,128)S(1)}, f32[1,128]{1,0:T(1,128)S(1)}, u32[]{:S(2)}, u32[]{:S(2)}) collective-permute-start(f32[1,128]{1,0:T(1,128)S(1)} %slice.248), channel_id=1, source_target_pairs={{4,0},{8,4},{12,8},{16,12},{20,16},{24,20},{28,24},{32,28},{36,32}... | collective-permute-start | bytes 1544 | tf_op jit(solution)/shard_map/ppermute | solution.py:29
  206.3 1.0 collective-permute-done.2
  (112 shorter events, 28.3 us)
Async XLA Ops:
  0.6 196.3 %copy-start = (bf16[256,256]{1,0:T(8,128)(2,1)S(1)}, bf16[256,256]{1,0:T(8,128)(2,1)}, u32[]{:S(2)}) copy-start(bf16[256,256]{1,0:T(8,128)(2,1)} %param.24) | copy-start | bytes 393220
  0.6 55.7 %copy-start.4 = (s32[512]{0:T(512)S(1)}, s32[512]{0:T(512)}, u32[]{:S(2)}) copy-start(s32[512]{0:T(512)} %param.19) | copy-start | bytes 6148
  0.7 49.9 %copy-start.1 = (bf16[27,256]{1,0:T(8,128)(2,1)S(1)}, bf16[27,256]{1,0:T(8,128)(2,1)}, u32[]{:S(2)}) copy-start(bf16[27,256]{1,0:T(8,128)(2,1)} %param.20) | copy-start | bytes 41476
  1.6 58.9 %collective-permute-start = (bf16[128,256]{1,0:T(8,128)(2,1)S(1)}, bf16[128,256]{1,0:T(8,128)(2,1)S(1)}, u32[]{:S(2)}, u32[]{:S(2)}) collective-permute-start(bf16[128,256]{1,0:T(8,128)(2,1)S(1)} %get-tuple-element.46), channel_id=1, source_target_pairs={{0,4},{4,8},{8,12},{12,16},{16,20},{20,24},{24,28},{28,32},{32,36}... | collective-permute-start | bytes 196616 | tf_op jit(solution)/shard_map/ppermute | solution.py:20
  6.2 54.4 %collective-permute-start.1 = (bf16[128,256]{1,0:T(8,128)(2,1)S(1)}, bf16[128,256]{1,0:T(8,128)(2,1)S(1)}, u32[]{:S(2)}, u32[]{:S(2)}) collective-permute-start(bf16[128,256]{1,0:T(8,128)(2,1)S(1)} %get-tuple-element.45), channel_id=1, source_target_pairs={{4,0},{8,4},{12,8},{16,12},{20,16},{24,20},{28,24},{32,28},{36,32}... | collective-permute-start | bytes 196616 | tf_op jit(solution)/shard_map/ppermute | solution.py:21
  14.4 104.7 %all-to-all-start.1 = ((s32[128,1,1]{2,1,0:T(1,128)}), s32[128,1,1]{2,1,0:T(1,128)S(1)}, u32[]{:S(2)}, u32[]{:S(2)}) async-start(s32[128,1,1]{2,1,0:T(1,128)} %copy.107), calls=%async_computation.1 | async-start | bytes 131072 | tf_op jit(solution)/shard_map/all_to_all | solution.py:123
  31.7 28.8 %copy-start.2 = (bf16[512,256]{1,0:T(8,128)(2,1)S(1)}, bf16[512,256]{1,0:T(8,128)(2,1)}, u32[]{:S(2)}) copy-start(bf16[512,256]{1,0:T(8,128)(2,1)} %param.15) | copy-start | bytes 786436
  60.6 9.2 %copy-start.13 = (s32[1024]{0:T(1024)S(1)}, s32[1024]{0:T(1024)}, u32[]{:S(2)}) copy-start(s32[1024]{0:T(1024)} %get-tuple-element.95) | copy-start | bytes 12292
  60.6 12.0 %copy-start.12 = (s32[1024]{0:T(1024)S(1)}, s32[1024]{0:T(1024)}, u32[]{:S(2)}) copy-start(s32[1024]{0:T(1024)} %get-tuple-element.94) | copy-start | bytes 12292
  60.6 14.8 %copy-start.11 = (s32[1024]{0:T(1024)S(1)}, s32[1024]{0:T(1024)}, u32[]{:S(2)}) copy-start(s32[1024]{0:T(1024)} %get-tuple-element.93) | copy-start | bytes 12292
  60.6 17.5 %copy-start.10 = (s32[1024]{0:T(1024)S(1)}, s32[1024]{0:T(1024)}, u32[]{:S(2)}) copy-start(s32[1024]{0:T(1024)} %get-tuple-element.92) | copy-start | bytes 12292
  63.6 17.4 %copy-start.9 = (s32[1024]{0:T(1024)S(1)}, s32[1024]{0:T(1024)}, u32[]{:S(2)}) copy-start(s32[1024]{0:T(1024)} %get-tuple-element.91) | copy-start | bytes 12292
  66.7 17.1 %copy-start.8 = (s32[1024]{0:T(1024)S(1)}, s32[1024]{0:T(1024)}, u32[]{:S(2)}) copy-start(s32[1024]{0:T(1024)} %get-tuple-element.90) | copy-start | bytes 12292
  69.7 16.8 %copy-start.7 = (s32[1024]{0:T(1024)S(1)}, s32[1024]{0:T(1024)}, u32[]{:S(2)}) copy-start(s32[1024]{0:T(1024)} %get-tuple-element.89) | copy-start | bytes 12292
  72.5 17.3 %copy-start.6 = (s32[1024]{0:T(1024)S(1)}, s32[1024]{0:T(1024)}, u32[]{:S(2)}) copy-start(s32[1024]{0:T(1024)} %get-tuple-element.88) | copy-start | bytes 12292
  75.4 17.3 %copy-start.5 = (s32[1024]{0:T(1024)S(1)}, s32[1024]{0:T(1024)}, u32[]{:S(2)}) copy-start(s32[1024]{0:T(1024)} %get-tuple-element.87) | copy-start | bytes 12292
  103.0 8.1 %copy-start.17 = (f32[256]{0:T(256)S(1)}, f32[256]{0:T(256)}, u32[]{:S(2)}) copy-start(f32[256]{0:T(256)} %param.22) | copy-start | bytes 3076
  103.0 8.1 %copy-start.18 = (f32[256]{0:T(256)S(1)}, f32[256]{0:T(256)}, u32[]{:S(2)}) copy-start(f32[256]{0:T(256)} %param.21) | copy-start | bytes 3076
  105.9 5.3 %copy-start.16 = (bf16[3,256,64]{1,2,0:T(8,128)(2,1)S(1)}, bf16[3,256,64]{1,2,0:T(8,128)(2,1)}, u32[]{:S(2)}) copy-start(bf16[3,256,64]{1,2,0:T(8,128)(2,1)} %param.23) | copy-start | bytes 294916
  105.9 5.7 %copy-start.14 = (s32[512]{0:T(512)S(1)}, s32[512]{0:T(512)}, u32[]{:S(2)}) copy-start(s32[512]{0:T(512)} %compare_select_fusion.16) | copy-start | bytes 6148
  119.2 31.8 %all-to-all-start = ((bf16[128,2,768]{2,1,0:T(2,128)(2,1)}), bf16[128,2,768]{2,1,0:T(2,128)(2,1)S(1)}, u32[]{:S(2)}, u32[]{:S(2)}) async-start(bf16[128,2,768]{2,1,0:T(2,128)(2,1)} %reshape.325), calls=%async_computation | async-start | bytes 786432 | tf_op jit(solution)/shard_map/all_to_all | solution.py:122
  160.9 10.4 %copy-start.15 = (s32[512]{0:T(512)S(1)}, s32[512]{0:T(512)}, u32[]{:S(2)}) copy-start(s32[512]{0:T(512)} %param.18) | copy-start | bytes 6148
  160.9 36.2 %copy-start.3 = (bf16[256,128]{1,0:T(8,128)(2,1)S(1)}, bf16[256,128]{1,0:T(8,128)(2,1)}, u32[]{:S(2)}) copy-start(bf16[256,128]{1,0:T(8,128)(2,1)} %param.25) | copy-start | bytes 196612
  165.9 18.3 %all-to-all-start.2 = ((bf16[128,2,256]{2,1,0:T(2,128)(2,1)}), bf16[128,2,256]{2,1,0:T(2,128)(2,1)S(1)}, u32[]{:S(2)}, u32[]{:S(2)}) async-start(bf16[128,2,256]{2,1,0:T(2,128)(2,1)} %reshape.327), calls=%async_computation.2 | async-start | bytes 262144 | tf_op jit(solution)/shard_map/all_to_all | solution.py:130
  176.0 5.0 %collective-permute-start.3 = (f32[1]{0:T(128)}, f32[1]{0:T(128)}, u32[]{:S(2)}, u32[]{:S(2)}) collective-permute-start(f32[1]{0:T(128)} %slice.207), channel_id=1, source_target_pairs={{4,0},{8,4},{12,8},{16,12},{20,16},{24,20},{28,24},{32,28},{36,32}... | collective-permute-start | bytes 20 | tf_op jit(solution)/shard_map/ppermute | solution.py:29
  201.0 6.4 %collective-permute-start.2 = (f32[1,128]{1,0:T(1,128)S(1)}, f32[1,128]{1,0:T(1,128)S(1)}, u32[]{:S(2)}, u32[]{:S(2)}) collective-permute-start(f32[1,128]{1,0:T(1,128)S(1)} %slice.248), channel_id=1, source_target_pairs={{4,0},{8,4},{12,8},{16,12},{20,16},{24,20},{28,24},{32,28},{36,32}... | collective-permute-start | bytes 1544 | tf_op jit(solution)/shard_map/ppermute | solution.py:29
where the time goes:
time: 213 us; the launch traced here: 208 us
  local copies, waits for them, and re-layouts  63.5 us (30%)
  starting transfers between devices  52.6 us (25%)
  other arithmetic  33.1 us (16%)
  matrix products  26.8 us (13%)
  waiting for transfers between devices  20.8 us (10%)
  blocking collectives  10.2 us (5%)
    gather x32, local copies, waits for them, and re-layouts, shards(): picked = padded[offsets_base + neighbor_offsets[:, neighbor_slot]]  45.2 us
    dot_general x16, matrix products, shards(): jnp.dot(selector, conv_weight, preferred_element_type=jnp.float32)  22.3 us
    all_to_all x1, starting transfers between devices, shards(): lax.all_to_all(send_counts, 'pts', split_axis=0, concat_axis=0, tiled=True)  15.5 us
    all_to_all x1, waiting for transfers between devices, shards(): lax.all_to_all(outgoing, 'pts', split_axis=0, concat_axis=0, tiled=True)  15.2 us
    all_to_all x1, starting transfers between devices, shards(): lax.all_to_all(outgoing, 'pts', split_axis=0, concat_axis=0, tiled=True)  14 us
    all_gather x1, blocking collectives, shards(): lax.all_gather(returned, 'ch', axis=1, tiled=True)  10.2 us
    ppermute x2, starting transfers between devices, from_behind(): return lax.ppermute(value, axis, pairs)  7.59 us
    ppermute x1, starting transfers between devices, padded_2(): after = lax.ppermute(initial, axis, down)  5.46 us
  transfers between devices with their start and end apart: 7, of which 4 were waited for; matrix products, arithmetic and copies ran while one was open for 48% of the time, Pallas kernels for 0%

commit v1 on v0

v1 whole, which is shorter than its diff:
```python
import functools
import math

import jax
import jax.numpy as jnp
from jax import lax
from jax.experimental import pallas as pl
from jax.experimental.pallas import tpu as pltpu
from jax.sharding import PartitionSpec as P

HD = 32
G = 128
ROWS = 128
HALF_SLOTS = 4
DEAD = -1e30
BF = jnp.bfloat16
F32 = jnp.float32
VMEM_BYTES = 24 * 1024 * 1024


def call(body, outs, scratch=(), flops=0, nbytes=0, name=None):
    def run(*args):
        return pl.pallas_call(
            body,
            out_shape=outs,
            in_specs=[pl.BlockSpec(memory_space=pltpu.VMEM)] * len(args),
            out_specs=jax.tree.map(lambda _: pl.BlockSpec(memory_space=pltpu.VMEM), outs),
            scratch_shapes=list(scratch),
            compiler_params=pltpu.CompilerParams(vmem_limit_bytes=VMEM_BYTES),
            cost_estimate=pl.CostEstimate(flops=flops, bytes_accessed=nbytes, transcendentals=0),
            name=name,
        )(*args)

    return run


def iota(shape, dim):
    return lax.broadcasted_iota(jnp.int32, shape, dim)


def hot(mask):
    return jnp.where(mask, 1.0, 0.0).astype(BF)


def dot(a, b):
    return lax.dot_general(a, b, (((1,), (0,)), ((), ())), preferred_element_type=F32)


def dot_t(a, b):
    return lax.dot_general(a, b, (((1,), (1,)), ((), ())), preferred_element_type=F32)


def conv_norm_block(points, window, offsets, kinds, weights, gain, bias):
    rows, span = points.shape[0], window.shape[0]
    target = offsets + iota(offsets.shape, 0) + G
    conv = jnp.zeros(points.shape, F32)
    group = 4
    for first in range(0, offsets.shape[1], group):
        picks = [hot(target[:, n : n + 1] == iota((rows, span), 1)) for n in range(first, first + group)]
        marks = [
            hot(kinds[:, n : n + 1] == iota((rows, weights.shape[0]), 1))
            for n in range(first, first + group)
        ]
        picked = dot(jnp.concatenate(picks, axis=0), window)
        scale = dot(jnp.concatenate(marks, axis=0), weights)
        part = picked * scale
        for n in range(group):
            conv = conv + part[n * rows : (n + 1) * rows]
    residual = (points.astype(F32) + conv).astype(BF)
    features = residual.astype(F32)
    average = jnp.mean(features, axis=1, keepdims=True)
    centered = features - average
    variance = jnp.mean(centered * centered, axis=1, keepdims=True)
    normed = (centered * lax.rsqrt(variance + 1e-05) * gain + bias).astype(BF)
    return residual, normed


def padded_weights(conv_weight):
    kinds = conv_weight.shape[0]
    fill = jnp.zeros((32 - kinds, conv_weight.shape[1]), F32)
    return jnp.concatenate([conv_weight.astype(F32), fill], axis=0).astype(BF)


def front_inner(points, offsets, kinds, owners, conv_weight, gain, bias, residual, normed, place, fetch, dead):
    total = points.shape[0]
    weights = padded_weights(conv_weight[...])
    for block in range(1, total // ROWS - 1):
        rows = slice(block * ROWS, (block + 1) * ROWS)
        window = points[block * ROWS - G : (block + 1) * ROWS + G, :]
        res, nor = conv_norm_block(
            points[rows, :], window, offsets[rows, :], kinds[rows, :], weights, gain[...], bias[...]
        )
        out = slice((block - 1) * ROWS, block * ROWS)
        residual[out, :] = res
        normed[out, :] = nor
    peers = place.shape[0] // HALF_SLOTS
    own = owners[...]
    match = iota((peers, total), 0) == own
    marks = hot(match)
    before = hot(iota((total, total), 0) < iota((total, total), 1))
    earlier = dot(marks, before)
    slot = jnp.sum(jnp.where(match, earlier, 0.0), axis=0, keepdims=True).astype(jnp.int32)
    low = own * HALF_SLOTS + (slot & (HALF_SLOTS - 1))
    high = slot >= HALF_SLOTS
    rows = place.shape[0]
    ups = iota((rows, total), 0)
    place_a = jnp.where(ups == jnp.where(high, -1, low), 1.0, 0.0)
    place_b = jnp.where(ups == jnp.where(high, low, -1), 1.0, 0.0)
    place[:, :total] = place_a.astype(BF)
    place[:, total:] = place_b.astype(BF)
    live_a = jnp.sum(place_a, axis=1, keepdims=True)
    live_b = jnp.sum(place_b, axis=1, keepdims=True)
    lane = iota((rows, 128), 1)
    dead[...] = jnp.where(jnp.where(lane < 64, live_a, live_b) > 0.5, 0.0, DEAD)
    spot = jnp.where(high, low + rows, low).astype(F32)
    column = jnp.transpose(jnp.broadcast_to(spot, (8, total)))[:, 0:1]
    fetch[...] = hot(column.astype(jnp.int32) == iota((total, 2 * rows), 1))


def front_edges(
    above, points, below, offsets, kinds, conv_weight, gain, bias, qkv_weight, inner, place, dead, residual, out, normed
):
    total = points.shape[0]
    weights = padded_weights(conv_weight[...])
    last = total - ROWS
    for start, window in (
        (0, jnp.concatenate([above[...], points[0 : ROWS + G, :]], axis=0)),
        (last, jnp.concatenate([points[last - G :, :], below[...]], axis=0)),
    ):
        rows = slice(start, start + ROWS)
        res, nor = conv_norm_block(
            points[rows, :], window, offsets[rows, :], kinds[rows, :], weights, gain[...], bias[...]
        )
        residual[(0 if start == 0 else ROWS) : (ROWS if start == 0 else 2 * ROWS), :] = res
        normed[rows, :] = nor
    normed[ROWS:last, :] = inner[...]
    q, k, v = (qkv_weight[t] for t in range(3))
    none = jnp.zeros(q.shape, BF)
    left = jnp.concatenate([q, none, k, none, v, none], axis=1)
    right = jnp.concatenate([none, q, none, k, none, v], axis=1)
    rows_in = normed[...]
    stacked = jnp.concatenate(
        [dot(rows_in, left).astype(BF), dot(rows_in, right).astype(BF)], axis=0
    )
    packed = dot(place[...], stacked)
    out[:, 0:128] = (packed[:, 0:128] + dead[...]).astype(BF)
    out[:, 128:] = packed[:, 128:].astype(BF)


def swap_halves(value):
    return jnp.concatenate([value[:, 64:], value[:, :64]], axis=1)


def attend(packed, out, keys, queries, values):
    half = packed.shape[0]
    lane = iota((half, 128), 1)
    q = packed[:, 0:128]
    k = packed[:, 128:256]
    v = packed[:, 256:384]
    qs, ks, vs = (swap_halves(x) for x in (q, k, v))
    zero = jnp.zeros((half, 128), F32)

    def dead_bias(x):
        return jnp.where(x.astype(F32) < 0.1 * DEAD, DEAD, 0.0)

    for part, (qq, kk, vv, flag) in enumerate(((q, k, v, qs), (qs, ks, vs, q))):
        rows = slice(part * half, (part + 1) * half)
        qf, kf, vf = (x.astype(F32) for x in (qq, kk, vv))
        keys[rows, :] = jnp.where(lane < 64, kf, jnp.where(lane == 64, dead_bias(flag), 0.0)).astype(BF)
        extra = jnp.where(lane == 64, 1.0, zero)
        for head in range(2):
            mine = (lane >= head * HD) & (lane < (head + 1) * HD)
            queries[head, rows, :] = jnp.where(mine, qf, extra).astype(BF)
            values[head, rows, :] = jnp.where(mine, vf, extra).astype(BF)
    factor = math.log2(math.e) / math.sqrt(HD)
    step = 128

    def one(index):
        base = pl.multiple_of(index * step, step)
        halves = []
        for part in range(2):
            results = []
            for head in range(2):
                mine = queries[head, pl.ds(part * half + base, step), :]
                scores = dot_t(mine, keys[...])
                top = jnp.max(scores, axis=1, keepdims=True)
                soft = jnp.exp2((scores - top) * factor).astype(BF)
                summed = dot(soft, values[head])
                results.append(summed / summed[:, 64:65])
            block_lane = iota((step, 128), 1)
            halves.append(jnp.where(block_lane < HD, results[0], results[1]))
        moved = jnp.concatenate([halves[1][:, 64:], halves[1][:, :64]], axis=1)
        block_lane = iota((step, 128), 1)
        out[pl.ds(base, step), :] = jnp.where(block_lane < 64, halves[0], moved).astype(BF)

    pl.loop(0, half // step)(one)


def fetch_rows(returned, fetch, out):
    half = returned.shape[0]
    value = returned[...]
    lane = iota((half, 128), 1)
    zero = jnp.zeros((half, 128), BF)
    moved = swap_halves(value)
    left = jnp.concatenate([jnp.where(lane < 64, value, zero), jnp.where(lane < 64, moved, zero)], axis=0)
    right = jnp.concatenate([jnp.where(lane < 64, zero, moved), jnp.where(lane < 64, zero, value)], axis=0)
    points = fetch.shape[0] // 2
    rows = (dot(fetch[:points, :], left) + dot(fetch[points:, :], right)).astype(BF)
    for peer in range(out.shape[0]):
        out[peer] = rows


def finish(gathered, edge_res, inner_res, proj_weight, clusters, block_out, sums, block):
    channels = gathered.shape[0]
    width = proj_weight.shape[1]
    part = width // channels
    wide = jnp.concatenate([gathered[c] for c in range(channels)], axis=1)
    proj = proj_weight[...]
    none = jnp.zeros((part, width), BF)
    low, high = [], []
    for c in range(channels):
        piece = proj[c * part : (c + 1) * part, :]
        low += [piece, none]
        high += [none, piece]
    points = block.shape[0] // 2
    last = 2 * points - ROWS
    first = dot(wide, jnp.concatenate(low, axis=0))
    second = dot(wide, jnp.concatenate(high, axis=0))
    block[0:ROWS, :] = (edge_res[0:ROWS, :].astype(F32) + first[0:ROWS]).astype(BF)
    block[ROWS:points, :] = (inner_res[0 : points - ROWS, :].astype(F32) + first[ROWS:]).astype(BF)
    block[points:last, :] = (inner_res[points - ROWS :, :].astype(F32) + second[: last - points]).astype(BF)
    block[last:, :] = (edge_res[ROWS:, :].astype(F32) + second[last - points :]).astype(BF)
    full = block[...]
    channel = lax.axis_index("ch")
    pick = hot(iota((width, part), 0) == iota((width, part), 1) + channel * part)
    block_out[...] = dot(full, pick).astype(BF)
    count = 2 * points // 4
    base = lax.axis_index("pts") * count - 1
    rows = sums.shape[0]
    member = jnp.where(iota((rows, 2 * points), 0) == clusters[...] - base, 1.0, 0.0)
    sums[:, :width] = dot(member.astype(BF), full)
    sums[:, width:] = jnp.broadcast_to(jnp.sum(member, axis=1, keepdims=True), (rows, 128))


def pool(sums, spill, pool_weight, out):
    count = out.shape[0]
    width = pool_weight.shape[0]
    own = sums[1 : count + 1, :]
    total = jnp.where(iota(own.shape, 0) == count - 1, own + spill[0:1, :], own)
    value = total[:, :width]
    high = value.astype(BF)
    low = (value - high.astype(F32)).astype(BF)
    weight = pool_weight[...]
    lifted = dot(high, weight) + dot(low, weight)
    mean = lifted / total[:, width:]
    out[...] = (mean * (1.0 + lax.erf(mean * math.sqrt(0.5))) * 0.5).astype(BF)


def shape(dims, kind=BF):
    return jax.ShapeDtypeStruct(dims, kind)


def shards(
    points_in,
    neighbor_offsets,
    kernel_ids,
    cluster_ids,
    owners,
    conv_weight,
    norm_gain,
    norm_bias,
    qkv_weight,
    proj_weight,
    pool_weight,
):
    total, width = points_in.shape
    nodes = lax.axis_size("pts")
    channels = lax.axis_size("ch")
    up = [(i, i + 1) for i in range(nodes - 1)]
    down = [(j, i) for i, j in up]
    above = lax.ppermute(points_in[total - G :], "pts", up)
    below = lax.ppermute(points_in[:G], "pts", down)
    gain, bias = norm_gain.reshape(1, width), norm_bias.reshape(1, width)
    slots = nodes * HALF_SLOTS
    inner_rows = total - 2 * ROWS
    inner_res, inner_normed, place, fetch, dead = call(
        front_inner,
        (
            shape((inner_rows, width)),
            shape((inner_rows, width)),
            shape((slots, 2 * total)),
            shape((total, 2 * slots)),
            shape((slots, 128), F32),
        ),
        flops=10**9,
        nbytes=4 * 10**6,
        name="front_inner",
    )(points_in, neighbor_offsets, kernel_ids, owners.reshape(1, total), conv_weight, gain, bias)
    edge_res, packed = call(
        front_edges,
        (shape((2 * ROWS, width)), shape((slots, 384))),
        scratch=(pltpu.VMEM((total, width), BF),),
        flops=10**9,
        nbytes=4 * 10**6,
        name="front_edges",
    )(
        above,
        points_in,
        below,
        neighbor_offsets,
        kernel_ids,
        conv_weight,
        gain,
        bias,
        qkv_weight,
        inner_normed,
        place,
        dead,
    )
    arrived = lax.all_to_all(
        packed.reshape(nodes, HALF_SLOTS, 384), "pts", split_axis=0, concat_axis=0, tiled=True
    ).reshape(slots, 384)
    attended = call(
        attend,
        shape((slots, 128)),
        scratch=(
            pltpu.VMEM((2 * slots, 128), BF),
            pltpu.VMEM((2, 2 * slots, 128), BF),
            pltpu.VMEM((2, 2 * slots, 128), BF),
        ),
        flops=10**9,
        nbytes=10**6,
        name="attend",
    )(arrived)
    returned = lax.all_to_all(
        attended.reshape(nodes, HALF_SLOTS, 128), "pts", split_axis=0, concat_axis=0, tiled=True
    ).reshape(slots, 128)
    rows = call(
        fetch_rows, shape((channels, total // 2, 128)), flops=10**8, nbytes=10**6, name="fetch_rows"
    )(returned, fetch)
    gathered = lax.all_to_all(rows, "ch", split_axis=0, concat_axis=0, tiled=True)
    clusters = total // 4
    block_out, sums = call(
        finish,
        (shape((total, width // channels)), shape((clusters + 8, width + 128), F32)),
        scratch=(pltpu.VMEM((total, width), BF),),
        flops=10**8,
        nbytes=10**6,
        name="finish",
    )(gathered, edge_res, inner_res, proj_weight, cluster_ids.reshape(1, total))
    spill = lax.ppermute(sums[:8], "pts", down)
    pooled = call(pool, shape((clusters, pool_weight.shape[1])), flops=10**7, nbytes=10**5, name="pool")(
        sums, spill, pool_weight
    )
    return block_out, pooled


def solution(mesh):
    return jax.shard_map(
        shards,
        mesh=mesh,
        in_specs=(
            P("pts", None),
            P("pts", None),
            P("pts", None),
            P("pts"),
            P("pts"),
            P(),
            P(),
            P(),
            P(None, None, "ch"),
            P(),
            P(None, "ch"),
        ),
        out_specs=(P("pts", "ch"), P("pts", "ch")),
        check_vma=False,
    )
```

time: 213 us -> 93.2 us (0.44); the launches traced: 208 us -> 92.8 us
  local copies, waits for them, and re-layouts: 63.5 us -> 4.26 us
  blocking collectives: 10.2 us -> 58 us
  starting transfers between devices: 52.6 us -> 14.4 us
  other arithmetic: 33.1 us -> 0 us
  matrix products: 26.8 us -> 0 us
  waiting for transfers between devices: 20.8 us -> 0.93 us
  Pallas kernels: 0 us -> 14.4 us
    all_to_all x0 -> x3, blocking collectives: none -> 58 us  [the longest x1 30.4 us: shards(): lax.all_to_all(packed.reshape(nodes, HALF_SLOTS, 384), 'pts', split_axis=...]
    gather x34 -> x0, local copies, waits for them, and re-layouts: 46.6 us -> none  [the longest x32 45.2 us: shards(): picked = padded[offsets_base + neighbor_offsets[:, neighbor_slot]]]
    all_to_all x3 -> x0, starting transfers between devices: 34.9 us -> none  [the longest x1 15.5 us: shards(): lax.all_to_all(send_counts, 'pts', split_axis=0, concat_axis=0, tiled=True)]
    dot_general x21 -> x0, matrix products: 26.8 us -> none  [the longest x16 22.3 us: shards(): jnp.dot(selector, conv_weight, preferred_element_type=jnp.float32)]
    all_to_all x3 -> x0, waiting for transfers between devices: 17.7 us -> none  [the longest x1 15.2 us: shards(): lax.all_to_all(outgoing, 'pts', split_axis=0, concat_axis=0, tiled=True)]
    pallas_call x0 -> x6, Pallas kernels: none -> 14.4 us  [run(): pl.pallas_call(body, out_shape=outs, in_specs=[pl.BlockSpec(memory_space=...]
    all_gather x1 -> x0, blocking collectives: 10.2 us -> none  [shards(): lax.all_gather(returned, 'ch', axis=1, tiled=True)]
    all_to_all x5 -> x0, other arithmetic: 9.87 us -> none  [the longest x2 5.35 us: shards(): lax.all_to_all(outgoing, 'pts', split_axis=0, concat_axis=0, tiled=True)]
  transfers between devices with their start and end apart: 7 -> 3, of which waited for: 4 -> 1; matrix products, arithmetic and copies ran while one was open for 48% -> 1% of each run, Pallas kernels for 0% -> 3%
where the time goes in v1:
time: 93.2 us; the launch traced here: 92.8 us
  blocking collectives  58 us (62%)
  starting transfers between devices  14.4 us (15%)
  Pallas kernels  14.4 us (15%)
  local copies, waits for them, and re-layouts  4.26 us (5%)
    all_to_all x1, blocking collectives, shards(): lax.all_to_all(packed.reshape(nodes, HALF_SLOTS, 384), 'pts', split_axis=...  30.4 us
    all_to_all x1, blocking collectives, shards(): lax.all_to_all(attended.reshape(nodes, HALF_SLOTS, 128), 'pts', split_axi...  17.8 us
    pallas_call x6, Pallas kernels, run(): pl.pallas_call(body, out_shape=outs, in_specs=[pl.BlockSpec(memory_space=...  14.4 us
    all_to_all x1, blocking collectives, shards(): lax.all_to_all(rows, 'ch', split_axis=0, concat_axis=0, tiled=True)  9.74 us
    ppermute x1, starting transfers between devices, shards(): below = lax.ppermute(points_in[:G], 'pts', down)  8.75 us
    ppermute x1, starting transfers between devices, shards(): spill = lax.ppermute(sums[:8], 'pts', down)  3.74 us
    unnamed x26, local copies, waits for them, and re-layouts  3.15 us
    ppermute x1, starting transfers between devices, shards(): above = lax.ppermute(points_in[total - G:], 'pts', up)  1.92 us
  transfers between devices with their start and end apart: 3, of which 1 were waited for; matrix products, arithmetic and copies ran while one was open for 1% of the time, Pallas kernels for 3%

profile of v1, /device:TPU:1, one launch (start us, length us, event | category | flops | bytes accessed | tf_op | source)
XLA Modules:
  0.0 92.8 jit_solution(13928842166627422489)
XLA Ops:
  0.6 0.0 copy-start.8
  0.6 0.9 fusion
  1.6 8.7 %collective-permute-start.1 = (bf16[128,256]{1,0:T(8,128)(2,1)S(1)}, bf16[128,256]{1,0:T(8,128)(2,1)S(1)}, u32[]{:S(2)}, u32[]{:S(2)}) collective-permute-start(bf16[128,256]{1,0:T(8,128)(2,1)S(1)} %get-tuple-element.22), channel_id=1, source_target_pairs={{4,0},{8,4},{12,8},{16,12},{20,16},{24,20},{28,24},{32,28},{36,32}... | collective-permute-start | bytes 196616 | tf_op jit(solution)/shard_map/ppermute | solution.py:282
  10.3 0.0 copy-start.9
  10.3 1.9 %collective-permute-start = (bf16[128,256]{1,0:T(8,128)(2,1)S(1)}, bf16[128,256]{1,0:T(8,128)(2,1)S(1)}, u32[]{:S(2)}, u32[]{:S(2)}) collective-permute-start(bf16[128,256]{1,0:T(8,128)(2,1)S(1)} %get-tuple-element.23), channel_id=1, source_target_pairs={{0,4},{4,8},{8,12},{12,16},{16,20},{20,24},{24,28},{28,32},{32,36}... | collective-permute-start | bytes 196616 | tf_op jit(solution)/shard_map/ppermute | solution.py:281
  12.3 0.0 copy-done.8
  12.3 0.2 copy.17.qkv_weight
  12.4 0.0 copy-done.9
  12.4 0.0 copy-start.10
  12.5 0.0 copy-start.2
  12.5 0.1 copy.15.offsets
  12.6 0.6 copy-done.10
  13.2 0.0 copy-start.4
  13.2 0.0 copy-start.7
  13.2 0.1 copy.16.kinds
  13.3 0.0 copy-start.5
  13.3 0.0 copy-start.6
  13.4 0.1 copy-done.2
  13.4 0.5 copy-done.4
  13.9 0.0 copy-done.7
  13.9 0.1 copy-done.5
  14.0 0.0 copy-done.6
  14.1 2.7 %front_inner.1 = (bf16[256,256]{1,0:T(8,128)(2,1)S(1)}, bf16[256,256]{1,0:T(8,128)(2,1)S(1)}, bf16[512,1024]{1,0:T(8,128)(2,1)S(1)}, bf16[512,1024]{1,0:T(8,128)(2,1)S(1)}, f32[512,128]{1,0:T(8,128)S(1)}) custom-call(bf16[512,256]{1,0:T(8,128)(2,1)S(1)} %copy-done.2, s32[512,16]{1,0:T(8,128)S(1)} %copy.15.offsets, s32[512,16]{1,0:T(8,128)S(1)} %copy.16.kinds, ...), custom_call_target="tpu_custom_call" | custom-call | flops 1000000000 | bytes 4000000 | tf_op jit(solution)/shard_map/front_inner/pallas_call | solution.py:23
  16.7 0.0 collective-permute-done.1.below
  16.7 0.0 collective-permute-done.above
  16.8 3.0 %front_edges.1 = (bf16[256,256]{1,0:T(8,128)(2,1)S(1)}, bf16[512,384]{1,0:T(8,128)(2,1)S(1)}) custom-call(bf16[128,256]{1,0:T(8,128)(2,1)S(1)} %collective-permute-done.above, bf16[512,256]{1,0:T(8,128)(2,1)S(1)} %copy-done.2, bf16[128,256]{1,0:T(8,128)(2,1)S(1)} %collective-permute-done.1.below, s32[512,16]{1,0:T(8,128)S(1)} %copy.15.offsets, ...), custom_call_target="tpu_custom_call" | custom-call | flops 1000000000 | bytes 4000000 | tf_op jit(solution)/shard_map/front_edges/pallas_call | solution.py:23
  19.8 0.1 reshape.31
  19.9 30.4 %all_to_all.15 = bf16[128,4,384]{2,1,0:T(4,128)(2,1)S(1)} all-to-all(bf16[128,4,384]{2,1,0:T(4,128)(2,1)S(1)} %reshape.31), channel_id=1, replica_groups=mesh['pts'=128,'ch'=4] {'pts'}, dimensions={0} | all-to-all | bytes 786432 | tf_op jit(solution)/shard_map/all_to_all | solution.py:320
  50.3 0.1 reshape.32.packed
  50.3 6.9 %attend.1 = bf16[512,128]{1,0:T(8,128)(2,1)S(1)} custom-call(bf16[512,384]{1,0:T(8,128)(2,1)S(1)} %reshape.32.packed), custom_call_target="tpu_custom_call" | custom-call | flops 1000000000 | bytes 1000000 | tf_op jit(solution)/shard_map/attend/pallas_call | solution.py:23
  57.3 17.8 %all_to_all.16 = bf16[128,4,128]{2,1,0:T(4,128)(2,1)S(1)} all-to-all(bf16[128,4,128]{2,1,0:T(4,128)(2,1)S(1)} %bitcast.7), channel_id=1, replica_groups=mesh['pts'=128,'ch'=4] {'pts'}, dimensions={0} | all-to-all | bytes 262144 | tf_op jit(solution)/shard_map/all_to_all | solution.py:335
  75.1 0.5 fetch_rows.1
  75.6 0.0 copy-start
  75.6 9.7 %all_to_all.17.gathered = bf16[4,256,128]{2,1,0:T(8,128)(2,1)S(1)} all-to-all(bf16[4,256,128]{2,1,0:T(8,128)(2,1)S(1)} %fetch_rows.1), channel_id=1, replica_groups=mesh['pts'=128,'ch'=4] {'ch'}, dimensions={0} | all-to-all | bytes 524288 | tf_op jit(solution)/shard_map/all_to_all | solution.py:341
  85.4 0.0 copy-start.3
  85.4 0.0 copy-done
  85.4 0.7 copy-done.3
  86.0 0.5 finish.1
  86.6 3.7 %collective-permute-start.2 = (f32[8,384]{1,0:T(8,128)S(1)}, f32[8,384]{1,0:T(8,128)S(1)}, u32[]{:S(2)}, u32[]{:S(2)}) collective-permute-start(f32[8,384]{1,0:T(8,128)S(1)} %slice.11), channel_id=1, source_target_pairs={{4,0},{8,4},{12,8},{16,12},{20,16},{24,20},{28,24},{32,28},{36,32}... | collective-permute-start | bytes 36872 | tf_op jit(solution)/shard_map/ppermute | solution.py:351
  90.3 0.0 copy-start.1
  90.3 0.7 copy.18
  91.0 0.9 collective-permute-done.2.spill
  92.0 0.0 copy-done.1
  92.0 0.8 pool.1
  (1 shorter events, 0.0 us)
Async XLA Ops:
  0.6 11.6 %copy-start.8 = (bf16[3,256,64]{1,2,0:T(8,128)(2,1)S(1)}, bf16[3,256,64]{1,2,0:T(8,128)(2,1)}, u32[]{:S(2)}) copy-start(bf16[3,256,64]{1,2,0:T(8,128)(2,1)} %param.19) | copy-start | bytes 294916
  1.6 15.2 %collective-permute-start.1 = (bf16[128,256]{1,0:T(8,128)(2,1)S(1)}, bf16[128,256]{1,0:T(8,128)(2,1)S(1)}, u32[]{:S(2)}, u32[]{:S(2)}) collective-permute-start(bf16[128,256]{1,0:T(8,128)(2,1)S(1)} %get-tuple-element.22), channel_id=1, source_target_pairs={{4,0},{8,4},{12,8},{16,12},{20,16},{24,20},{28,24},{32,28},{36,32}... | collective-permute-start | bytes 196616 | tf_op jit(solution)/shard_map/ppermute | solution.py:282
  10.3 2.1 %copy-start.9 = (s32[512,16]{0,1:T(8,128)S(1)}, s32[512,16]{0,1:T(8,128)}, u32[]{:S(2)}) copy-start(s32[512,16]{0,1:T(8,128)} %param.12) | copy-start | bytes 98308
  10.3 6.4 %collective-permute-start = (bf16[128,256]{1,0:T(8,128)(2,1)S(1)}, bf16[128,256]{1,0:T(8,128)(2,1)S(1)}, u32[]{:S(2)}, u32[]{:S(2)}) collective-permute-start(bf16[128,256]{1,0:T(8,128)(2,1)S(1)} %get-tuple-element.23), channel_id=1, source_target_pairs={{0,4},{4,8},{8,12},{12,16},{16,20},{20,24},{24,28},{28,32},{32,36}... | collective-permute-start | bytes 196616 | tf_op jit(solution)/shard_map/ppermute | solution.py:281
  12.4 0.8 copy-start.10
  12.5 1.0 %copy-start.2 = (bf16[512,256]{1,0:T(8,128)(2,1)S(1)}, bf16[512,256]{1,0:T(8,128)(2,1)}, u32[]{:S(2)}) copy-start(bf16[512,256]{1,0:T(8,128)(2,1)} %points.3) | copy-start | bytes 786436
  13.2 0.7 copy-start.4
  13.2 0.7 copy-start.7
  13.3 0.7 copy-start.5
  13.3 0.7 copy-start.6
  75.6 9.8 %copy-start = (bf16[256,256]{1,0:T(8,128)(2,1)S(1)}, bf16[256,256]{1,0:T(8,128)(2,1)}, u32[]{:S(2)}) copy-start(bf16[256,256]{1,0:T(8,128)(2,1)} %proj_weight.1) | copy-start | bytes 393220
  85.4 0.7 copy-start.3
  86.6 5.4 %collective-permute-start.2 = (f32[8,384]{1,0:T(8,128)S(1)}, f32[8,384]{1,0:T(8,128)S(1)}, u32[]{:S(2)}, u32[]{:S(2)}) collective-permute-start(f32[8,384]{1,0:T(8,128)S(1)} %slice.11), channel_id=1, source_target_pairs={{4,0},{8,4},{12,8},{16,12},{20,16},{24,20},{28,24},{32,28},{36,32}... | collective-permute-start | bytes 36872 | tf_op jit(solution)/shard_map/ppermute | solution.py:351
  90.3 1.7 %copy-start.1 = (bf16[256,128]{1,0:T(8,128)(2,1)S(1)}, bf16[256,128]{1,0:T(8,128)(2,1)}, u32[]{:S(2)}) copy-start(bf16[256,128]{1,0:T(8,128)(2,1)} %pool_weight.1) | copy-start | bytes 196612

commit v2 on v1

--- a/solution.py
+++ b/solution.py
@@ -50,8 +50,38 @@
     return lax.dot_general(a, b, (((1,), (1,)), ((), ())), preferred_element_type=F32)
 
 
+def stage(count):
+    def body(*refs):
+        sources, targets, sems = refs[:count], refs[count:-1], refs[-1]
+        pairs = list(zip(sources, targets[:count], strict=True))
+        points = sources[0]
+        pairs.append((points.at[pl.ds(points.shape[0] - G, G), :], targets[count]))
+        pairs.append((points.at[pl.ds(0, G), :], targets[count + 1]))
+        copies = [pltpu.make_async_copy(a, b, sems.at[n]) for n, (a, b) in enumerate(pairs)]
+        for copy in copies:
+            copy.start()
+        for copy in copies:
+            copy.wait()
+
+    def run(*args):
+        outs = [jax.ShapeDtypeStruct(a.shape, a.dtype) for a in args]
+        outs += [jax.ShapeDtypeStruct((G, args[0].shape[1]), args[0].dtype)] * 2
+        return pl.pallas_call(
+            body,
+            out_shape=outs,
+            in_specs=[pl.BlockSpec(memory_space=pltpu.HBM)] * count,
+            out_specs=[pl.BlockSpec(memory_space=pltpu.VMEM)] * (count + 2),
+            scratch_shapes=[pltpu.SemaphoreType.DMA((count + 2,))],
+            compiler_params=pltpu.CompilerParams(vmem_limit_bytes=VMEM_BYTES),
+            name="stage",
+        )(*(pltpu.with_memory_space_constraint(a, pltpu.HBM) for a in args))
+
+    return run
+
+
 def conv_norm_block(points, window, offsets, kinds, weights, gain, bias):
     rows, span = points.shape[0], window.shape[0]
+    offsets, kinds = jnp.transpose(offsets), jnp.transpose(kinds)
     target = offsets + iota(offsets.shape, 0) + G
     conv = jnp.zeros(points.shape, F32)
     group = 4
@@ -88,7 +118,7 @@
         rows = slice(block * ROWS, (block + 1) * ROWS)
         window = points[block * ROWS - G : (block + 1) * ROWS + G, :]
         res, nor = conv_norm_block(
-            points[rows, :], window, offsets[rows, :], kinds[rows, :], weights, gain[...], bias[...]
+            points[rows, :], window, offsets[:, rows], kinds[:, rows], weights, gain[...], bias[...]
         )
         out = slice((block - 1) * ROWS, block * ROWS)
         residual[out, :] = res
@@ -129,18 +159,18 @@
     ):
         rows = slice(start, start + ROWS)
         res, nor = conv_norm_block(
-            points[rows, :], window, offsets[rows, :], kinds[rows, :], weights, gain[...], bias[...]
+            points[rows, :], window, offsets[:, rows], kinds[:, rows], weights, gain[...], bias[...]
         )
         residual[(0 if start == 0 else ROWS) : (ROWS if start == 0 else 2 * ROWS), :] = res
         normed[rows, :] = nor
     normed[ROWS:last, :] = inner[...]
     q, k, v = (qkv_weight[t] for t in range(3))
     none = jnp.zeros(q.shape, BF)
-    left = jnp.concatenate([q, none, k, none, v, none], axis=1)
-    right = jnp.concatenate([none, q, none, k, none, v], axis=1)
+    left = jnp.concatenate([q, none, k, none, v, none], axis=0)
+    right = jnp.concatenate([none, q, none, k, none, v], axis=0)
     rows_in = normed[...]
     stacked = jnp.concatenate(
-        [dot(rows_in, left).astype(BF), dot(rows_in, right).astype(BF)], axis=0
+        [dot_t(rows_in, left).astype(BF), dot_t(rows_in, right).astype(BF)], axis=0
     )
     packed = dot(place[...], stacked)
     out[:, 0:128] = (packed[:, 0:128] + dead[...]).astype(BF)
@@ -163,35 +193,35 @@
     def dead_bias(x):
         return jnp.where(x.astype(F32) < 0.1 * DEAD, DEAD, 0.0)
 
+    step = 128
     for part, (qq, kk, vv, flag) in enumerate(((q, k, v, qs), (qs, ks, vs, q))):
         rows = slice(part * half, (part + 1) * half)
         qf, kf, vf = (x.astype(F32) for x in (qq, kk, vv))
         keys[rows, :] = jnp.where(lane < 64, kf, jnp.where(lane == 64, dead_bias(flag), 0.0)).astype(BF)
         extra = jnp.where(lane == 64, 1.0, zero)
+        values[rows, :] = jnp.where(lane < 64, vf, extra).astype(BF)
         for head in range(2):
             mine = (lane >= head * HD) & (lane < (head + 1) * HD)
-            queries[head, rows, :] = jnp.where(mine, qf, extra).astype(BF)
-            values[head, rows, :] = jnp.where(mine, vf, extra).astype(BF)
+            query = jnp.where(mine, qf, extra).astype(BF)
+            for index in range(half // step):
+                start = (index * 4 + part * 2 + head) * step
+                queries[start : start + step, :] = query[index * step : (index + 1) * step, :]
     factor = math.log2(math.e) / math.sqrt(HD)
-    step = 128
 
     def one(index):
-        base = pl.multiple_of(index * step, step)
-        halves = []
-        for part in range(2):
-            results = []
-            for head in range(2):
-                mine = queries[head, pl.ds(part * half + base, step), :]
-                scores = dot_t(mine, keys[...])
-                top = jnp.max(scores, axis=1, keepdims=True)
-                soft = jnp.exp2((scores - top) * factor).astype(BF)
-                summed = dot(soft, values[head])
-                results.append(summed / summed[:, 64:65])
-            block_lane = iota((step, 128), 1)
-            halves.append(jnp.where(block_lane < HD, results[0], results[1]))
-        moved = jnp.concatenate([halves[1][:, 64:], halves[1][:, :64]], axis=1)
+        mine = queries[pl.ds(pl.multiple_of(index * 4 * step, 4 * step), 4 * step), :]
+        scores = dot_t(mine, keys[...])
+        top = jnp.max(scores, axis=1, keepdims=True)
+        soft = jnp.exp2((scores - top) * factor).astype(BF)
+        summed = dot(soft, values[...])
+        result = summed / summed[:, 64:65]
+        pieces = [result[n * step : (n + 1) * step] for n in range(4)]
         block_lane = iota((step, 128), 1)
-        out[pl.ds(base, step), :] = jnp.where(block_lane < 64, halves[0], moved).astype(BF)
+        first = jnp.where(block_lane < HD, pieces[0], pieces[1])
+        second = jnp.where(block_lane < HD, pieces[2], pieces[3])
+        moved = jnp.concatenate([second[:, 64:], second[:, :64]], axis=1)
+        rows = pl.ds(pl.multiple_of(index * step, step), step)
+        out[rows, :] = jnp.where(block_lane < 64, first, moved).astype(BF)
 
     pl.loop(0, half // step)(one)
 
@@ -232,8 +262,8 @@
     block[last:, :] = (edge_res[ROWS:, :].astype(F32) + second[last - points :]).astype(BF)
     full = block[...]
     channel = lax.axis_index("ch")
-    pick = hot(iota((width, part), 0) == iota((width, part), 1) + channel * part)
-    block_out[...] = dot(full, pick).astype(BF)
+    pick = hot(iota((part, width), 1) == iota((part, width), 0) + channel * part)
+    block_out[...] = dot_t(pick, full).astype(BF)
     count = 2 * points // 4
     base = lax.axis_index("pts") * count - 1
     rows = sums.shape[0]
@@ -278,9 +308,25 @@
     channels = lax.axis_size("ch")
     up = [(i, i + 1) for i in range(nodes - 1)]
     down = [(j, i) for i, j in up]
-    above = lax.ppermute(points_in[total - G :], "pts", up)
-    below = lax.ppermute(points_in[:G], "pts", down)
-    gain, bias = norm_gain.reshape(1, width), norm_bias.reshape(1, width)
+    offsets, kinds = jnp.transpose(neighbor_offsets), jnp.transpose(kernel_ids)
+    args = (
+        points_in,
+        offsets,
+        kinds,
+        owners.reshape(1, total),
+        conv_weight,
+        norm_gain.reshape(1, width),
+        norm_bias.reshape(1, width),
+        jnp.transpose(qkv_weight, (0, 2, 1)),
+        proj_weight,
+        pool_weight,
+        cluster_ids.reshape(1, total),
+    )
+    staged = stage(len(args))(*args)
+    points, offsets, kinds, own, conv_weight, gain, bias, qkv_weight, proj_weight, pool_weight = staged[:10]
+    clusters_here, tail, head = staged[10:]
+    above = lax.ppermute(tail, "pts", up)
+    below = lax.ppermute(head, "pts", down)
     slots = nodes * HALF_SLOTS
     inner_rows = total - 2 * ROWS
     inner_res, inner_normed, place, fetch, dead = call(
@@ -295,7 +341,7 @@
         flops=10**9,
         nbytes=4 * 10**6,
         name="front_inner",
-    )(points_in, neighbor_offsets, kernel_ids, owners.reshape(1, total), conv_weight, gain, bias)
+    )(points, offsets, kinds, own, conv_weight, gain, bias)
     edge_res, packed = call(
         front_edges,
         (shape((2 * ROWS, width)), shape((slots, 384))),
@@ -305,10 +351,10 @@
         name="front_edges",
     )(
         above,
-        points_in,
+        points,
         below,
-        neighbor_offsets,
-        kernel_ids,
+        offsets,
+        kinds,
         conv_weight,
         gain,
         bias,
@@ -325,8 +371,8 @@
         shape((slots, 128)),
         scratch=(
             pltpu.VMEM((2 * slots, 128), BF),
-            pltpu.VMEM((2, 2 * slots, 128), BF),
-            pltpu.VMEM((2, 2 * slots, 128), BF),
+            pltpu.VMEM((4 * slots, 128), BF),
+            pltpu.VMEM((2 * slots, 128), BF),
         ),
         flops=10**9,
         nbytes=10**6,
@@ -342,17 +388,17 @@
     clusters = total // 4
     block_out, sums = call(
         finish,
-        (shape((total, width // channels)), shape((clusters + 8, width + 128), F32)),
+        (shape((width // channels, total)), shape((clusters + 8, width + 128), F32)),
         scratch=(pltpu.VMEM((total, width), BF),),
         flops=10**8,
         nbytes=10**6,
         name="finish",
-    )(gathered, edge_res, inner_res, proj_weight, cluster_ids.reshape(1, total))
+    )(gathered, edge_res, inner_res, proj_weight, clusters_here)
     spill = lax.ppermute(sums[:8], "pts", down)
     pooled = call(pool, shape((clusters, pool_weight.shape[1])), flops=10**7, nbytes=10**5, name="pool")(
         sums, spill, pool_weight
     )
-    return block_out, pooled
+    return jnp.transpose(block_out), pooled
 
 
 def solution(mesh):

time: 93.2 us -> 92.7 us (level)
  local copies, waits for them, and re-layouts: 4.26 us -> 0.19 us
  blocking collectives: 58 us -> 60.2 us
  Pallas kernels: 14.4 us -> 15.8 us
    unnamed x26 -> x0, local copies, waits for them, and re-layouts: 3.15 us -> none
    all_to_all x1, blocking collectives: 30.4 us -> 32.8 us  [shards(): lax.all_to_all(packed.reshape(nodes, HALF_SLOTS, 384), 'pts', split_axis=...]
    pallas_call x6 -> x7, Pallas kernels: 14.4 us -> 15.8 us  [run(): pl.pallas_call(body, out_shape=outs, in_specs=[pl.BlockSpec(memory_space=...]
  transfers between devices with their start and end apart: 3 -> 3, of which waited for: 1 -> 1; matrix products, arithmetic and copies ran while one was open for 1% -> 0% of each run, Pallas kernels for 3% -> 3%
where the time goes in v2:
time: 92.7 us; the launch traced here: 92.4 us
  blocking collectives  60.2 us (65%)
  Pallas kernels  15.8 us (17%)
  starting transfers between devices  13.8 us (15%)
  waiting for transfers between devices  1.67 us (2%)
    all_to_all x1, blocking collectives, shards(): lax.all_to_all(packed.reshape(nodes, HALF_SLOTS, 384), 'pts', split_axis=...  32.8 us
    all_to_all x1, blocking collectives, shards(): lax.all_to_all(attended.reshape(nodes, HALF_SLOTS, 128), 'pts', split_axi...  17.8 us
    pallas_call x7, Pallas kernels, run(): pl.pallas_call(body, out_shape=outs, in_specs=[pl.BlockSpec(memory_space=...  15.8 us
    all_to_all x1, blocking collectives, shards(): lax.all_to_all(rows, 'ch', split_axis=0, concat_axis=0, tiled=True)  9.61 us
    ppermute x1, starting transfers between devices, shards(): below = lax.ppermute(head, 'pts', down)  5.46 us
    ppermute x1, starting transfers between devices, shards(): above = lax.ppermute(tail, 'pts', up)  4.58 us
    ppermute x1, starting transfers between devices, shards(): spill = lax.ppermute(sums[:8], 'pts', down)  3.72 us
  transfers between devices with their start and end apart: 3, of which 1 were waited for; matrix products, arithmetic and copies ran while one was open for 0% of the time, Pallas kernels for 3%

profile of v2, /device:TPU:1, one launch (start us, length us, event | category | flops | bytes accessed | tf_op | source)
XLA Modules:
  0.0 92.4 jit_solution(15295204000810612093)
XLA Ops:
  0.6 1.3 %stage.1 = (bf16[512,256]{1,0:T(8,128)(2,1)S(1)}, s32[16,512]{1,0:T(8,128)S(1)}, s32[16,512]{1,0:T(8,128)S(1)}, s32[1,512]{1,0:T(1,128)S(1)}, bf16[27,256]{1,0:T...) custom-call(bf16[512,256]{1,0:T(8,128)(2,1)} %refs_0_.1, ...), custom_call_target="tpu_custom_call" | custom-call | tf_op jit(solution)/shard_map/stage/pallas_call | solution.py:69
  1.9 4.6 %collective-permute-start = (bf16[128,256]{1,0:T(8,128)(2,1)S(1)}, bf16[128,256]{1,0:T(8,128)(2,1)S(1)}, u32[]{:S(2)}, u32[]{:S(2)}) collective-permute-start(bf16[128,256]{1,0:T(8,128)(2,1)S(1)} %get-tuple-element.24), channel_id=1, source_target_pairs={{0,4},{4,8},{8,12},{12,16},{16,20},{20,24},{24,28},{28,32},{32,36}... | collective-permute-start | bytes 196616 | tf_op jit(solution)/shard_map/ppermute | solution.py:328
  6.5 5.5 %collective-permute-start.1 = (bf16[128,256]{1,0:T(8,128)(2,1)S(1)}, bf16[128,256]{1,0:T(8,128)(2,1)S(1)}, u32[]{:S(2)}, u32[]{:S(2)}) collective-permute-start(bf16[128,256]{1,0:T(8,128)(2,1)S(1)} %get-tuple-element.26), channel_id=1, source_target_pairs={{4,0},{8,4},{12,8},{16,12},{20,16},{24,20},{28,24},{32,28},{36,32}... | collective-permute-start | bytes 196616 | tf_op jit(solution)/shard_map/ppermute | solution.py:329
  12.0 3.0 %front_inner.1 = (bf16[256,256]{1,0:T(8,128)(2,1)S(1)}, bf16[256,256]{1,0:T(8,128)(2,1)S(1)}, bf16[512,1024]{1,0:T(8,128)(2,1)S(1)}, bf16[512,1024]{1,0:T(8,128)(2,1)S(1)}, f32[512,128]{1,0:T(8,128)S(1)}) custom-call(bf16[512,256]{1,0:T(8,128)(2,1)S(1)} %get-tuple-element.25.points, s32[16,512]{1,0:T(8,128)S(1)} %get-tuple-element.27.offsets, ...), custom_call_target="tpu_custom_call" | custom-call | flops 1000000000 | bytes 4000000 | tf_op jit(solution)/shard_map/front_inner/pallas_call | solution.py:23
  15.0 0.0 collective-permute-done.above
  15.0 0.0 collective-permute-done.1.below
  15.0 3.1 %front_edges.1 = (bf16[256,256]{1,0:T(8,128)(2,1)S(1)}, bf16[512,384]{1,0:T(8,128)(2,1)S(1)}) custom-call(bf16[128,256]{1,0:T(8,128)(2,1)S(1)} %collective-permute-done.above, bf16[512,256]{1,0:T(8,128)(2,1)S(1)} %get-tuple-element.25.points, bf16[128,256]{1,0:T(8,128)(2,1)S(1)} %collective-permute-done.1.below, s32[16,512]{1,0:T(8,128)S(1)} %get-tuple-element.27.offsets, ...), custom_call_target="tpu_custom_call" | custom-call | flops 1000000000 | bytes 4000000 | tf_op jit(solution)/shard_map/front_edges/pallas_call | solution.py:23
  18.1 0.1 reshape.32
  18.2 32.8 %all_to_all.15 = bf16[128,4,384]{2,1,0:T(4,128)(2,1)S(1)} all-to-all(bf16[128,4,384]{2,1,0:T(4,128)(2,1)S(1)} %reshape.32), channel_id=1, replica_groups=mesh['pts'=128,'ch'=4] {'pts'}, dimensions={0} | all-to-all | bytes 786432 | tf_op jit(solution)/shard_map/all_to_all | solution.py:366
  51.0 0.1 reshape.33.packed
  51.1 6.0 %attend.1 = bf16[512,128]{1,0:T(8,128)(2,1)S(1)} custom-call(bf16[512,384]{1,0:T(8,128)(2,1)S(1)} %reshape.33.packed), custom_call_target="tpu_custom_call" | custom-call | flops 1000000000 | bytes 1000000 | tf_op jit(solution)/shard_map/attend/pallas_call | solution.py:23
  57.1 17.8 %all_to_all.16 = bf16[128,4,128]{2,1,0:T(4,128)(2,1)S(1)} all-to-all(bf16[128,4,128]{2,1,0:T(4,128)(2,1)S(1)} %bitcast.11), channel_id=1, replica_groups=mesh['pts'=128,'ch'=4] {'pts'}, dimensions={0} | all-to-all | bytes 262144 | tf_op jit(solution)/shard_map/all_to_all | solution.py:381
  74.9 0.5 fetch_rows.1
  75.5 9.6 %all_to_all.17.gathered = bf16[4,256,128]{2,1,0:T(8,128)(2,1)S(1)} all-to-all(bf16[4,256,128]{2,1,0:T(8,128)(2,1)S(1)} %fetch_rows.1), channel_id=1, replica_groups=mesh['pts'=128,'ch'=4] {'ch'}, dimensions={0} | all-to-all | bytes 524288 | tf_op jit(solution)/shard_map/all_to_all | solution.py:387
  85.1 1.1 %finish.1 = (bf16[64,512]{1,0:T(8,128)(2,1)}, f32[136,384]{1,0:T(8,128)S(1)}) custom-call(bf16[4,256,128]{2,1,0:T(8,128)(2,1)S(1)} %all_to_all.17.gathered, bf16[256,256]{1,0:T(8,128)(2,1)S(1)} %get-tuple-element.39.edge_res, bf16[256,256]{1,0:T(8,128)(2,1)S(1)} %get-tuple-element.40.inner_res, bf16[256,256]{1,0:T(8,128)(2,1)S(1)} %get-tuple-element.41.proj_weight, ...), custom_call_target="tpu_custom_call" | custom-call | flops 100000000 | bytes 1000000 | tf_op jit(solution)/shard_map/finish/pallas_call | solution.py:23
  86.2 3.7 %collective-permute-start.2 = (f32[8,384]{1,0:T(8,128)S(1)}, f32[8,384]{1,0:T(8,128)S(1)}, u32[]{:S(2)}, u32[]{:S(2)}) collective-permute-start(f32[8,384]{1,0:T(8,128)S(1)} %slice.3), channel_id=1, source_target_pairs={{4,0},{8,4},{12,8},{16,12},{20,16},{24,20},{28,24},{32,28},{36,32}... | collective-permute-start | bytes 36872 | tf_op jit(solution)/shard_map/ppermute | solution.py:397
  89.9 1.7 %collective-permute-done.2.spill = f32[8,384]{1,0:T(8,128)S(1)} collective-permute-done((f32[8,384]{1,0:T(8,128)S(1)}, f32[8,384]{1,0:T(8,128)S(1)}, u32[]{:S(2)}, u32[]{:S(2)}) %collective-permute-start.2) | collective-permute-done | bytes 12320 | tf_op jit(solution)/shard_map/ppermute | solution.py:397
  91.6 0.8 pool.1
  (1 shorter events, 0.0 us)
Async XLA Ops:
  1.9 13.0 %collective-permute-start = (bf16[128,256]{1,0:T(8,128)(2,1)S(1)}, bf16[128,256]{1,0:T(8,128)(2,1)S(1)}, u32[]{:S(2)}, u32[]{:S(2)}) collective-permute-start(bf16[128,256]{1,0:T(8,128)(2,1)S(1)} %get-tuple-element.24), channel_id=1, source_target_pairs={{0,4},{4,8},{8,12},{12,16},{16,20},{20,24},{24,28},{28,32},{32,36}... | collective-permute-start | bytes 196616 | tf_op jit(solution)/shard_map/ppermute | solution.py:328
  6.5 8.4 %collective-permute-start.1 = (bf16[128,256]{1,0:T(8,128)(2,1)S(1)}, bf16[128,256]{1,0:T(8,128)(2,1)S(1)}, u32[]{:S(2)}, u32[]{:S(2)}) collective-permute-start(bf16[128,256]{1,0:T(8,128)(2,1)S(1)} %get-tuple-element.26), channel_id=1, source_target_pairs={{4,0},{8,4},{12,8},{16,12},{20,16},{24,20},{28,24},{32,28},{36,32}... | collective-permute-start | bytes 196616 | tf_op jit(solution)/shard_map/ppermute | solution.py:329
  86.2 5.4 %collective-permute-start.2 = (f32[8,384]{1,0:T(8,128)S(1)}, f32[8,384]{1,0:T(8,128)S(1)}, u32[]{:S(2)}, u32[]{:S(2)}) collective-permute-start(f32[8,384]{1,0:T(8,128)S(1)} %slice.3), channel_id=1, source_target_pairs={{4,0},{8,4},{12,8},{16,12},{20,16},{24,20},{28,24},{32,28},{36,32}... | collective-permute-start | bytes 36872 | tf_op jit(solution)/shard_map/ppermute | solution.py:397

commit v3 on v2

--- a/solution.py
+++ b/solution.py
@@ -13,6 +13,8 @@
 ROWS = 128
 HALF_SLOTS = 4
 DEAD = -1e30
+SHIFT_BITS = 10
+SHIFT = 1 << SHIFT_BITS
 BF = jnp.bfloat16
 F32 = jnp.float32
 VMEM_BYTES = 24 * 1024 * 1024
@@ -79,23 +81,30 @@
     return run
 
 
-def conv_norm_block(points, window, offsets, kinds, weights, gain, bias):
+def conv_norm_block(points, window, offsets, kinds, weights, gain, bias, between=()):
     rows, span = points.shape[0], window.shape[0]
-    offsets, kinds = jnp.transpose(offsets), jnp.transpose(kinds)
-    target = offsets + iota(offsets.shape, 0) + G
+    between = list(between)
+    target = jnp.transpose(offsets + jnp.transpose(jnp.broadcast_to(iota((rows, 1), 0), (rows, offsets.shape[0]))) + G)
+    code = target + jnp.transpose(kinds) * SHIFT
     conv = jnp.zeros(points.shape, F32)
     group = 4
-    for first in range(0, offsets.shape[1], group):
-        picks = [hot(target[:, n : n + 1] == iota((rows, span), 1)) for n in range(first, first + group)]
-        marks = [
-            hot(kinds[:, n : n + 1] == iota((rows, weights.shape[0]), 1))
-            for n in range(first, first + group)
-        ]
+    for first in range(0, offsets.shape[0], group):
+        picks, marks = [], []
+        for n in range(first, first + group):
+            value = jnp.broadcast_to(code[:, n : n + 1], (rows, 128))
+            place, kind = value & (SHIFT - 1), lax.shift_right_logical(value, SHIFT_BITS)
+            wide = jnp.concatenate([hot(place == iota((rows, 128), 1) + lanes) for lanes in range(0, span, 128)], axis=1)
+            picks.append(wide)
+            marks.append(hot(kind == iota((rows, 128), 1)))
         picked = dot(jnp.concatenate(picks, axis=0), window)
         scale = dot(jnp.concatenate(marks, axis=0), weights)
         part = picked * scale
         for n in range(group):
             conv = conv + part[n * rows : (n + 1) * rows]
+        if between:
+            between.pop(0)()
+    for step in between:
+        step()
     residual = (points.astype(F32) + conv).astype(BF)
     features = residual.astype(F32)
     average = jnp.mean(features, axis=1, keepdims=True)
@@ -107,44 +116,61 @@
 
 def padded_weights(conv_weight):
     kinds = conv_weight.shape[0]
-    fill = jnp.zeros((32 - kinds, conv_weight.shape[1]), F32)
+    fill = jnp.zeros((128 - kinds, conv_weight.shape[1]), F32)
     return jnp.concatenate([conv_weight.astype(F32), fill], axis=0).astype(BF)
 
 
 def front_inner(points, offsets, kinds, owners, conv_weight, gain, bias, residual, normed, place, fetch, dead):
     total = points.shape[0]
     weights = padded_weights(conv_weight[...])
-    for block in range(1, total // ROWS - 1):
+    slots = place.shape[0] // 2
+    peers = slots // HALF_SLOTS
+    own = owners[...]
+    match = iota((peers, total), 0) == own
+    before = hot(iota((total, total), 0) < iota((total, total), 1))
+    earlier = dot(hot(match), before)
+    slot = jnp.sum(jnp.where(match, earlier, 0.0), axis=0, keepdims=True).astype(jnp.int32)
+    low = own * HALF_SLOTS + (slot & (HALF_SLOTS - 1))
+    spot = jnp.where(slot >= HALF_SLOTS, low + slots, low)
+    column = jnp.transpose(jnp.broadcast_to(spot, (8, total)))[:, 0:1]
+
+    def build_place(start):
+        lane = iota((ROWS, 128), 1)
+        rows = slice(start, start + ROWS)
+        live = []
+        for half in range(2):
+            here = slice(half * slots + start, half * slots + start + ROWS)
+            mask = jnp.where(iota((ROWS, total), 0) + (half * slots + start) == spot, 1.0, 0.0)
+            place[here, :] = mask.astype(BF)
+            live.append(jnp.sum(mask, axis=1, keepdims=True))
+        dead[rows, :] = jnp.where(jnp.where(lane < 64, live[0], live[1]) > 0.5, 0.0, DEAD)
+
+    def build_fetch(start):
+        rows = slice(start, start + ROWS)
+        here = jnp.broadcast_to(column[rows, :], (ROWS, 128))
+        for lanes in range(0, 2 * slots, 128):
+            fetch[rows, lanes : lanes + 128] = hot(here == iota((ROWS, 128), 1) + lanes)
+
+    pieces = [functools.partial(build_place, n) for n in range(0, slots, ROWS)]
+    pieces += [functools.partial(build_fetch, n) for n in range(0, total, ROWS)]
+    blocks = range(1, total // ROWS - 1)
+    share = len(pieces) // len(blocks)
+    for block in blocks:
         rows = slice(block * ROWS, (block + 1) * ROWS)
         window = points[block * ROWS - G : (block + 1) * ROWS + G, :]
         res, nor = conv_norm_block(
-            points[rows, :], window, offsets[:, rows], kinds[:, rows], weights, gain[...], bias[...]
+            points[rows, :],
+            window,
+            offsets[:, rows],
+            kinds[:, rows],
+            weights,
+            gain[...],
+            bias[...],
+            pieces[(block - 1) * share : block * share],
         )
         out = slice((block - 1) * ROWS, block * ROWS)
         residual[out, :] = res
         normed[out, :] = nor
-    peers = place.shape[0] // HALF_SLOTS
-    own = owners[...]
-    match = iota((peers, total), 0) == own
-    marks = hot(match)
-    before = hot(iota((total, total), 0) < iota((total, total), 1))
-    earlier = dot(marks, before)
-    slot = jnp.sum(jnp.where(match, earlier, 0.0), axis=0, keepdims=True).astype(jnp.int32)
-    low = own * HALF_SLOTS + (slot & (HALF_SLOTS - 1))
-    high = slot >= HALF_SLOTS
-    rows = place.shape[0]
-    ups = iota((rows, total), 0)
-    place_a = jnp.where(ups == jnp.where(high, -1, low), 1.0, 0.0)
-    place_b = jnp.where(ups == jnp.where(high, low, -1), 1.0, 0.0)
-    place[:, :total] = place_a.astype(BF)
-    place[:, total:] = place_b.astype(BF)
-    live_a = jnp.sum(place_a, axis=1, keepdims=True)
-    live_b = jnp.sum(place_b, axis=1, keepdims=True)
-    lane = iota((rows, 128), 1)
-    dead[...] = jnp.where(jnp.where(lane < 64, live_a, live_b) > 0.5, 0.0, DEAD)
-    spot = jnp.where(high, low + rows, low).astype(F32)
-    column = jnp.transpose(jnp.broadcast_to(spot, (8, total)))[:, 0:1]
-    fetch[...] = hot(column.astype(jnp.int32) == iota((total, 2 * rows), 1))
 
 
 def front_edges(
@@ -168,11 +194,11 @@
     none = jnp.zeros(q.shape, BF)
     left = jnp.concatenate([q, none, k, none, v, none], axis=0)
     right = jnp.concatenate([none, q, none, k, none, v], axis=0)
-    rows_in = normed[...]
-    stacked = jnp.concatenate(
-        [dot_t(rows_in, left).astype(BF), dot_t(rows_in, right).astype(BF)], axis=0
+    placed = dot(place[...], normed[...]).astype(BF)
+    slots = out.shape[0]
+    packed = dot_t(
+        jnp.concatenate([placed[:slots], placed[slots:]], axis=1), jnp.concatenate([left, right], axis=1)
     )
-    packed = dot(place[...], stacked)
     out[:, 0:128] = (packed[:, 0:128] + dead[...]).astype(BF)
     out[:, 128:] = packed[:, 128:].astype(BF)
 
@@ -207,23 +233,31 @@
                 start = (index * 4 + part * 2 + head) * step
                 queries[start : start + step, :] = query[index * step : (index + 1) * step, :]
     factor = math.log2(math.e) / math.sqrt(HD)
-
-    def one(index):
-        mine = queries[pl.ds(pl.multiple_of(index * 4 * step, 4 * step), 4 * step), :]
-        scores = dot_t(mine, keys[...])
+    block_lane = iota((step, 128), 1)
+
+    def scores_of(chunk):
+        return dot_t(queries[chunk * 2 * step : (chunk + 1) * 2 * step, :], keys[...])
+
+    def attended_of(scores):
         top = jnp.max(scores, axis=1, keepdims=True)
         soft = jnp.exp2((scores - top) * factor).astype(BF)
         summed = dot(soft, values[...])
         result = summed / summed[:, 64:65]
-        pieces = [result[n * step : (n + 1) * step] for n in range(4)]
-        block_lane = iota((step, 128), 1)
-        first = jnp.where(block_lane < HD, pieces[0], pieces[1])
-        second = jnp.where(block_lane < HD, pieces[2], pieces[3])
-        moved = jnp.concatenate([second[:, 64:], second[:, :64]], axis=1)
-        rows = pl.ds(pl.multiple_of(index * step, step), step)
-        out[rows, :] = jnp.where(block_lane < 64, first, moved).astype(BF)
-
-    pl.loop(0, half // step)(one)
+        return jnp.where(block_lane < HD, result[:step], result[step:])
+
+    chunks = 2 * half // step
+    ahead = [scores_of(0)]
+    done = []
+    for chunk in range(chunks):
+        if chunk + 1 < chunks:
+            ahead.append(scores_of(chunk + 1))
+        done.append(attended_of(ahead.pop(0)))
+        if len(done) == 2:
+            first, second = done
+            done = []
+            moved = jnp.concatenate([second[:, 64:], second[:, :64]], axis=1)
+            rows = slice((chunk // 2) * step, (chunk // 2 + 1) * step)
+            out[rows, :] = jnp.where(block_lane < 64, first, moved).astype(BF)
 
 
 def fetch_rows(returned, fetch, out):
@@ -334,7 +368,7 @@
         (
             shape((inner_rows, width)),
             shape((inner_rows, width)),
-            shape((slots, 2 * total)),
+            shape((2 * slots, total)),
             shape((total, 2 * slots)),
             shape((slots, 128), F32),
         ),

time: 92.7 us -> 89.5 us (0.965)
  Pallas kernels: 15.8 us -> 12.6 us
    pallas_call x7, Pallas kernels: 15.8 us -> 12.6 us  [run(): pl.pallas_call(body, out_shape=outs, in_specs=[pl.BlockSpec(memory_space=...]
where the time goes in v3:
time: 89.5 us; the launch traced here: 89.2 us
  blocking collectives  60.2 us (67%)
  starting transfers between devices  13.8 us (15%)
  Pallas kernels  12.6 us (14%)
  waiting for transfers between devices  1.67 us (2%)
    all_to_all x1, blocking collectives, shards(): lax.all_to_all(packed.reshape(nodes, HALF_SLOTS, 384), 'pts', split_axis=...  32.8 us
    all_to_all x1, blocking collectives, shards(): lax.all_to_all(attended.reshape(nodes, HALF_SLOTS, 128), 'pts', split_axi...  17.8 us
    pallas_call x7, Pallas kernels, run(): pl.pallas_call(body, out_shape=outs, in_specs=[pl.BlockSpec(memory_space=...  12.6 us
    all_to_all x1, blocking collectives, shards(): lax.all_to_all(rows, 'ch', split_axis=0, concat_axis=0, tiled=True)  9.61 us
    ppermute x1, starting transfers between devices, shards(): below = lax.ppermute(head, 'pts', down)  5.46 us
    ppermute x1, starting transfers between devices, shards(): above = lax.ppermute(tail, 'pts', up)  4.58 us
    ppermute x1, starting transfers between devices, shards(): spill = lax.ppermute(sums[:8], 'pts', down)  3.72 us
  transfers between devices with their start and end apart: 3, of which 1 were waited for; matrix products, arithmetic and copies ran while one was open for 0% of the time, Pallas kernels for 3%

profile of v3, /device:TPU:1, one launch (start us, length us, event | category | flops | bytes accessed | tf_op | source)
XLA Modules:
  0.0 89.2 jit_solution(456991213146285563)
XLA Ops:
  0.6 1.3 %stage.1 = (bf16[512,256]{1,0:T(8,128)(2,1)S(1)}, s32[16,512]{1,0:T(8,128)S(1)}, s32[16,512]{1,0:T(8,128)S(1)}, s32[1,512]{1,0:T(1,128)S(1)}, bf16[27,256]{1,0:T...) custom-call(bf16[512,256]{1,0:T(8,128)(2,1)} %refs_0_.1, ...), custom_call_target="tpu_custom_call" | custom-call | tf_op jit(solution)/shard_map/stage/pallas_call | solution.py:71
  1.9 4.6 %collective-permute-start = (bf16[128,256]{1,0:T(8,128)(2,1)S(1)}, bf16[128,256]{1,0:T(8,128)(2,1)S(1)}, u32[]{:S(2)}, u32[]{:S(2)}) collective-permute-start(bf16[128,256]{1,0:T(8,128)(2,1)S(1)} %get-tuple-element.24), channel_id=1, source_target_pairs={{0,4},{4,8},{8,12},{12,16},{16,20},{20,24},{24,28},{28,32},{32,36}... | collective-permute-start | bytes 196616 | tf_op jit(solution)/shard_map/ppermute | solution.py:362
  6.5 5.5 %collective-permute-start.1 = (bf16[128,256]{1,0:T(8,128)(2,1)S(1)}, bf16[128,256]{1,0:T(8,128)(2,1)S(1)}, u32[]{:S(2)}, u32[]{:S(2)}) collective-permute-start(bf16[128,256]{1,0:T(8,128)(2,1)S(1)} %get-tuple-element.26), channel_id=1, source_target_pairs={{4,0},{8,4},{12,8},{16,12},{20,16},{24,20},{28,24},{32,28},{36,32}... | collective-permute-start | bytes 196616 | tf_op jit(solution)/shard_map/ppermute | solution.py:363
  12.0 2.7 %front_inner.1 = (bf16[256,256]{1,0:T(8,128)(2,1)S(1)}, bf16[256,256]{1,0:T(8,128)(2,1)S(1)}, bf16[1024,512]{1,0:T(8,128)(2,1)S(1)}, bf16[512,1024]{1,0:T(8,128)(2,1)S(1)}, f32[512,128]{1,0:T(8,128)S(1)}) custom-call(bf16[512,256]{1,0:T(8,128)(2,1)S(1)} %get-tuple-element.25.points, s32[16,512]{1,0:T(8,128)S(1)} %get-tuple-element.27.offsets, ...), custom_call_target="tpu_custom_call" | custom-call | flops 1000000000 | bytes 4000000 | tf_op jit(solution)/shard_map/front_inner/pallas_call | solution.py:25
  14.7 0.0 collective-permute-done.above
  14.8 0.0 collective-permute-done.1.below
  14.8 3.1 %front_edges.1 = (bf16[256,256]{1,0:T(8,128)(2,1)S(1)}, bf16[512,384]{1,0:T(8,128)(2,1)S(1)}) custom-call(bf16[128,256]{1,0:T(8,128)(2,1)S(1)} %collective-permute-done.above, bf16[512,256]{1,0:T(8,128)(2,1)S(1)} %get-tuple-element.25.points, bf16[128,256]{1,0:T(8,128)(2,1)S(1)} %collective-permute-done.1.below, s32[16,512]{1,0:T(8,128)S(1)} %get-tuple-element.27.offsets, ...), custom_call_target="tpu_custom_call" | custom-call | flops 1000000000 | bytes 4000000 | tf_op jit(solution)/shard_map/front_edges/pallas_call | solution.py:25
  17.9 0.1 reshape.32
  18.0 32.8 %all_to_all.15 = bf16[128,4,384]{2,1,0:T(4,128)(2,1)S(1)} all-to-all(bf16[128,4,384]{2,1,0:T(4,128)(2,1)S(1)} %reshape.32), channel_id=1, replica_groups=mesh['pts'=128,'ch'=4] {'pts'}, dimensions={0} | all-to-all | bytes 786432 | tf_op jit(solution)/shard_map/all_to_all | solution.py:400
  50.8 0.1 reshape.33.packed
  50.9 3.0 %attend.1 = bf16[512,128]{1,0:T(8,128)(2,1)S(1)} custom-call(bf16[512,384]{1,0:T(8,128)(2,1)S(1)} %reshape.33.packed), custom_call_target="tpu_custom_call" | custom-call | flops 1000000000 | bytes 1000000 | tf_op jit(solution)/shard_map/attend/pallas_call | solution.py:25
  53.9 17.8 %all_to_all.16 = bf16[128,4,128]{2,1,0:T(4,128)(2,1)S(1)} all-to-all(bf16[128,4,128]{2,1,0:T(4,128)(2,1)S(1)} %bitcast.11), channel_id=1, replica_groups=mesh['pts'=128,'ch'=4] {'pts'}, dimensions={0} | all-to-all | bytes 262144 | tf_op jit(solution)/shard_map/all_to_all | solution.py:415
  71.7 0.5 fetch_rows.1
  72.2 9.6 %all_to_all.17.gathered = bf16[4,256,128]{2,1,0:T(8,128)(2,1)S(1)} all-to-all(bf16[4,256,128]{2,1,0:T(8,128)(2,1)S(1)} %fetch_rows.1), channel_id=1, replica_groups=mesh['pts'=128,'ch'=4] {'ch'}, dimensions={0} | all-to-all | bytes 524288 | tf_op jit(solution)/shard_map/all_to_all | solution.py:421
  81.9 1.1 %finish.1 = (bf16[64,512]{1,0:T(8,128)(2,1)}, f32[136,384]{1,0:T(8,128)S(1)}) custom-call(bf16[4,256,128]{2,1,0:T(8,128)(2,1)S(1)} %all_to_all.17.gathered, bf16[256,256]{1,0:T(8,128)(2,1)S(1)} %get-tuple-element.39.edge_res, bf16[256,256]{1,0:T(8,128)(2,1)S(1)} %get-tuple-element.40.inner_res, bf16[256,256]{1,0:T(8,128)(2,1)S(1)} %get-tuple-element.41.proj_weight, ...), custom_call_target="tpu_custom_call" | custom-call | flops 100000000 | bytes 1000000 | tf_op jit(solution)/shard_map/finish/pallas_call | solution.py:25
  83.0 3.7 %collective-permute-start.2 = (f32[8,384]{1,0:T(8,128)S(1)}, f32[8,384]{1,0:T(8,128)S(1)}, u32[]{:S(2)}, u32[]{:S(2)}) collective-permute-start(f32[8,384]{1,0:T(8,128)S(1)} %slice.3), channel_id=1, source_target_pairs={{4,0},{8,4},{12,8},{16,12},{20,16},{24,20},{28,24},{32,28},{36,32}... | collective-permute-start | bytes 36872 | tf_op jit(solution)/shard_map/ppermute | solution.py:431
  86.7 1.7 %collective-permute-done.2.spill = f32[8,384]{1,0:T(8,128)S(1)} collective-permute-done((f32[8,384]{1,0:T(8,128)S(1)}, f32[8,384]{1,0:T(8,128)S(1)}, u32[]{:S(2)}, u32[]{:S(2)}) %collective-permute-start.2) | collective-permute-done | bytes 12320 | tf_op jit(solution)/shard_map/ppermute | solution.py:431
  88.4 0.8 pool.1
  (1 shorter events, 0.0 us)
Async XLA Ops:
  1.9 12.8 %collective-permute-start = (bf16[128,256]{1,0:T(8,128)(2,1)S(1)}, bf16[128,256]{1,0:T(8,128)(2,1)S(1)}, u32[]{:S(2)}, u32[]{:S(2)}) collective-permute-start(bf16[128,256]{1,0:T(8,128)(2,1)S(1)} %get-tuple-element.24), channel_id=1, source_target_pairs={{0,4},{4,8},{8,12},{12,16},{16,20},{20,24},{24,28},{28,32},{32,36}... | collective-permute-start | bytes 196616 | tf_op jit(solution)/shard_map/ppermute | solution.py:362
  6.5 8.2 %collective-permute-start.1 = (bf16[128,256]{1,0:T(8,128)(2,1)S(1)}, bf16[128,256]{1,0:T(8,128)(2,1)S(1)}, u32[]{:S(2)}, u32[]{:S(2)}) collective-permute-start(bf16[128,256]{1,0:T(8,128)(2,1)S(1)} %get-tuple-element.26), channel_id=1, source_target_pairs={{4,0},{8,4},{12,8},{16,12},{20,16},{24,20},{28,24},{32,28},{36,32}... | collective-permute-start | bytes 196616 | tf_op jit(solution)/shard_map/ppermute | solution.py:363
  83.0 5.4 %collective-permute-start.2 = (f32[8,384]{1,0:T(8,128)S(1)}, f32[8,384]{1,0:T(8,128)S(1)}, u32[]{:S(2)}, u32[]{:S(2)}) collective-permute-start(f32[8,384]{1,0:T(8,128)S(1)} %slice.3), channel_id=1, source_target_pairs={{4,0},{8,4},{12,8},{16,12},{20,16},{24,20},{28,24},{32,28},{36,32}... | collective-permute-start | bytes 36872 | tf_op jit(solution)/shard_map/ppermute | solution.py:431

commit v4 on v3

--- a/solution.py
+++ b/solution.py
@@ -15,6 +15,9 @@
 DEAD = -1e30
 SHIFT_BITS = 10
 SHIFT = 1 << SHIFT_BITS
+LEAD = 8
+HALO = G + 2 * LEAD
+EXTRA = 16
 BF = jnp.bfloat16
 F32 = jnp.float32
 VMEM_BYTES = 24 * 1024 * 1024
@@ -52,28 +55,57 @@
     return lax.dot_general(a, b, (((1,), (1,)), ((), ())), preferred_element_type=F32)
 
 
+def lead_facts(offsets, kinds, owners, clusters, first_cluster):
+    own = owners[:, :128]
+    lane = iota(own.shape, 1)
+    slot = jnp.zeros(own.shape, F32)
+    for back in (1, 2):
+        same = (own == jnp.concatenate([own[:, 128 - back :], own[:, : 128 - back]], axis=1)) & (lane >= back)
+        slot = slot + jnp.where(same, 1.0, 0.0)
+    lead = jnp.where(clusters[:, :128] < first_cluster, 1.0, 0.0)
+    lines = [
+        offsets[:, :128].astype(F32),
+        kinds[:, :128].astype(F32),
+        jnp.broadcast_to(own.astype(F32), (8, 128)),
+        jnp.broadcast_to(slot, (8, 128)),
+        jnp.broadcast_to(lead, (8, 128)),
+        jnp.zeros((72, 128), F32),
+    ]
+    return jnp.transpose(jnp.concatenate(lines, axis=0))[:LEAD, :]
+
+
 def stage(count):
     def body(*refs):
-        sources, targets, sems = refs[:count], refs[count:-1], refs[-1]
-        pairs = list(zip(sources, targets[:count], strict=True))
-        points = sources[0]
-        pairs.append((points.at[pl.ds(points.shape[0] - G, G), :], targets[count]))
-        pairs.append((points.at[pl.ds(0, G), :], targets[count + 1]))
-        copies = [pltpu.make_async_copy(a, b, sems.at[n]) for n, (a, b) in enumerate(pairs)]
+        sources, targets = refs[:count], refs[count : 2 * count]
+        first, second, sems = refs[2 * count :]
+        copies = [
+            pltpu.make_async_copy(a, b, sems.at[n]) for n, (a, b) in enumerate(zip(sources, targets, strict=True))
+        ]
         for copy in copies:
             copy.start()
         for copy in copies:
             copy.wait()
+        points, offsets, kinds, owners = targets[:4]
+        clusters = targets[-1]
+        total, width = points.shape
+        index = lax.axis_index("pts")
+        even = lax.rem(index, 2) == 0
+        facts = lead_facts(offsets[...], kinds[...], owners[...], clusters[...], index * (total // 4))
+        facts = jnp.concatenate([facts, jnp.zeros((LEAD, width - 128), F32)], axis=1)
+        head = jnp.concatenate([points[0:G, :].astype(F32), points[G : G + LEAD, :].astype(F32), facts], axis=0)
+        tail = jnp.concatenate([points[total - G :, :].astype(F32), jnp.zeros((2 * LEAD, width), F32)], axis=0)
+        first[...] = jnp.where(even, tail, head).astype(BF)
+        second[...] = jnp.where(even, head, tail).astype(BF)
 
     def run(*args):
         outs = [jax.ShapeDtypeStruct(a.shape, a.dtype) for a in args]
-        outs += [jax.ShapeDtypeStruct((G, args[0].shape[1]), args[0].dtype)] * 2
+        outs += [jax.ShapeDtypeStruct((HALO, args[0].shape[1]), args[0].dtype)] * 2
         return pl.pallas_call(
             body,
             out_shape=outs,
             in_specs=[pl.BlockSpec(memory_space=pltpu.HBM)] * count,
             out_specs=[pl.BlockSpec(memory_space=pltpu.VMEM)] * (count + 2),
-            scratch_shapes=[pltpu.SemaphoreType.DMA((count + 2,))],
+            scratch_shapes=[pltpu.SemaphoreType.DMA((count,))],
             compiler_params=pltpu.CompilerParams(vmem_limit_bytes=VMEM_BYTES),
             name="stage",
         )(*(pltpu.with_memory_space_constraint(a, pltpu.HBM) for a in args))
@@ -81,14 +113,18 @@
     return run
 
 
-def conv_norm_block(points, window, offsets, kinds, weights, gain, bias, between=()):
+def codes(offsets, kinds):
+    rows = offsets.shape[1]
+    target = jnp.transpose(offsets) + iota((rows, offsets.shape[0]), 0) + G
+    return target + jnp.transpose(kinds) * SHIFT
+
+
+def conv_norm_block(points, window, code, weights, gain, bias, between=()):
     rows, span = points.shape[0], window.shape[0]
     between = list(between)
-    target = jnp.transpose(offsets + jnp.transpose(jnp.broadcast_to(iota((rows, 1), 0), (rows, offsets.shape[0]))) + G)
-    code = target + jnp.transpose(kinds) * SHIFT
     conv = jnp.zeros(points.shape, F32)
     group = 4
-    for first in range(0, offsets.shape[0], group):
+    for first in range(0, code.shape[1], group):
         picks, marks = [], []
         for n in range(first, first + group):
             value = jnp.broadcast_to(code[:, n : n + 1], (rows, 128))
@@ -161,8 +197,7 @@
         res, nor = conv_norm_block(
             points[rows, :],
             window,
-            offsets[:, rows],
-            kinds[:, rows],
+            codes(offsets[:, rows], kinds[:, rows]),
             weights,
             gain[...],
             bias[...],
@@ -174,28 +209,66 @@
 
 
 def front_edges(
-    above, points, below, offsets, kinds, conv_weight, gain, bias, qkv_weight, inner, place, dead, residual, out, normed
+    got_first,
+    got_second,
+    points,
+    offsets,
+    kinds,
+    conv_weight,
+    gain,
+    bias,
+    qkv_weight,
+    inner,
+    place,
+    dead,
+    residual,
+    out,
+    extra_res,
+    extra_fetch,
+    extra_lead,
+    normed,
 ):
-    total = points.shape[0]
+    total, width = points.shape
     weights = padded_weights(conv_weight[...])
     last = total - ROWS
-    for start, window in (
-        (0, jnp.concatenate([above[...], points[0 : ROWS + G, :]], axis=0)),
-        (last, jnp.concatenate([points[last - G :, :], below[...]], axis=0)),
-    ):
-        rows = slice(start, start + ROWS)
-        res, nor = conv_norm_block(
-            points[rows, :], window, offsets[:, rows], kinds[:, rows], weights, gain[...], bias[...]
-        )
-        residual[(0 if start == 0 else ROWS) : (ROWS if start == 0 else 2 * ROWS), :] = res
-        normed[rows, :] = nor
+    even = lax.rem(lax.axis_index("pts"), 2) == 0
+    one, two = got_first[...].astype(F32), got_second[...].astype(F32)
+    above = jnp.where(even, two[:G], one[:G]).astype(BF)
+    below = jnp.where(even, one, two)
+    facts = below[G + LEAD :, :128]
+    window = jnp.concatenate([above, points[0 : ROWS + G, :]], axis=0)
+    res, nor = conv_norm_block(
+        points[0:ROWS, :], window, codes(offsets[:, :ROWS], kinds[:, :ROWS]), weights, gain[...], bias[...]
+    )
+    residual[0:ROWS, :] = res
+    normed[0:ROWS, :] = nor
     normed[ROWS:last, :] = inner[...]
+    near = offsets.shape[0]
+    facts_int = facts.astype(jnp.int32)
+    extra_code = facts_int[:, :near] + iota((LEAD, near), 0) + ROWS + G + facts_int[:, near : 2 * near] * SHIFT
+    blank = jnp.zeros((EXTRA - LEAD, near), jnp.int32)
+    code = jnp.concatenate([codes(offsets[:, last:], kinds[:, last:]), extra_code, blank], axis=0)
+    reach = below[: G + LEAD]
+    fill = jnp.zeros((512 - 2 * ROWS - G - LEAD, width), F32)
+    window = jnp.concatenate([points[last - G :, :], jnp.concatenate([reach, fill], axis=0).astype(BF)], axis=0)
+    more = jnp.concatenate([reach[:LEAD], jnp.zeros((EXTRA - LEAD, width), F32)], axis=0).astype(BF)
+    res, nor = conv_norm_block(
+        jnp.concatenate([points[last:, :], more], axis=0), window, code, weights, gain[...], bias[...]
+    )
+    residual[ROWS:, :] = res[:ROWS]
+    normed[last:, :] = nor[:ROWS]
+    extra_res[...] = res[ROWS:]
+    slots = out.shape[0]
+    full = jnp.concatenate([facts, jnp.zeros((EXTRA - LEAD, 128), F32)], axis=0)
+    owner, slot, lead = (full[:, 2 * near + 8 * n : 2 * near + 8 * n + 1] for n in range(3))
+    spot = (owner * HALF_SLOTS + slot).astype(jnp.int32)
+    extra_fetch[...] = hot(spot == iota((EXTRA, slots), 1))
+    extra_lead[...] = jnp.broadcast_to(lead, (EXTRA, 128))
     q, k, v = (qkv_weight[t] for t in range(3))
     none = jnp.zeros(q.shape, BF)
     left = jnp.concatenate([q, none, k, none, v, none], axis=0)
     right = jnp.concatenate([none, q, none, k, none, v], axis=0)
     placed = dot(place[...], normed[...]).astype(BF)
-    slots = out.shape[0]
     packed = dot_t(
         jnp.concatenate([placed[:slots], placed[slots:]], axis=1), jnp.concatenate([left, right], axis=1)
     )
@@ -207,7 +280,7 @@
     return jnp.concatenate([value[:, 64:], value[:, :64]], axis=1)
 
 
-def attend(packed, out, keys, queries, values):
+def attend(packed, out, keys, queries, values, kept):
     half = packed.shape[0]
     lane = iota((half, 128), 1)
     q = packed[:, 0:128]
@@ -257,12 +330,16 @@
             done = []
             moved = jnp.concatenate([second[:, 64:], second[:, :64]], axis=1)
             rows = slice((chunk // 2) * step, (chunk // 2 + 1) * step)
-            out[rows, :] = jnp.where(block_lane < 64, first, moved).astype(BF)
-
-
-def fetch_rows(returned, fetch, out):
+            both = jnp.where(block_lane < 64, first, moved)
+            out[rows, :128] = both.astype(BF)
+            kept[rows, :] = both
+    kept[half:, :] = jnp.zeros((8, 128), F32)
+    out[:, 128:] = kept[HALF_SLOTS : half + HALF_SLOTS, :].astype(BF)
+
+
+def fetch_rows(returned, fetch, extra_fetch, out):
     half = returned.shape[0]
-    value = returned[...]
+    value = returned[:, :128]
     lane = iota((half, 128), 1)
     zero = jnp.zeros((half, 128), BF)
     moved = swap_halves(value)
@@ -270,11 +347,25 @@
     right = jnp.concatenate([jnp.where(lane < 64, zero, moved), jnp.where(lane < 64, zero, value)], axis=0)
     points = fetch.shape[0] // 2
     rows = (dot(fetch[:points, :], left) + dot(fetch[points:, :], right)).astype(BF)
+    extra = dot(extra_fetch[...], returned[:, 128:]).astype(BF)
     for peer in range(out.shape[0]):
-        out[peer] = rows
-
-
-def finish(gathered, edge_res, inner_res, proj_weight, clusters, block_out, sums, block):
+        out[peer, :points, :] = rows
+        out[peer, points:, :] = extra
+
+
+def finish(
+    gathered,
+    edge_res,
+    inner_res,
+    extra_res,
+    extra_lead,
+    proj_weight,
+    pool_weight,
+    clusters,
+    block_out,
+    pooled,
+    block,
+):
     channels = gathered.shape[0]
     width = proj_weight.shape[1]
     part = width // channels
@@ -289,35 +380,30 @@
     points = block.shape[0] // 2
     last = 2 * points - ROWS
     first = dot(wide, jnp.concatenate(low, axis=0))
-    second = dot(wide, jnp.concatenate(high, axis=0))
+    second = dot(wide[:points], jnp.concatenate(high, axis=0))
     block[0:ROWS, :] = (edge_res[0:ROWS, :].astype(F32) + first[0:ROWS]).astype(BF)
-    block[ROWS:points, :] = (inner_res[0 : points - ROWS, :].astype(F32) + first[ROWS:]).astype(BF)
+    block[ROWS:points, :] = (inner_res[0 : points - ROWS, :].astype(F32) + first[ROWS:points]).astype(BF)
     block[points:last, :] = (inner_res[points - ROWS :, :].astype(F32) + second[: last - points]).astype(BF)
     block[last:, :] = (edge_res[ROWS:, :].astype(F32) + second[last - points :]).astype(BF)
+    extra = (extra_res[...].astype(F32) + first[points:]).astype(BF).astype(F32)
+    lead = extra_lead[...]
+    spill = jnp.sum(jnp.where(lead[:, 0:1] > 0.5, extra, 0.0), axis=0, keepdims=True)
+    spill_count = jnp.sum(lead, axis=0, keepdims=True)
     full = block[...]
     channel = lax.axis_index("ch")
     pick = hot(iota((part, width), 1) == iota((part, width), 0) + channel * part)
     block_out[...] = dot_t(pick, full).astype(BF)
-    count = 2 * points // 4
-    base = lax.axis_index("pts") * count - 1
-    rows = sums.shape[0]
-    member = jnp.where(iota((rows, 2 * points), 0) == clusters[...] - base, 1.0, 0.0)
-    sums[:, :width] = dot(member.astype(BF), full)
-    sums[:, width:] = jnp.broadcast_to(jnp.sum(member, axis=1, keepdims=True), (rows, 128))
-
-
-def pool(sums, spill, pool_weight, out):
-    count = out.shape[0]
-    width = pool_weight.shape[0]
-    own = sums[1 : count + 1, :]
-    total = jnp.where(iota(own.shape, 0) == count - 1, own + spill[0:1, :], own)
-    value = total[:, :width]
-    high = value.astype(BF)
-    low = (value - high.astype(F32)).astype(BF)
+    count = pooled.shape[0]
+    base = lax.axis_index("pts") * count
+    member = jnp.where(iota((count, 2 * points), 0) == clusters[...] - base, 1.0, 0.0)
+    final = iota((count, 1), 0) == count - 1
+    value = dot(member.astype(BF), full) + jnp.where(final, spill, 0.0)
+    number = jnp.sum(member, axis=1, keepdims=True) + jnp.where(final, spill_count, 0.0)
+    upper = value.astype(BF)
+    lower = (value - upper.astype(F32)).astype(BF)
     weight = pool_weight[...]
-    lifted = dot(high, weight) + dot(low, weight)
-    mean = lifted / total[:, width:]
-    out[...] = (mean * (1.0 + lax.erf(mean * math.sqrt(0.5))) * 0.5).astype(BF)
+    mean = (dot(upper, weight) + dot(lower, weight)) / number
+    pooled[...] = (mean * (1.0 + lax.erf(mean * math.sqrt(0.5))) * 0.5).astype(BF)
 
 
 def shape(dims, kind=BF):
@@ -340,8 +426,8 @@
     total, width = points_in.shape
     nodes = lax.axis_size("pts")
     channels = lax.axis_size("ch")
-    up = [(i, i + 1) for i in range(nodes - 1)]
-    down = [(j, i) for i, j in up]
+    inside = [(i, i ^ 1) for i in range(nodes)]
+    across = [(i, ((i + 1) ^ 1) - 1) for i in range(1, nodes - 1)]
     offsets, kinds = jnp.transpose(neighbor_offsets), jnp.transpose(kernel_ids)
     args = (
         points_in,
@@ -358,9 +444,9 @@
     )
     staged = stage(len(args))(*args)
     points, offsets, kinds, own, conv_weight, gain, bias, qkv_weight, proj_weight, pool_weight = staged[:10]
-    clusters_here, tail, head = staged[10:]
-    above = lax.ppermute(tail, "pts", up)
-    below = lax.ppermute(head, "pts", down)
+    clusters_here, first, second = staged[10:]
+    got_first = lax.ppermute(first, "pts", inside)
+    got_second = lax.ppermute(second, "pts", across)
     slots = nodes * HALF_SLOTS
     inner_rows = total - 2 * ROWS
     inner_res, inner_normed, place, fetch, dead = call(
@@ -376,17 +462,23 @@
         nbytes=4 * 10**6,
         name="front_inner",
     )(points, offsets, kinds, own, conv_weight, gain, bias)
-    edge_res, packed = call(
+    edge_res, packed, extra_res, extra_fetch, extra_lead = call(
         front_edges,
-        (shape((2 * ROWS, width)), shape((slots, 384))),
+        (
+            shape((2 * ROWS, width)),
+            shape((slots, 384)),
+            shape((EXTRA, width)),
+            shape((EXTRA, slots)),
+            shape((EXTRA, 128), F32),
+        ),
         scratch=(pltpu.VMEM((total, width), BF),),
         flops=10**9,
         nbytes=4 * 10**6,
         name="front_edges",
     )(
-        above,
+        got_first,
+        got_second,
         points,
-        below,
         offsets,
         kinds,
         conv_weight,
@@ -402,36 +494,32 @@
     ).reshape(slots, 384)
     attended = call(
         attend,
-        shape((slots, 128)),
+        shape((slots, 256)),
         scratch=(
             pltpu.VMEM((2 * slots, 128), BF),
             pltpu.VMEM((4 * slots, 128), BF),
             pltpu.VMEM((2 * slots, 128), BF),
+            pltpu.VMEM((slots + 8, 128), F32),
         ),
         flops=10**9,
         nbytes=10**6,
         name="attend",
     )(arrived)
     returned = lax.all_to_all(
-        attended.reshape(nodes, HALF_SLOTS, 128), "pts", split_axis=0, concat_axis=0, tiled=True
-    ).reshape(slots, 128)
+        attended.reshape(nodes, HALF_SLOTS, 256), "pts", split_axis=0, concat_axis=0, tiled=True
+    ).reshape(slots, 256)
     rows = call(
-        fetch_rows, shape((channels, total // 2, 128)), flops=10**8, nbytes=10**6, name="fetch_rows"
-    )(returned, fetch)
+        fetch_rows, shape((channels, total // 2 + EXTRA, 128)), flops=10**8, nbytes=10**6, name="fetch_rows"
+    )(returned, fetch, extra_fetch)
     gathered = lax.all_to_all(rows, "ch", split_axis=0, concat_axis=0, tiled=True)
-    clusters = total // 4
-    block_out, sums = call(
+    block_out, pooled = call(
         finish,
-        (shape((width // channels, total)), shape((clusters + 8, width + 128), F32)),
+        (shape((width // channels, total)), shape((total // 4, pool_weight.shape[1]))),
         scratch=(pltpu.VMEM((total, width), BF),),
         flops=10**8,
         nbytes=10**6,
         name="finish",
-    )(gathered, edge_res, inner_res, proj_weight, clusters_here)
-    spill = lax.ppermute(sums[:8], "pts", down)
-    pooled = call(pool, shape((clusters, pool_weight.shape[1])), flops=10**7, nbytes=10**5, name="pool")(
-        sums, spill, pool_weight
-    )
+    )(gathered, edge_res, inner_res, extra_res, extra_lead, proj_weight, pool_weight, clusters_here)
     return jnp.transpose(block_out), pooled
 
 

time: 89.5 us -> 86 us (0.961)
  starting transfers between devices: 13.8 us -> 10.7 us
    ppermute x3 -> x2, starting transfers between devices: 13.8 us -> 10.7 us  [the longest x1 8.75 us: shards(): got_first = lax.ppermute(first, 'pts', inside)]
    all_to_all x1, blocking collectives: 17.8 us -> 20.3 us  [shards(): lax.all_to_all(attended.reshape(nodes, HALF_SLOTS, 256), 'pts', split_axi...]
    all_to_all x1, blocking collectives: 32.8 us -> 30.4 us  [shards(): lax.all_to_all(packed.reshape(nodes, HALF_SLOTS, 384), 'pts', split_axis=...]
    pallas_call x7 -> x6, Pallas kernels: 12.6 us -> 12.1 us  [run(): pl.pallas_call(body, out_shape=outs, in_specs=[pl.BlockSpec(memory_space=...]
  transfers between devices with their start and end apart: 3 -> 2, of which waited for: 1 -> 1; matrix products, arithmetic and copies ran while one was open for 0% -> 0% of each run, Pallas kernels for 3% -> 3%
where the time goes in v4:
time: 86 us; the launch traced here: 85.7 us
  blocking collectives  60.9 us (71%)
  Pallas kernels  12.1 us (14%)
  starting transfers between devices  10.7 us (12%)
  waiting for transfers between devices  1.07 us (1%)
    all_to_all x1, blocking collectives, shards(): lax.all_to_all(packed.reshape(nodes, HALF_SLOTS, 384), 'pts', split_axis=...  30.4 us
    all_to_all x1, blocking collectives, shards(): lax.all_to_all(attended.reshape(nodes, HALF_SLOTS, 256), 'pts', split_axi...  20.3 us
    pallas_call x6, Pallas kernels, run(): pl.pallas_call(body, out_shape=outs, in_specs=[pl.BlockSpec(memory_space=...  12.1 us
    all_to_all x1, blocking collectives, shards(): lax.all_to_all(rows, 'ch', split_axis=0, concat_axis=0, tiled=True)  10.1 us
    ppermute x1, starting transfers between devices, shards(): got_first = lax.ppermute(first, 'pts', inside)  8.75 us
    ppermute x1, starting transfers between devices, shards(): got_second = lax.ppermute(second, 'pts', across)  1.92 us
  transfers between devices with their start and end apart: 2, of which 1 were waited for; matrix products, arithmetic and copies ran while one was open for 0% of the time, Pallas kernels for 3%

profile of v4, /device:TPU:1, one launch (start us, length us, event | category | flops | bytes accessed | tf_op | source)
XLA Modules:
  0.0 85.7 jit_solution(3552197469224372611)
XLA Ops:
  0.6 1.4 %stage.1 = (bf16[512,256]{1,0:T(8,128)(2,1)S(1)}, s32[16,512]{1,0:T(8,128)S(1)}, s32[16,512]{1,0:T(8,128)S(1)}, s32[1,512]{1,0:T(1,128)S(1)}, bf16[27,256]{1,0:T...) custom-call(bf16[512,256]{1,0:T(8,128)(2,1)} %refs_0_.1, ...), custom_call_target="tpu_custom_call" | custom-call | tf_op jit(solution)/shard_map/stage/pallas_call | solution.py:103
  2.0 8.7 %collective-permute-start = (bf16[144,256]{1,0:T(8,128)(2,1)S(1)}, bf16[144,256]{1,0:T(8,128)(2,1)S(1)}, u32[]{:S(2)}, u32[]{:S(2)}) collective-permute-start(bf16[144,256]{1,0:T(8,128)(2,1)S(1)} %get-tuple-element.27), channel_id=1, source_target_pairs={{0,4},{4,0},{8,12},{12,8},{16,20},{20,16},{24,28},{28,24},{32,36},... | collective-permute-start | bytes 221192 | tf_op jit(solution)/shard_map/ppermute | solution.py:448
  10.8 1.9 %collective-permute-start.1 = (bf16[144,256]{1,0:T(8,128)(2,1)S(1)}, bf16[144,256]{1,0:T(8,128)(2,1)S(1)}, u32[]{:S(2)}, u32[]{:S(2)}) collective-permute-start(bf16[144,256]{1,0:T(8,128)(2,1)S(1)} %get-tuple-element.28), channel_id=1, source_target_pairs={{4,8},{8,4},{12,16},{16,12},{20,24},{24,20},{28,32},{32,28},{36,40... | collective-permute-start | bytes 221192 | tf_op jit(solution)/shard_map/ppermute | solution.py:449
  12.7 2.7 %front_inner.1 = (bf16[256,256]{1,0:T(8,128)(2,1)S(1)}, bf16[256,256]{1,0:T(8,128)(2,1)S(1)}, bf16[1024,512]{1,0:T(8,128)(2,1)S(1)}, bf16[512,1024]{1,0:T(8,128)(2,1)S(1)}, f32[512,128]{1,0:T(8,128)S(1)}) custom-call(bf16[512,256]{1,0:T(8,128)(2,1)S(1)} %get-tuple-element.29.points, s32[16,512]{1,0:T(8,128)S(1)} %get-tuple-element.30.offsets, ...), custom_call_target="tpu_custom_call" | custom-call | flops 1000000000 | bytes 4000000 | tf_op jit(solution)/shard_map/front_inner/pallas_call | solution.py:28
  15.4 0.0 collective-permute-done.got_first
  15.4 1.1 %collective-permute-done.1.got_second = bf16[144,256]{1,0:T(8,128)(2,1)S(1)} collective-permute-done((bf16[144,256]{1,0:T(8,128)(2,1)S(1)}, bf16[144,256]{1,0:T(8,128)(2,1)S(1)}, u32[]{:S(2)}, u32[]{:S(2)}) %collective-permute-start.1) | collective-permute-done | bytes 73760 | tf_op jit(solution)/shard_map/ppermute | solution.py:449
  16.4 3.2 %front_edges.1 = (bf16[256,256]{1,0:T(8,128)(2,1)S(1)}, bf16[512,384]{1,0:T(8,128)(2,1)S(1)}, bf16[16,256]{1,0:T(8,128)(2,1)S(1)}, bf16[16,512]{1,0:T(8,128)(2,1)S(1)}, f32[16,128]{1,0:T(8,128)S(1)}) custom-call(bf16[144,256]{1,0:T(8,128)(2,1)S(1)} %collective-permute-done.got_first, bf16[144,256]{1,0:T(8,128)(2,1)S(1)} %collective-permute-done.1.got_second, ...), custom_call_target="tpu_custom_call" | custom-call | flops 1000000000 | bytes 4000000 | tf_op jit(solution)/shard_map/front_edges/pallas_call | solution.py:28
  19.6 0.1 reshape.32
  19.7 30.4 %all_to_all.15 = bf16[128,4,384]{2,1,0:T(4,128)(2,1)S(1)} all-to-all(bf16[128,4,384]{2,1,0:T(4,128)(2,1)S(1)} %reshape.32), channel_id=1, replica_groups=mesh['pts'=128,'ch'=4] {'pts'}, dimensions={0} | all-to-all | bytes 786432 | tf_op jit(solution)/shard_map/all_to_all | solution.py:492
  50.2 0.1 reshape.33.packed
  50.3 3.0 %attend.1 = bf16[512,256]{1,0:T(8,128)(2,1)S(1)} custom-call(bf16[512,384]{1,0:T(8,128)(2,1)S(1)} %reshape.33.packed), custom_call_target="tpu_custom_call" | custom-call | flops 1000000000 | bytes 1000000 | tf_op jit(solution)/shard_map/attend/pallas_call | solution.py:28
  53.3 0.1 reshape.34
  53.4 20.3 %all_to_all.16 = bf16[128,4,256]{2,1,0:T(4,128)(2,1)S(1)} all-to-all(bf16[128,4,256]{2,1,0:T(4,128)(2,1)S(1)} %reshape.34), channel_id=1, replica_groups=mesh['pts'=128,'ch'=4] {'pts'}, dimensions={0} | all-to-all | bytes 524288 | tf_op jit(solution)/shard_map/all_to_all | solution.py:508
  73.7 0.1 reshape.35.returned
  73.8 0.5 fetch_rows.1
  74.3 10.1 %all_to_all.17.gathered = bf16[4,272,128]{2,1,0:T(8,128)(2,1)S(1)} all-to-all(bf16[4,272,128]{2,1,0:T(8,128)(2,1)S(1)} %fetch_rows.1), channel_id=1, replica_groups=mesh['pts'=128,'ch'=4] {'ch'}, dimensions={0} | all-to-all | bytes 557056 | tf_op jit(solution)/shard_map/all_to_all | solution.py:514
  84.4 1.3 %finish.1 = (bf16[64,512]{1,0:T(8,128)(2,1)}, bf16[128,128]{1,0:T(8,128)(2,1)}) custom-call(bf16[4,272,128]{2,1,0:T(8,128)(2,1)S(1)} %all_to_all.17.gathered, bf16[256,256]{1,0:T(8,128)(2,1)S(1)} %get-tuple-element.43.edge_res, bf16[256,256]{1,0:T(8,128)(2,1)S(1)} %get-tuple-element.44.inner_res, bf16[16,256]{1,0:T(8,128)(2,1)S(1)} %get-tuple-element.45.extra_res, ...), custom_call_target="tpu_custom_call" | custom-call | flops 100000000 | bytes 1000000 | tf_op jit(solution)/shard_map/finish/pallas_call | solution.py:28
Async XLA Ops:
  2.0 13.4 %collective-permute-start = (bf16[144,256]{1,0:T(8,128)(2,1)S(1)}, bf16[144,256]{1,0:T(8,128)(2,1)S(1)}, u32[]{:S(2)}, u32[]{:S(2)}) collective-permute-start(bf16[144,256]{1,0:T(8,128)(2,1)S(1)} %get-tuple-element.27), channel_id=1, source_target_pairs={{0,4},{4,0},{8,12},{12,8},{16,20},{20,16},{24,28},{28,24},{32,36},... | collective-permute-start | bytes 221192 | tf_op jit(solution)/shard_map/ppermute | solution.py:448
  10.8 5.7 %collective-permute-start.1 = (bf16[144,256]{1,0:T(8,128)(2,1)S(1)}, bf16[144,256]{1,0:T(8,128)(2,1)S(1)}, u32[]{:S(2)}, u32[]{:S(2)}) collective-permute-start(bf16[144,256]{1,0:T(8,128)(2,1)S(1)} %get-tuple-element.28), channel_id=1, source_target_pairs={{4,8},{8,4},{12,16},{16,12},{20,24},{24,20},{28,32},{32,28},{36,40... | collective-permute-start | bytes 221192 | tf_op jit(solution)/shard_map/ppermute | solution.py:449

commit v5 on v4

--- a/solution.py
+++ b/solution.py
@@ -18,6 +18,7 @@
 LEAD = 8
 HALO = G + 2 * LEAD
 EXTRA = 16
+GROUP = 4
 BF = jnp.bfloat16
 F32 = jnp.float32
 VMEM_BYTES = 24 * 1024 * 1024
@@ -113,34 +114,57 @@
     return run
 
 
-def codes(offsets, kinds):
+def codes(offsets, kinds=None):
     rows = offsets.shape[1]
     target = jnp.transpose(offsets) + iota((rows, offsets.shape[0]), 0) + G
-    return target + jnp.transpose(kinds) * SHIFT
-
-
-def conv_norm_block(points, window, code, weights, gain, bias, between=()):
-    rows, span = points.shape[0], window.shape[0]
+    return target if kinds is None else target + jnp.transpose(kinds) * SHIFT
+
+
+def windowed_sum(code, shift, window, scale_of, between=()):
+    rows, span = code.shape[0], window.shape[0]
     between = list(between)
-    conv = jnp.zeros(points.shape, F32)
-    group = 4
-    for first in range(0, code.shape[1], group):
-        picks, marks = [], []
-        for n in range(first, first + group):
-            value = jnp.broadcast_to(code[:, n : n + 1], (rows, 128))
-            place, kind = value & (SHIFT - 1), lax.shift_right_logical(value, SHIFT_BITS)
-            wide = jnp.concatenate([hot(place == iota((rows, 128), 1) + lanes) for lanes in range(0, span, 128)], axis=1)
-            picks.append(wide)
-            marks.append(hot(kind == iota((rows, 128), 1)))
+    conv = jnp.zeros((rows, window.shape[1]), F32)
+    for first in range(0, code.shape[1], GROUP):
+        picks, kinds = [], []
+        for n in range(first, first + GROUP):
+            place = jnp.broadcast_to(code[:, n : n + 1], (rows, 128))
+            if scale_of.marked:
+                kinds.append(lax.shift_right_logical(place, SHIFT_BITS))
+                place = place & (SHIFT - 1)
+            lane = iota((rows, 128), 1) + shift
+            picks.append(jnp.concatenate([hot(place == lane + lanes) for lanes in range(0, span, 128)], axis=1))
         picked = dot(jnp.concatenate(picks, axis=0), window)
-        scale = dot(jnp.concatenate(marks, axis=0), weights)
-        part = picked * scale
-        for n in range(group):
+        part = picked * scale_of(first // GROUP, kinds)
+        for n in range(GROUP):
             conv = conv + part[n * rows : (n + 1) * rows]
         if between:
             between.pop(0)()
     for step in between:
         step()
+    return conv
+
+
+def scale_by(weights, keep=None):
+    def scale_of(group, kinds):
+        marks = [hot(kind == iota(kind.shape, 1)) for kind in kinds]
+        scale = dot(jnp.concatenate(marks, axis=0), weights)
+        if keep is not None:
+            keep[group] = scale.astype(BF)
+        return scale
+
+    scale_of.marked = True
+    return scale_of
+
+
+def kept_scale(kept):
+    def scale_of(group, kinds):
+        return kept[group].astype(F32)
+
+    scale_of.marked = False
+    return scale_of
+
+
+def normalize(points, conv, gain, bias):
     residual = (points.astype(F32) + conv).astype(BF)
     features = residual.astype(F32)
     average = jnp.mean(features, axis=1, keepdims=True)
@@ -156,7 +180,23 @@
     return jnp.concatenate([conv_weight.astype(F32), fill], axis=0).astype(BF)
 
 
-def front_inner(points, offsets, kinds, owners, conv_weight, gain, bias, residual, normed, place, fetch, dead):
+def front_inner(
+    points,
+    offsets,
+    kinds,
+    owners,
+    conv_weight,
+    gain,
+    bias,
+    residual,
+    normed,
+    place,
+    fetch,
+    dead,
+    partial,
+    top_scale,
+    end_scale,
+):
     total = points.shape[0]
     weights = padded_weights(conv_weight[...])
     slots = place.shape[0] // 2
@@ -168,7 +208,9 @@
     slot = jnp.sum(jnp.where(match, earlier, 0.0), axis=0, keepdims=True).astype(jnp.int32)
     low = own * HALF_SLOTS + (slot & (HALF_SLOTS - 1))
     spot = jnp.where(slot >= HALF_SLOTS, low + slots, low)
-    column = jnp.transpose(jnp.broadcast_to(spot, (8, total)))[:, 0:1]
+    quarter = (slot >> 2) * 2 + (slot & 1)
+    back = quarter * (2 * peers) + own * 2 + ((slot & (HALF_SLOTS - 1)) >> 1)
+    column = jnp.transpose(jnp.broadcast_to(back, (8, total)))[:, 0:1]
 
     def build_place(start):
         lane = iota((ROWS, 128), 1)
@@ -190,22 +232,36 @@
     pieces = [functools.partial(build_place, n) for n in range(0, slots, ROWS)]
     pieces += [functools.partial(build_fetch, n) for n in range(0, total, ROWS)]
     blocks = range(1, total // ROWS - 1)
-    share = len(pieces) // len(blocks)
+    share = len(pieces) // (len(blocks) + 2)
     for block in blocks:
         rows = slice(block * ROWS, (block + 1) * ROWS)
         window = points[block * ROWS - G : (block + 1) * ROWS + G, :]
-        res, nor = conv_norm_block(
-            points[rows, :],
+        conv = windowed_sum(
+            codes(offsets[:, rows], kinds[:, rows]),
+            0,
             window,
-            codes(offsets[:, rows], kinds[:, rows]),
-            weights,
-            gain[...],
-            bias[...],
+            scale_by(weights),
             pieces[(block - 1) * share : block * share],
         )
+        res, nor = normalize(points[rows, :], conv, gain[...], bias[...])
         out = slice((block - 1) * ROWS, block * ROWS)
         residual[out, :] = res
         normed[out, :] = nor
+    last = total - ROWS
+    partial[0:ROWS, :] = windowed_sum(
+        codes(offsets[:, :ROWS], kinds[:, :ROWS]),
+        G,
+        points[0 : ROWS + G, :],
+        scale_by(weights, top_scale),
+        pieces[2 * share : 3 * share],
+    )
+    partial[ROWS:, :] = windowed_sum(
+        codes(offsets[:, last:], kinds[:, last:]),
+        0,
+        points[last - G :, :],
+        scale_by(weights, end_scale),
+        pieces[3 * share :],
+    )
 
 
 def front_edges(
@@ -221,6 +277,9 @@
     inner,
     place,
     dead,
+    partial,
+    top_scale,
+    end_scale,
     residual,
     out,
     extra_res,
@@ -236,32 +295,37 @@
     above = jnp.where(even, two[:G], one[:G]).astype(BF)
     below = jnp.where(even, one, two)
     facts = below[G + LEAD :, :128]
-    window = jnp.concatenate([above, points[0 : ROWS + G, :]], axis=0)
-    res, nor = conv_norm_block(
-        points[0:ROWS, :], window, codes(offsets[:, :ROWS], kinds[:, :ROWS]), weights, gain[...], bias[...]
-    )
+    conv = partial[0:ROWS, :] + windowed_sum(
+        codes(offsets[:, :ROWS]), 0, above, kept_scale(top_scale)
+    )
+    res, nor = normalize(points[0:ROWS, :], conv, gain[...], bias[...])
     residual[0:ROWS, :] = res
     normed[0:ROWS, :] = nor
     normed[ROWS:last, :] = inner[...]
+    conv = partial[ROWS:, :] + windowed_sum(
+        codes(offsets[:, last:]),
+        ROWS + G,
+        below[:G].astype(BF),
+        kept_scale(end_scale),
+    )
+    res, nor = normalize(points[last:, :], conv, gain[...], bias[...])
+    residual[ROWS:, :] = res
+    normed[last:, :] = nor
     near = offsets.shape[0]
     facts_int = facts.astype(jnp.int32)
-    extra_code = facts_int[:, :near] + iota((LEAD, near), 0) + ROWS + G + facts_int[:, near : 2 * near] * SHIFT
+    extra_code = facts_int[:, :near] + iota((LEAD, near), 0) + G + facts_int[:, near : 2 * near] * SHIFT
     blank = jnp.zeros((EXTRA - LEAD, near), jnp.int32)
-    code = jnp.concatenate([codes(offsets[:, last:], kinds[:, last:]), extra_code, blank], axis=0)
     reach = below[: G + LEAD]
-    fill = jnp.zeros((512 - 2 * ROWS - G - LEAD, width), F32)
-    window = jnp.concatenate([points[last - G :, :], jnp.concatenate([reach, fill], axis=0).astype(BF)], axis=0)
-    more = jnp.concatenate([reach[:LEAD], jnp.zeros((EXTRA - LEAD, width), F32)], axis=0).astype(BF)
-    res, nor = conv_norm_block(
-        jnp.concatenate([points[last:, :], more], axis=0), window, code, weights, gain[...], bias[...]
-    )
-    residual[ROWS:, :] = res[:ROWS]
-    normed[last:, :] = nor[:ROWS]
-    extra_res[...] = res[ROWS:]
+    fill = jnp.zeros((256 - G - LEAD, width), F32)
+    window = jnp.concatenate([points[last:, :], jnp.concatenate([reach, fill], axis=0).astype(BF)], axis=0)
+    more = jnp.concatenate([reach[:LEAD], jnp.zeros((EXTRA - LEAD, width), F32)], axis=0)
+    conv = windowed_sum(jnp.concatenate([extra_code, blank], axis=0), 0, window, scale_by(weights))
+    extra_res[...] = (more + conv).astype(BF)
     slots = out.shape[0]
     full = jnp.concatenate([facts, jnp.zeros((EXTRA - LEAD, 128), F32)], axis=0)
     owner, slot, lead = (full[:, 2 * near + 8 * n : 2 * near + 8 * n + 1] for n in range(3))
-    spot = (owner * HALF_SLOTS + slot).astype(jnp.int32)
+    index = slot.astype(jnp.int32)
+    spot = (index & 1) * (slots // 2) + owner.astype(jnp.int32) * 2 + (index >> 1)
     extra_fetch[...] = hot(spot == iota((EXTRA, slots), 1))
     extra_lead[...] = jnp.broadcast_to(lead, (EXTRA, 128))
     q, k, v = (qkv_weight[t] for t in range(3))
@@ -331,23 +395,28 @@
             moved = jnp.concatenate([second[:, 64:], second[:, :64]], axis=1)
             rows = slice((chunk // 2) * step, (chunk // 2 + 1) * step)
             both = jnp.where(block_lane < 64, first, moved)
-            out[rows, :128] = both.astype(BF)
             kept[rows, :] = both
     kept[half:, :] = jnp.zeros((8, 128), F32)
-    out[:, 128:] = kept[HALF_SLOTS : half + HALF_SLOTS, :].astype(BF)
+    pairs = half // 2
+    lane = iota((pairs, 128), 1)
+    out[:, :128] = kept[pl.ds(0, pairs, stride=2), :].astype(BF)
+    out[:, 128:256] = kept[pl.ds(1, pairs, stride=2), :].astype(BF)
+    near, far = kept[pl.ds(HALF_SLOTS, pairs, stride=2), :], kept[pl.ds(HALF_SLOTS + 1, pairs, stride=2), :]
+    out[:, 256:] = jnp.where(lane < 64, near, swap_halves(far)).astype(BF)
 
 
 def fetch_rows(returned, fetch, extra_fetch, out):
-    half = returned.shape[0]
-    value = returned[:, :128]
-    lane = iota((half, 128), 1)
-    zero = jnp.zeros((half, 128), BF)
-    moved = swap_halves(value)
-    left = jnp.concatenate([jnp.where(lane < 64, value, zero), jnp.where(lane < 64, moved, zero)], axis=0)
-    right = jnp.concatenate([jnp.where(lane < 64, zero, moved), jnp.where(lane < 64, zero, value)], axis=0)
+    tiles = [returned[:, n * 128 : (n + 1) * 128] for n in range(3)]
+    lane = iota(tiles[0].shape, 1)
+    zero = jnp.zeros(tiles[0].shape, BF)
+    moved = [swap_halves(tile) for tile in tiles]
+    order = [tiles[0], tiles[1], moved[0], moved[1]]
+    other = [moved[0], moved[1], tiles[0], tiles[1]]
+    left = jnp.concatenate([jnp.where(lane < 64, tile, zero) for tile in order], axis=0)
+    right = jnp.concatenate([jnp.where(lane < 64, zero, tile) for tile in other], axis=0)
     points = fetch.shape[0] // 2
     rows = (dot(fetch[:points, :], left) + dot(fetch[points:, :], right)).astype(BF)
-    extra = dot(extra_fetch[...], returned[:, 128:]).astype(BF)
+    extra = dot(extra_fetch[...], jnp.concatenate([tiles[2], moved[2]], axis=0)).astype(BF)
     for peer in range(out.shape[0]):
         out[peer, :points, :] = rows
         out[peer, points:, :] = extra
@@ -424,6 +493,7 @@
     pool_weight,
 ):
     total, width = points_in.shape
+    entries = neighbor_offsets.shape[1]
     nodes = lax.axis_size("pts")
     channels = lax.axis_size("ch")
     inside = [(i, i ^ 1) for i in range(nodes)]
@@ -449,7 +519,7 @@
     got_second = lax.ppermute(second, "pts", across)
     slots = nodes * HALF_SLOTS
     inner_rows = total - 2 * ROWS
-    inner_res, inner_normed, place, fetch, dead = call(
+    inner_res, inner_normed, place, fetch, dead, partial, top_scale, end_scale = call(
         front_inner,
         (
             shape((inner_rows, width)),
@@ -457,6 +527,9 @@
             shape((2 * slots, total)),
             shape((total, 2 * slots)),
             shape((slots, 128), F32),
+            shape((2 * ROWS, width), F32),
+            shape((entries // GROUP, GROUP * ROWS, width)),
+            shape((entries // GROUP, GROUP * ROWS, width)),
         ),
         flops=10**9,
         nbytes=4 * 10**6,
@@ -488,13 +561,16 @@
         inner_normed,
         place,
         dead,
+        partial,
+        top_scale,
+        end_scale,
     )
     arrived = lax.all_to_all(
         packed.reshape(nodes, HALF_SLOTS, 384), "pts", split_axis=0, concat_axis=0, tiled=True
     ).reshape(slots, 384)
     attended = call(
         attend,
-        shape((slots, 256)),
+        shape((slots // 2, 384)),
         scratch=(
             pltpu.VMEM((2 * slots, 128), BF),
             pltpu.VMEM((4 * slots, 128), BF),
@@ -506,8 +582,8 @@
         name="attend",
     )(arrived)
     returned = lax.all_to_all(
-        attended.reshape(nodes, HALF_SLOTS, 256), "pts", split_axis=0, concat_axis=0, tiled=True
-    ).reshape(slots, 256)
+        attended.reshape(nodes, 2, 384), "pts", split_axis=0, concat_axis=0, tiled=True
+    ).reshape(slots // 2, 384)
     rows = call(
         fetch_rows, shape((channels, total // 2 + EXTRA, 128)), flops=10**8, nbytes=10**6, name="fetch_rows"
     )(returned, fetch, extra_fetch)

time: 86 us -> 84 us (0.977)
  blocking collectives: 60.9 us -> 59.5 us
  waiting for transfers between devices: 1.07 us -> 0.01 us
    all_to_all x1, blocking collectives: 20.3 us -> 19.1 us  [shards(): lax.all_to_all(attended.reshape(nodes, 2, 384), 'pts', split_axis=0, conc...]
    ppermute x1, waiting for transfers between devices: 1.06 us -> 0.01 us  [shards(): got_second = lax.ppermute(second, 'pts', across)]
  transfers between devices with their start and end apart: 2 -> 2, of which waited for: 1 -> 0; matrix products, arithmetic and copies ran while one was open for 0% -> 0% of each run, Pallas kernels for 3% -> 5%
where the time goes in v5:
time: 84 us; the launch traced here: 83.8 us
  blocking collectives  59.5 us (71%)
  Pallas kernels  12.6 us (15%)
  starting transfers between devices  10.7 us (13%)
    all_to_all x1, blocking collectives, shards(): lax.all_to_all(packed.reshape(nodes, HALF_SLOTS, 384), 'pts', split_axis=...  30.4 us
    all_to_all x1, blocking collectives, shards(): lax.all_to_all(attended.reshape(nodes, 2, 384), 'pts', split_axis=0, conc...  19.1 us
    pallas_call x6, Pallas kernels, run(): pl.pallas_call(body, out_shape=outs, in_specs=[pl.BlockSpec(memory_space=...  12.6 us
    all_to_all x1, blocking collectives, shards(): lax.all_to_all(rows, 'ch', split_axis=0, concat_axis=0, tiled=True)  10.1 us
    ppermute x1, starting transfers between devices, shards(): got_first = lax.ppermute(first, 'pts', inside)  8.75 us
    ppermute x1, starting transfers between devices, shards(): got_second = lax.ppermute(second, 'pts', across)  1.92 us
  transfers between devices with their start and end apart: 2, of which 0 were waited for; matrix products, arithmetic and copies ran while one was open for 0% of the time, Pallas kernels for 5%

profile of v5, /device:TPU:1, one launch (start us, length us, event | category | flops | bytes accessed | tf_op | source)
XLA Modules:
  0.0 83.8 jit_solution(1855664208324336975)
XLA Ops:
  0.6 1.4 %stage.1 = (bf16[512,256]{1,0:T(8,128)(2,1)S(1)}, s32[16,512]{1,0:T(8,128)S(1)}, s32[16,512]{1,0:T(8,128)S(1)}, s32[1,512]{1,0:T(1,128)S(1)}, bf16[27,256]{1,0:T...) custom-call(bf16[512,256]{1,0:T(8,128)(2,1)} %refs_0_.1, ...), custom_call_target="tpu_custom_call" | custom-call | tf_op jit(solution)/shard_map/stage/pallas_call | solution.py:104
  2.0 8.7 %collective-permute-start = (bf16[144,256]{1,0:T(8,128)(2,1)S(1)}, bf16[144,256]{1,0:T(8,128)(2,1)S(1)}, u32[]{:S(2)}, u32[]{:S(2)}) collective-permute-start(bf16[144,256]{1,0:T(8,128)(2,1)S(1)} %get-tuple-element.30), channel_id=1, source_target_pairs={{0,4},{4,0},{8,12},{12,8},{16,20},{20,16},{24,28},{28,24},{32,36},... | collective-permute-start | bytes 221192 | tf_op jit(solution)/shard_map/ppermute | solution.py:518
  10.8 1.9 %collective-permute-start.1 = (bf16[144,256]{1,0:T(8,128)(2,1)S(1)}, bf16[144,256]{1,0:T(8,128)(2,1)S(1)}, u32[]{:S(2)}, u32[]{:S(2)}) collective-permute-start(bf16[144,256]{1,0:T(8,128)(2,1)S(1)} %get-tuple-element.31), channel_id=1, source_target_pairs={{4,8},{8,4},{12,16},{16,12},{20,24},{24,20},{28,32},{32,28},{36,40... | collective-permute-start | bytes 221192 | tf_op jit(solution)/shard_map/ppermute | solution.py:519
  12.7 3.8 %front_inner.1 = (bf16[256,256]{1,0:T(8,128)(2,1)S(1)}, bf16[256,256]{1,0:T(8,128)(2,1)S(1)}, bf16[1024,512]{1,0:T(8,128)(2,1)S(1)}, bf16[512,1024]{1,0:T(8,128)...) custom-call(bf16[512,256]{1,0:T(8,128)(2,1)S(1)} %get-tuple-element., ...), custom_call_target="tpu_custom_call" | custom-call | flops 1000000000 | bytes 4000000 | tf_op jit(solution)/shard_map/front_inner/pallas_call | solution.py:29
  16.5 0.0 collective-permute-done.got_first
  16.5 0.0 collective-permute-done.1.got_second
  16.5 2.4 %front_edges.1 = (bf16[256,256]{1,0:T(8,128)(2,1)S(1)}, bf16[512,384]{1,0:T(8,128)(2,1)S(1)}, bf16[16,256]{1,0:T(8,128)(2,1)S(1)}, bf16[16,512]{1,0:T(8,128)(2,1)S(1)}, f32[16,128]{1,0:T(8,128)S(1)}) custom-call(bf16[144,256]{1,0:T(8,128)(2,1)S(1)} %collective-permute-done.got_first, bf16[144,256]{1,0:T(8,128)(2,1)S(1)} %collective-permute-done.1.got_second, ...), custom_call_target="tpu_custom_call" | custom-call | flops 1000000000 | bytes 4000000 | tf_op jit(solution)/shard_map/front_edges/pallas_call | solution.py:29
  19.0 0.1 reshape.32
  19.1 30.4 %all_to_all.15 = bf16[128,4,384]{2,1,0:T(4,128)(2,1)S(1)} all-to-all(bf16[128,4,384]{2,1,0:T(4,128)(2,1)S(1)} %reshape.32), channel_id=1, replica_groups=mesh['pts'=128,'ch'=4] {'pts'}, dimensions={0} | all-to-all | bytes 786432 | tf_op jit(solution)/shard_map/all_to_all | solution.py:568
  49.4 0.1 reshape.33.packed
  49.5 3.1 %attend.1 = bf16[256,384]{1,0:T(8,128)(2,1)S(1)} custom-call(bf16[512,384]{1,0:T(8,128)(2,1)S(1)} %reshape.33.packed), custom_call_target="tpu_custom_call" | custom-call | flops 1000000000 | bytes 1000000 | tf_op jit(solution)/shard_map/attend/pallas_call | solution.py:29
  52.6 0.1 reshape.34
  52.7 19.1 %all_to_all.16 = bf16[128,2,384]{2,1,0:T(2,128)(2,1)S(1)} all-to-all(bf16[128,2,384]{2,1,0:T(2,128)(2,1)S(1)} %reshape.34), channel_id=1, replica_groups=mesh['pts'=128,'ch'=4] {'pts'}, dimensions={0} | all-to-all | bytes 393216 | tf_op jit(solution)/shard_map/all_to_all | solution.py:584
  71.8 0.1 reshape.35.returned
  71.9 0.5 fetch_rows.1
  72.4 10.1 %all_to_all.17.gathered = bf16[4,272,128]{2,1,0:T(8,128)(2,1)S(1)} all-to-all(bf16[4,272,128]{2,1,0:T(8,128)(2,1)S(1)} %fetch_rows.1), channel_id=1, replica_groups=mesh['pts'=128,'ch'=4] {'ch'}, dimensions={0} | all-to-all | bytes 557056 | tf_op jit(solution)/shard_map/all_to_all | solution.py:590
  82.5 1.3 %finish.1 = (bf16[64,512]{1,0:T(8,128)(2,1)}, bf16[128,128]{1,0:T(8,128)(2,1)}) custom-call(bf16[4,272,128]{2,1,0:T(8,128)(2,1)S(1)} %all_to_all.17.gathered, bf16[256,256]{1,0:T(8,128)(2,1)S(1)} %get-tuple-element.49.edge_res, bf16[256,256]{1,0:T(8,128)(2,1)S(1)} %get-tuple-element.50.inner_res, bf16[16,256]{1,0:T(8,128)(2,1)S(1)} %get-tuple-element.51.extra_res, ...), custom_call_target="tpu_custom_call" | custom-call | flops 100000000 | bytes 1000000 | tf_op jit(solution)/shard_map/finish/pallas_call | solution.py:29
Async XLA Ops:
  2.0 14.5 %collective-permute-start = (bf16[144,256]{1,0:T(8,128)(2,1)S(1)}, bf16[144,256]{1,0:T(8,128)(2,1)S(1)}, u32[]{:S(2)}, u32[]{:S(2)}) collective-permute-start(bf16[144,256]{1,0:T(8,128)(2,1)S(1)} %get-tuple-element.30), channel_id=1, source_target_pairs={{0,4},{4,0},{8,12},{12,8},{16,20},{20,16},{24,28},{28,24},{32,36},... | collective-permute-start | bytes 221192 | tf_op jit(solution)/shard_map/ppermute | solution.py:518
  10.8 5.8 %collective-permute-start.1 = (bf16[144,256]{1,0:T(8,128)(2,1)S(1)}, bf16[144,256]{1,0:T(8,128)(2,1)S(1)}, u32[]{:S(2)}, u32[]{:S(2)}) collective-permute-start(bf16[144,256]{1,0:T(8,128)(2,1)S(1)} %get-tuple-element.31), channel_id=1, source_target_pairs={{4,8},{8,4},{12,16},{16,12},{20,24},{24,20},{28,32},{32,28},{36,40... | collective-permute-start | bytes 221192 | tf_op jit(solution)/shard_map/ppermute | solution.py:519

commit v6 on v5

--- a/solution.py
+++ b/solution.py
@@ -13,8 +13,6 @@
 ROWS = 128
 HALF_SLOTS = 4
 DEAD = -1e30
-SHIFT_BITS = 10
-SHIFT = 1 << SHIFT_BITS
 LEAD = 8
 HALO = G + 2 * LEAD
 EXTRA = 16
@@ -114,27 +112,30 @@
     return run
 
 
-def codes(offsets, kinds=None):
-    rows = offsets.shape[1]
-    target = jnp.transpose(offsets) + iota((rows, offsets.shape[0]), 0) + G
-    return target if kinds is None else target + jnp.transpose(kinds) * SHIFT
-
-
-def windowed_sum(code, shift, window, scale_of, between=()):
+def codes(offsets):
+    return jnp.transpose(offsets.astype(F32)) + iota((offsets.shape[1], offsets.shape[0]), 0).astype(F32)
+
+
+def columns(kinds):
+    return jnp.transpose(kinds.astype(F32))
+
+
+def marks_of(values, n, first, span):
+    value = jnp.broadcast_to(values[:, n : n + 1], (values.shape[0], 128)).astype(BF)
+    lane = iota(value.shape, 1).astype(F32)
+    one, none = jnp.ones(value.shape, BF), jnp.zeros(value.shape, BF)
+    tiles = [jnp.where(value == (lane + (first + lanes)).astype(BF), one, none) for lanes in range(0, span, 128)]
+    return tiles[0] if len(tiles) == 1 else jnp.concatenate(tiles, axis=1)
+
+
+def windowed_sum(code, first_row, window, scale_of, between=()):
     rows, span = code.shape[0], window.shape[0]
     between = list(between)
     conv = jnp.zeros((rows, window.shape[1]), F32)
     for first in range(0, code.shape[1], GROUP):
-        picks, kinds = [], []
-        for n in range(first, first + GROUP):
-            place = jnp.broadcast_to(code[:, n : n + 1], (rows, 128))
-            if scale_of.marked:
-                kinds.append(lax.shift_right_logical(place, SHIFT_BITS))
-                place = place & (SHIFT - 1)
-            lane = iota((rows, 128), 1) + shift
-            picks.append(jnp.concatenate([hot(place == lane + lanes) for lanes in range(0, span, 128)], axis=1))
+        picks = [marks_of(code, n, first_row - G, span) for n in range(first, first + GROUP)]
         picked = dot(jnp.concatenate(picks, axis=0), window)
-        part = picked * scale_of(first // GROUP, kinds)
+        part = picked * scale_of(first // GROUP)
         for n in range(GROUP):
             conv = conv + part[n * rows : (n + 1) * rows]
         if between:
@@ -144,24 +145,19 @@
     return conv
 
 
-def scale_by(weights, keep=None):
-    def scale_of(group, kinds):
-        marks = [hot(kind == iota(kind.shape, 1)) for kind in kinds]
+def scale_by(weights, kinds, keep=None):
+    def scale_of(group):
+        marks = [marks_of(kinds, n, 0, 128) for n in range(group * GROUP, (group + 1) * GROUP)]
         scale = dot(jnp.concatenate(marks, axis=0), weights)
         if keep is not None:
             keep[group] = scale.astype(BF)
         return scale
 
-    scale_of.marked = True
     return scale_of
 
 
 def kept_scale(kept):
-    def scale_of(group, kinds):
-        return kept[group].astype(F32)
-
-    scale_of.marked = False
-    return scale_of
+    return lambda group: kept[group].astype(F32)
 
 
 def normalize(points, conv, gain, bias):
@@ -180,6 +176,16 @@
     return jnp.concatenate([conv_weight.astype(F32), fill], axis=0).astype(BF)
 
 
+def projection(qkv_weight):
+    q, k, v = (qkv_weight[t] for t in range(3))
+    return jnp.concatenate([q, k, v, jnp.zeros(q.shape, BF)], axis=0)
+
+
+def projected(rows, qkv_weight):
+    value = dot_t(rows, projection(qkv_weight))
+    return jnp.where(iota(value.shape, 1) == value.shape[1] - 64, 1.0, value).astype(BF)
+
+
 def front_inner(
     points,
     offsets,
@@ -188,14 +194,16 @@
     conv_weight,
     gain,
     bias,
+    qkv_weight,
     residual,
-    normed,
+    base,
     place,
     fetch,
-    dead,
     partial,
     top_scale,
     end_scale,
+    normed,
+    place_inner,
 ):
     total = points.shape[0]
     weights = padded_weights(conv_weight[...])
@@ -211,23 +219,28 @@
     quarter = (slot >> 2) * 2 + (slot & 1)
     back = quarter * (2 * peers) + own * 2 + ((slot & (HALF_SLOTS - 1)) >> 1)
     column = jnp.transpose(jnp.broadcast_to(back, (8, total)))[:, 0:1]
+    one, none = jnp.ones((ROWS, 128), BF), jnp.zeros((ROWS, 128), BF)
+    tile_row = jnp.broadcast_to((spot >> 7).astype(F32), (ROWS, total)).astype(BF)
+    mark_row = hot(iota((ROWS, total), 0) == (spot & 127))
+    blank_row = jnp.zeros((ROWS, total), BF)
 
     def build_place(start):
-        lane = iota((ROWS, 128), 1)
-        rows = slice(start, start + ROWS)
-        live = []
-        for half in range(2):
-            here = slice(half * slots + start, half * slots + start + ROWS)
-            mask = jnp.where(iota((ROWS, total), 0) + (half * slots + start) == spot, 1.0, 0.0)
-            place[here, :] = mask.astype(BF)
-            live.append(jnp.sum(mask, axis=1, keepdims=True))
-        dead[rows, :] = jnp.where(jnp.where(lane < 64, live[0], live[1]) > 0.5, 0.0, DEAD)
+        for tile in (start // ROWS, (start + slots) // ROWS):
+            here = slice(tile * ROWS, (tile + 1) * ROWS)
+            mask = jnp.where(tile_row == jnp.full((ROWS, total), tile, BF), mark_row, blank_row)
+            place[here, :ROWS] = mask[:, :ROWS]
+            place_inner[here, :] = mask[:, ROWS : total - ROWS]
+            place[here, ROWS:] = mask[:, total - ROWS :]
 
     def build_fetch(start):
         rows = slice(start, start + ROWS)
-        here = jnp.broadcast_to(column[rows, :], (ROWS, 128))
-        for lanes in range(0, 2 * slots, 128):
-            fetch[rows, lanes : lanes + 128] = hot(here == iota((ROWS, 128), 1) + lanes)
+        value = jnp.broadcast_to(column[rows, :], (ROWS, 128))
+        mark = jnp.where((value & 127).astype(F32).astype(BF) == iota((ROWS, 128), 1).astype(F32).astype(BF), one, none)
+        tile_of = (value >> 7).astype(F32).astype(BF)
+        for tile in range(2 * slots // 128):
+            fetch[rows, tile * 128 : (tile + 1) * 128] = jnp.where(
+                tile_of == jnp.full((ROWS, 128), tile, BF), mark, none
+            )
 
     pieces = [functools.partial(build_place, n) for n in range(0, slots, ROWS)]
     pieces += [functools.partial(build_fetch, n) for n in range(0, total, ROWS)]
@@ -237,10 +250,10 @@
         rows = slice(block * ROWS, (block + 1) * ROWS)
         window = points[block * ROWS - G : (block + 1) * ROWS + G, :]
         conv = windowed_sum(
-            codes(offsets[:, rows], kinds[:, rows]),
+            codes(offsets[:, rows]),
             0,
             window,
-            scale_by(weights),
+            scale_by(weights, columns(kinds[:, rows])),
             pieces[(block - 1) * share : block * share],
         )
         res, nor = normalize(points[rows, :], conv, gain[...], bias[...])
@@ -249,19 +262,20 @@
         normed[out, :] = nor
     last = total - ROWS
     partial[0:ROWS, :] = windowed_sum(
-        codes(offsets[:, :ROWS], kinds[:, :ROWS]),
+        codes(offsets[:, :ROWS]),
         G,
         points[0 : ROWS + G, :],
-        scale_by(weights, top_scale),
+        scale_by(weights, columns(kinds[:, :ROWS]), top_scale),
         pieces[2 * share : 3 * share],
     )
     partial[ROWS:, :] = windowed_sum(
-        codes(offsets[:, last:], kinds[:, last:]),
+        codes(offsets[:, last:]),
         0,
         points[last - G :, :],
-        scale_by(weights, end_scale),
+        scale_by(weights, columns(kinds[:, last:]), end_scale),
         pieces[3 * share :],
     )
+    base[...] = dot(place_inner[...], projected(normed[...], qkv_weight)).astype(BF)
 
 
 def front_edges(
@@ -274,9 +288,8 @@
     gain,
     bias,
     qkv_weight,
-    inner,
+    base,
     place,
-    dead,
     partial,
     top_scale,
     end_scale,
@@ -285,7 +298,6 @@
     extra_res,
     extra_fetch,
     extra_lead,
-    normed,
 ):
     total, width = points.shape
     weights = padded_weights(conv_weight[...])
@@ -298,53 +310,48 @@
     conv = partial[0:ROWS, :] + windowed_sum(
         codes(offsets[:, :ROWS]), 0, above, kept_scale(top_scale)
     )
-    res, nor = normalize(points[0:ROWS, :], conv, gain[...], bias[...])
+    res, top = normalize(points[0:ROWS, :], conv, gain[...], bias[...])
     residual[0:ROWS, :] = res
-    normed[0:ROWS, :] = nor
-    normed[ROWS:last, :] = inner[...]
     conv = partial[ROWS:, :] + windowed_sum(
         codes(offsets[:, last:]),
         ROWS + G,
         below[:G].astype(BF),
         kept_scale(end_scale),
     )
-    res, nor = normalize(points[last:, :], conv, gain[...], bias[...])
+    res, end = normalize(points[last:, :], conv, gain[...], bias[...])
     residual[ROWS:, :] = res
-    normed[last:, :] = nor
+    slots = out.shape[0]
+    placed = dot(place[...], projected(jnp.concatenate([top, end], axis=0), qkv_weight)) + base[...].astype(F32)
+    near_half, far_half = placed[:slots], placed[slots:]
+    lane = iota((slots, 128), 1)
+    near_moved, far_moved = swap_halves(near_half[:, :128]), swap_halves(far_half[:, :128])
+    query = jnp.where(lane < 64, near_half[:, :128], far_moved)
+    live = jnp.where(lane < 64, near_half[:, 192:193], far_half[:, 192:193])
+    out[:, 0:128] = jnp.where(live > 0.5, query, DEAD).astype(BF)
+    out[:, 128:256] = jnp.where(lane < 64, near_moved, far_half[:, :128]).astype(BF)
+    out[:, 256:] = jnp.where(lane < 64, near_half[:, 128:], swap_halves(far_half[:, 128:])).astype(BF)
     near = offsets.shape[0]
-    facts_int = facts.astype(jnp.int32)
-    extra_code = facts_int[:, :near] + iota((LEAD, near), 0) + G + facts_int[:, near : 2 * near] * SHIFT
-    blank = jnp.zeros((EXTRA - LEAD, near), jnp.int32)
+    padded = jnp.concatenate([facts, jnp.zeros((EXTRA - LEAD, 128), F32)], axis=0)
+    code = padded[:, :near] + jnp.where(iota((EXTRA, near), 0) < LEAD, iota((EXTRA, near), 0), 0).astype(F32)
     reach = below[: G + LEAD]
     fill = jnp.zeros((256 - G - LEAD, width), F32)
     window = jnp.concatenate([points[last:, :], jnp.concatenate([reach, fill], axis=0).astype(BF)], axis=0)
     more = jnp.concatenate([reach[:LEAD], jnp.zeros((EXTRA - LEAD, width), F32)], axis=0)
-    conv = windowed_sum(jnp.concatenate([extra_code, blank], axis=0), 0, window, scale_by(weights))
+    conv = windowed_sum(code, 0, window, scale_by(weights, padded[:, near : 2 * near]))
     extra_res[...] = (more + conv).astype(BF)
-    slots = out.shape[0]
     full = jnp.concatenate([facts, jnp.zeros((EXTRA - LEAD, 128), F32)], axis=0)
     owner, slot, lead = (full[:, 2 * near + 8 * n : 2 * near + 8 * n + 1] for n in range(3))
     index = slot.astype(jnp.int32)
     spot = (index & 1) * (slots // 2) + owner.astype(jnp.int32) * 2 + (index >> 1)
     extra_fetch[...] = hot(spot == iota((EXTRA, slots), 1))
     extra_lead[...] = jnp.broadcast_to(lead, (EXTRA, 128))
-    q, k, v = (qkv_weight[t] for t in range(3))
-    none = jnp.zeros(q.shape, BF)
-    left = jnp.concatenate([q, none, k, none, v, none], axis=0)
-    right = jnp.concatenate([none, q, none, k, none, v], axis=0)
-    placed = dot(place[...], normed[...]).astype(BF)
-    packed = dot_t(
-        jnp.concatenate([placed[:slots], placed[slots:]], axis=1), jnp.concatenate([left, right], axis=1)
-    )
-    out[:, 0:128] = (packed[:, 0:128] + dead[...]).astype(BF)
-    out[:, 128:] = packed[:, 128:].astype(BF)
 
 
 def swap_halves(value):
     return jnp.concatenate([value[:, 64:], value[:, :64]], axis=1)
 
 
-def attend(packed, out, keys, queries, values, kept):
+def attend(packed, out, keys, values, kept):
     half = packed.shape[0]
     lane = iota((half, 128), 1)
     q = packed[:, 0:128]
@@ -357,23 +364,27 @@
         return jnp.where(x.astype(F32) < 0.1 * DEAD, DEAD, 0.0)
 
     step = 128
-    for part, (qq, kk, vv, flag) in enumerate(((q, k, v, qs), (qs, ks, vs, q))):
+    extra = jnp.where(lane == 64, 1.0, zero)
+    for part, (kk, flag) in enumerate(((k, qs), (ks, q))):
         rows = slice(part * half, (part + 1) * half)
-        qf, kf, vf = (x.astype(F32) for x in (qq, kk, vv))
-        keys[rows, :] = jnp.where(lane < 64, kf, jnp.where(lane == 64, dead_bias(flag), 0.0)).astype(BF)
-        extra = jnp.where(lane == 64, 1.0, zero)
-        values[rows, :] = jnp.where(lane < 64, vf, extra).astype(BF)
-        for head in range(2):
-            mine = (lane >= head * HD) & (lane < (head + 1) * HD)
-            query = jnp.where(mine, qf, extra).astype(BF)
-            for index in range(half // step):
-                start = (index * 4 + part * 2 + head) * step
-                queries[start : start + step, :] = query[index * step : (index + 1) * step, :]
+        keys[rows, :] = jnp.where(lane < 64, kk.astype(F32), jnp.where(lane == 64, dead_bias(flag), 0.0)).astype(BF)
+
+    def fill_values():
+        for part, vv in enumerate((v, vs)):
+            rows = slice(part * half, (part + 1) * half)
+            values[rows, :] = jnp.where(lane < 64, vv.astype(F32), extra).astype(BF)
+
     factor = math.log2(math.e) / math.sqrt(HD)
     block_lane = iota((step, 128), 1)
 
     def scores_of(chunk):
-        return dot_t(queries[chunk * 2 * step : (chunk + 1) * 2 * step, :], keys[...])
+        rows = slice((chunk // 2) * step, (chunk // 2 + 1) * step)
+        mine = (q, qs)[chunk % 2][rows].astype(F32)
+        pair = []
+        for head in range(2):
+            inside = (block_lane >= head * HD) & (block_lane < (head + 1) * HD)
+            pair.append(jnp.where(inside, mine, extra[:step]).astype(BF))
+        return dot_t(jnp.concatenate(pair, axis=0), keys[...])
 
     def attended_of(scores):
         top = jnp.max(scores, axis=1, keepdims=True)
@@ -384,6 +395,7 @@
 
     chunks = 2 * half // step
     ahead = [scores_of(0)]
+    fill_values()
     done = []
     for chunk in range(chunks):
         if chunk + 1 < chunks:
@@ -519,22 +531,22 @@
     got_second = lax.ppermute(second, "pts", across)
     slots = nodes * HALF_SLOTS
     inner_rows = total - 2 * ROWS
-    inner_res, inner_normed, place, fetch, dead, partial, top_scale, end_scale = call(
+    inner_res, base, place, fetch, partial, top_scale, end_scale = call(
         front_inner,
         (
             shape((inner_rows, width)),
-            shape((inner_rows, width)),
-            shape((2 * slots, total)),
+            shape((2 * slots, width)),
+            shape((2 * slots, 2 * ROWS)),
             shape((total, 2 * slots)),
-            shape((slots, 128), F32),
             shape((2 * ROWS, width), F32),
             shape((entries // GROUP, GROUP * ROWS, width)),
             shape((entries // GROUP, GROUP * ROWS, width)),
         ),
+        scratch=(pltpu.VMEM((inner_rows, width), BF), pltpu.VMEM((2 * slots, inner_rows), BF)),
         flops=10**9,
         nbytes=4 * 10**6,
         name="front_inner",
-    )(points, offsets, kinds, own, conv_weight, gain, bias)
+    )(points, offsets, kinds, own, conv_weight, gain, bias, qkv_weight)
     edge_res, packed, extra_res, extra_fetch, extra_lead = call(
         front_edges,
         (
@@ -544,7 +556,6 @@
             shape((EXTRA, slots)),
             shape((EXTRA, 128), F32),
         ),
-        scratch=(pltpu.VMEM((total, width), BF),),
         flops=10**9,
         nbytes=4 * 10**6,
         name="front_edges",
@@ -558,9 +569,8 @@
         gain,
         bias,
         qkv_weight,
-        inner_normed,
+        base,
         place,
-        dead,
         partial,
         top_scale,
         end_scale,
@@ -573,7 +583,6 @@
         shape((slots // 2, 384)),
         scratch=(
             pltpu.VMEM((2 * slots, 128), BF),
-            pltpu.VMEM((4 * slots, 128), BF),
             pltpu.VMEM((2 * slots, 128), BF),
             pltpu.VMEM((slots + 8, 128), F32),
         ),

time: 84 us -> 83.5 us (level)
  no operation moved by 1% of the time
where the time goes in v6:
time: 83.5 us; the launch traced here: 83.2 us
  blocking collectives  59.3 us (71%)
  Pallas kernels  12.2 us (15%)
  starting transfers between devices  10.7 us (13%)
    all_to_all x1, blocking collectives, shards(): lax.all_to_all(packed.reshape(nodes, HALF_SLOTS, 384), 'pts', split_axis=...  30.1 us
    all_to_all x1, blocking collectives, shards(): lax.all_to_all(attended.reshape(nodes, 2, 384), 'pts', split_axis=0, conc...  19.1 us
    pallas_call x6, Pallas kernels, run(): pl.pallas_call(body, out_shape=outs, in_specs=[pl.BlockSpec(memory_space=...  12.2 us
    all_to_all x1, blocking collectives, shards(): lax.all_to_all(rows, 'ch', split_axis=0, concat_axis=0, tiled=True)  10.1 us
    ppermute x1, starting transfers between devices, shards(): got_first = lax.ppermute(first, 'pts', inside)  8.75 us
    ppermute x1, starting transfers between devices, shards(): got_second = lax.ppermute(second, 'pts', across)  1.92 us
  transfers between devices with their start and end apart: 2, of which 0 were waited for; matrix products, arithmetic and copies ran while one was open for 0% of the time, Pallas kernels for 5%

profile of v6, /device:TPU:1, one launch (start us, length us, event | category | flops | bytes accessed | tf_op | source)
XLA Modules:
  0.0 83.2 jit_solution(17520057553411304378)
XLA Ops:
  0.6 1.4 %stage.1 = (bf16[512,256]{1,0:T(8,128)(2,1)S(1)}, s32[16,512]{1,0:T(8,128)S(1)}, s32[16,512]{1,0:T(8,128)S(1)}, s32[1,512]{1,0:T(1,128)S(1)}, bf16[27,256]{1,0:T...) custom-call(bf16[512,256]{1,0:T(8,128)(2,1)} %refs_0_.1, ...), custom_call_target="tpu_custom_call" | custom-call | tf_op jit(solution)/shard_map/stage/pallas_call | solution.py:102
  2.0 8.7 %collective-permute-start = (bf16[144,256]{1,0:T(8,128)(2,1)S(1)}, bf16[144,256]{1,0:T(8,128)(2,1)S(1)}, u32[]{:S(2)}, u32[]{:S(2)}) collective-permute-start(bf16[144,256]{1,0:T(8,128)(2,1)S(1)} %get-tuple-element.29), channel_id=1, source_target_pairs={{0,4},{4,0},{8,12},{12,8},{16,20},{20,16},{24,28},{28,24},{32,36},... | collective-permute-start | bytes 221192 | tf_op jit(solution)/shard_map/ppermute | solution.py:530
  10.8 1.9 %collective-permute-start.1 = (bf16[144,256]{1,0:T(8,128)(2,1)S(1)}, bf16[144,256]{1,0:T(8,128)(2,1)S(1)}, u32[]{:S(2)}, u32[]{:S(2)}) collective-permute-start(bf16[144,256]{1,0:T(8,128)(2,1)S(1)} %get-tuple-element.30), channel_id=1, source_target_pairs={{4,8},{8,4},{12,16},{16,12},{20,24},{24,20},{28,32},{32,28},{36,40... | collective-permute-start | bytes 221192 | tf_op jit(solution)/shard_map/ppermute | solution.py:531
  12.7 4.0 %front_inner.1 = (bf16[256,256]{1,0:T(8,128)(2,1)S(1)}, bf16[1024,256]{1,0:T(8,128)(2,1)S(1)}, bf16[1024,256]{1,0:T(8,128)(2,1)S(1)}, bf16[512,1024]{1,0:T(8,128...) custom-call(bf16[512,256]{1,0:T(8,128)(2,1)S(1)} %get-tuple-element.31.points, ...), custom_call_target="tpu_custom_call" | custom-call | flops 1000000000 | bytes 4000000 | tf_op jit(solution)/shard_map/front_inner/pallas_call | solution.py:27
  16.7 0.0 collective-permute-done.got_first
  16.7 0.0 collective-permute-done.1.got_second
  16.8 1.9 %front_edges.1 = (bf16[256,256]{1,0:T(8,128)(2,1)S(1)}, bf16[512,384]{1,0:T(8,128)(2,1)S(1)}, bf16[16,256]{1,0:T(8,128)(2,1)S(1)}, bf16[16,512]{1,0:T(8,128)(2,1)S(1)}, f32[16,128]{1,0:T(8,128)S(1)}) custom-call(bf16[144,256]{1,0:T(8,128)(2,1)S(1)} %collective-permute-done.got_first, bf16[144,256]{1,0:T(8,128)(2,1)S(1)} %collective-permute-done.1.got_second, ...), custom_call_target="tpu_custom_call" | custom-call | flops 1000000000 | bytes 4000000 | tf_op jit(solution)/shard_map/front_edges/pallas_call | solution.py:27
  18.6 0.1 reshape.32
  18.7 30.1 %all_to_all.15 = bf16[128,4,384]{2,1,0:T(4,128)(2,1)S(1)} all-to-all(bf16[128,4,384]{2,1,0:T(4,128)(2,1)S(1)} %reshape.32), channel_id=1, replica_groups=mesh['pts'=128,'ch'=4] {'pts'}, dimensions={0} | all-to-all | bytes 786432 | tf_op jit(solution)/shard_map/all_to_all | solution.py:578
  48.9 0.1 reshape.33.packed
  49.0 3.1 %attend.1 = bf16[256,384]{1,0:T(8,128)(2,1)S(1)} custom-call(bf16[512,384]{1,0:T(8,128)(2,1)S(1)} %reshape.33.packed), custom_call_target="tpu_custom_call" | custom-call | flops 1000000000 | bytes 1000000 | tf_op jit(solution)/shard_map/attend/pallas_call | solution.py:27
  52.1 0.1 reshape.34
  52.1 19.1 %all_to_all.16 = bf16[128,2,384]{2,1,0:T(2,128)(2,1)S(1)} all-to-all(bf16[128,2,384]{2,1,0:T(2,128)(2,1)S(1)} %reshape.34), channel_id=1, replica_groups=mesh['pts'=128,'ch'=4] {'pts'}, dimensions={0} | all-to-all | bytes 393216 | tf_op jit(solution)/shard_map/all_to_all | solution.py:593
  71.2 0.1 reshape.35.returned
  71.3 0.5 fetch_rows.1
  71.8 10.1 %all_to_all.17.gathered = bf16[4,272,128]{2,1,0:T(8,128)(2,1)S(1)} all-to-all(bf16[4,272,128]{2,1,0:T(8,128)(2,1)S(1)} %fetch_rows.1), channel_id=1, replica_groups=mesh['pts'=128,'ch'=4] {'ch'}, dimensions={0} | all-to-all | bytes 557056 | tf_op jit(solution)/shard_map/all_to_all | solution.py:599
  81.9 1.3 %finish.1 = (bf16[64,512]{1,0:T(8,128)(2,1)}, bf16[128,128]{1,0:T(8,128)(2,1)}) custom-call(bf16[4,272,128]{2,1,0:T(8,128)(2,1)S(1)} %all_to_all.17.gathered, bf16[256,256]{1,0:T(8,128)(2,1)S(1)} %get-tuple-element.47.edge_res, bf16[256,256]{1,0:T(8,128)(2,1)S(1)} %get-tuple-element.48.inner_res, bf16[16,256]{1,0:T(8,128)(2,1)S(1)} %get-tuple-element.49.extra_res, ...), custom_call_target="tpu_custom_call" | custom-call | flops 100000000 | bytes 1000000 | tf_op jit(solution)/shard_map/finish/pallas_call | solution.py:27
Async XLA Ops:
  2.0 14.7 %collective-permute-start = (bf16[144,256]{1,0:T(8,128)(2,1)S(1)}, bf16[144,256]{1,0:T(8,128)(2,1)S(1)}, u32[]{:S(2)}, u32[]{:S(2)}) collective-permute-start(bf16[144,256]{1,0:T(8,128)(2,1)S(1)} %get-tuple-element.29), channel_id=1, source_target_pairs={{0,4},{4,0},{8,12},{12,8},{16,20},{20,16},{24,28},{28,24},{32,36},... | collective-permute-start | bytes 221192 | tf_op jit(solution)/shard_map/ppermute | solution.py:530
  10.8 6.0 %collective-permute-start.1 = (bf16[144,256]{1,0:T(8,128)(2,1)S(1)}, bf16[144,256]{1,0:T(8,128)(2,1)S(1)}, u32[]{:S(2)}, u32[]{:S(2)}) collective-permute-start(bf16[144,256]{1,0:T(8,128)(2,1)S(1)} %get-tuple-element.30), channel_id=1, source_target_pairs={{4,8},{8,4},{12,16},{16,12},{20,24},{24,20},{28,32},{32,28},{36,40... | collective-permute-start | bytes 221192 | tf_op jit(solution)/shard_map/ppermute | solution.py:531

commit v7 on v6

--- a/solution.py
+++ b/solution.py
@@ -22,13 +22,13 @@
 VMEM_BYTES = 24 * 1024 * 1024
 
 
-def call(body, outs, scratch=(), flops=0, nbytes=0, name=None):
+def call(body, outs, scratch=(), flops=0, nbytes=0, name=None, out_space=pltpu.VMEM):
     def run(*args):
         return pl.pallas_call(
             body,
             out_shape=outs,
             in_specs=[pl.BlockSpec(memory_space=pltpu.VMEM)] * len(args),
-            out_specs=jax.tree.map(lambda _: pl.BlockSpec(memory_space=pltpu.VMEM), outs),
+            out_specs=jax.tree.map(lambda _: pl.BlockSpec(memory_space=out_space), outs),
             scratch_shapes=list(scratch),
             compiler_params=pltpu.CompilerParams(vmem_limit_bytes=VMEM_BYTES),
             cost_estimate=pl.CostEstimate(flops=flops, bytes_accessed=nbytes, transcendentals=0),
@@ -82,19 +82,22 @@
         ]
         for copy in copies:
             copy.start()
-        for copy in copies:
-            copy.wait()
         points, offsets, kinds, owners = targets[:4]
         clusters = targets[-1]
         total, width = points.shape
         index = lax.axis_index("pts")
         even = lax.rem(index, 2) == 0
+        for copy in (*copies[1:4], copies[-1]):
+            copy.wait()
         facts = lead_facts(offsets[...], kinds[...], owners[...], clusters[...], index * (total // 4))
         facts = jnp.concatenate([facts, jnp.zeros((LEAD, width - 128), F32)], axis=1)
+        copies[0].wait()
         head = jnp.concatenate([points[0:G, :].astype(F32), points[G : G + LEAD, :].astype(F32), facts], axis=0)
         tail = jnp.concatenate([points[total - G :, :].astype(F32), jnp.zeros((2 * LEAD, width), F32)], axis=0)
         first[...] = jnp.where(even, tail, head).astype(BF)
         second[...] = jnp.where(even, head, tail).astype(BF)
+        for copy in copies[4:-1]:
+            copy.wait()
 
     def run(*args):
         outs = [jax.ShapeDtypeStruct(a.shape, a.dtype) for a in args]
@@ -120,24 +123,35 @@
     return jnp.transpose(kinds.astype(F32))
 
 
-def marks_of(values, n, first, span):
-    value = jnp.broadcast_to(values[:, n : n + 1], (values.shape[0], 128)).astype(BF)
+def spread(values, keep=None):
+    def value_of(n):
+        value = jnp.broadcast_to(values[:, n : n + 1], (values.shape[0], 128)).astype(BF)
+        if keep is not None:
+            keep[n] = value
+        return value
+
+    return value_of
+
+
+def marks_of(value, first, span):
     lane = iota(value.shape, 1).astype(F32)
     one, none = jnp.ones(value.shape, BF), jnp.zeros(value.shape, BF)
     tiles = [jnp.where(value == (lane + (first + lanes)).astype(BF), one, none) for lanes in range(0, span, 128)]
     return tiles[0] if len(tiles) == 1 else jnp.concatenate(tiles, axis=1)
 
 
-def windowed_sum(code, first_row, window, scale_of, between=()):
-    rows, span = code.shape[0], window.shape[0]
+def windowed_sum(value_of, entries, first_row, window, scale_of, between=()):
+    span = window.shape[0]
     between = list(between)
-    conv = jnp.zeros((rows, window.shape[1]), F32)
-    for first in range(0, code.shape[1], GROUP):
-        picks = [marks_of(code, n, first_row - G, span) for n in range(first, first + GROUP)]
+    conv = None
+    for first in range(0, entries, GROUP):
+        picks = [marks_of(value_of(n), first_row - G, span) for n in range(first, first + GROUP)]
+        rows = picks[0].shape[0]
         picked = dot(jnp.concatenate(picks, axis=0), window)
         part = picked * scale_of(first // GROUP)
         for n in range(GROUP):
-            conv = conv + part[n * rows : (n + 1) * rows]
+            piece = part[n * rows : (n + 1) * rows]
+            conv = piece if conv is None else conv + piece
         if between:
             between.pop(0)()
     for step in between:
@@ -147,17 +161,17 @@
 
 def scale_by(weights, kinds, keep=None):
     def scale_of(group):
-        marks = [marks_of(kinds, n, 0, 128) for n in range(group * GROUP, (group + 1) * GROUP)]
+        marks = [marks_of(spread(kinds)(n), 0, 128) for n in range(group * GROUP, (group + 1) * GROUP)]
         scale = dot(jnp.concatenate(marks, axis=0), weights)
         if keep is not None:
-            keep[group] = scale.astype(BF)
+            keep[group] = scale
         return scale
 
     return scale_of
 
 
 def kept_scale(kept):
-    return lambda group: kept[group].astype(F32)
+    return lambda group: kept[group]
 
 
 def normalize(points, conv, gain, bias):
@@ -176,14 +190,15 @@
     return jnp.concatenate([conv_weight.astype(F32), fill], axis=0).astype(BF)
 
 
-def projection(qkv_weight):
+def projected(rows, qkv_weight):
     q, k, v = (qkv_weight[t] for t in range(3))
-    return jnp.concatenate([q, k, v, jnp.zeros(q.shape, BF)], axis=0)
-
-
-def projected(rows, qkv_weight):
-    value = dot_t(rows, projection(qkv_weight))
-    return jnp.where(iota(value.shape, 1) == value.shape[1] - 64, 1.0, value).astype(BF)
+    none = jnp.zeros(q.shape, BF)
+    near = dot_t(rows, jnp.concatenate([q, k, v, none], axis=0))
+    far = dot_t(rows, jnp.concatenate([k, q, none, v], axis=0))
+    lane = iota(near.shape, 1)
+    near = jnp.where(lane >= 192, 1.0, near)
+    far = jnp.where((lane >= 128) & (lane < 192), 1.0, far)
+    return near.astype(BF), far.astype(BF)
 
 
 def front_inner(
@@ -202,6 +217,8 @@
     partial,
     top_scale,
     end_scale,
+    top_code,
+    end_code,
     normed,
     place_inner,
 ):
@@ -250,7 +267,8 @@
         rows = slice(block * ROWS, (block + 1) * ROWS)
         window = points[block * ROWS - G : (block + 1) * ROWS + G, :]
         conv = windowed_sum(
-            codes(offsets[:, rows]),
+            spread(codes(offsets[:, rows])),
+            offsets.shape[0],
             0,
             window,
             scale_by(weights, columns(kinds[:, rows])),
@@ -262,28 +280,30 @@
         normed[out, :] = nor
     last = total - ROWS
     partial[0:ROWS, :] = windowed_sum(
-        codes(offsets[:, :ROWS]),
+        spread(codes(offsets[:, :ROWS]), top_code),
+        offsets.shape[0],
         G,
         points[0 : ROWS + G, :],
         scale_by(weights, columns(kinds[:, :ROWS]), top_scale),
         pieces[2 * share : 3 * share],
     )
     partial[ROWS:, :] = windowed_sum(
-        codes(offsets[:, last:]),
+        spread(codes(offsets[:, last:]), end_code),
+        offsets.shape[0],
         0,
         points[last - G :, :],
         scale_by(weights, columns(kinds[:, last:]), end_scale),
         pieces[3 * share :],
     )
-    base[...] = dot(place_inner[...], projected(normed[...], qkv_weight)).astype(BF)
+    near, far = projected(normed[...], qkv_weight)
+    base[:slots, :] = dot(place_inner[:slots, :], near).astype(BF)
+    base[slots:, :] = dot(place_inner[slots:, :], far).astype(BF)
 
 
 def front_edges(
     got_first,
     got_second,
     points,
-    offsets,
-    kinds,
     conv_weight,
     gain,
     bias,
@@ -293,6 +313,8 @@
     partial,
     top_scale,
     end_scale,
+    top_code,
+    end_code,
     residual,
     out,
     extra_res,
@@ -308,12 +330,13 @@
     below = jnp.where(even, one, two)
     facts = below[G + LEAD :, :128]
     conv = partial[0:ROWS, :] + windowed_sum(
-        codes(offsets[:, :ROWS]), 0, above, kept_scale(top_scale)
+        lambda n: top_code[n], top_code.shape[0], 0, above, kept_scale(top_scale)
     )
     res, top = normalize(points[0:ROWS, :], conv, gain[...], bias[...])
     residual[0:ROWS, :] = res
     conv = partial[ROWS:, :] + windowed_sum(
-        codes(offsets[:, last:]),
+        lambda n: end_code[n],
+        end_code.shape[0],
         ROWS + G,
         below[:G].astype(BF),
         kept_scale(end_scale),
@@ -321,23 +344,24 @@
     res, end = normalize(points[last:, :], conv, gain[...], bias[...])
     residual[ROWS:, :] = res
     slots = out.shape[0]
-    placed = dot(place[...], projected(jnp.concatenate([top, end], axis=0), qkv_weight)) + base[...].astype(F32)
-    near_half, far_half = placed[:slots], placed[slots:]
-    lane = iota((slots, 128), 1)
-    near_moved, far_moved = swap_halves(near_half[:, :128]), swap_halves(far_half[:, :128])
-    query = jnp.where(lane < 64, near_half[:, :128], far_moved)
-    live = jnp.where(lane < 64, near_half[:, 192:193], far_half[:, 192:193])
-    out[:, 0:128] = jnp.where(live > 0.5, query, DEAD).astype(BF)
-    out[:, 128:256] = jnp.where(lane < 64, near_moved, far_half[:, :128]).astype(BF)
-    out[:, 256:] = jnp.where(lane < 64, near_half[:, 128:], swap_halves(far_half[:, 128:])).astype(BF)
-    near = offsets.shape[0]
+    near, far = projected(jnp.concatenate([top, end], axis=0), qkv_weight)
+    near_half = dot(place[:slots, :], near) + base[:slots, :].astype(F32)
+    far_half = dot(place[slots:, :], far) + base[slots:, :].astype(F32)
+    left = iota((slots, 128), 1) < 64
+    out[:, 0:128] = jnp.where(left, near_half[:, :128], far_half[:, :128]).astype(BF)
+    key = jnp.where(left, far_half[:, :128], near_half[:, :128])
+    live = jnp.where(left, far_half[:, 128:], near_half[:, 128:])
+    out[:, 128:256] = jnp.where(live > 0.5, key, DEAD).astype(BF)
+    out[:, 256:] = jnp.where(left, near_half[:, 128:], far_half[:, 128:]).astype(BF)
+
+    near = top_code.shape[0]
     padded = jnp.concatenate([facts, jnp.zeros((EXTRA - LEAD, 128), F32)], axis=0)
     code = padded[:, :near] + jnp.where(iota((EXTRA, near), 0) < LEAD, iota((EXTRA, near), 0), 0).astype(F32)
     reach = below[: G + LEAD]
     fill = jnp.zeros((256 - G - LEAD, width), F32)
     window = jnp.concatenate([points[last:, :], jnp.concatenate([reach, fill], axis=0).astype(BF)], axis=0)
     more = jnp.concatenate([reach[:LEAD], jnp.zeros((EXTRA - LEAD, width), F32)], axis=0)
-    conv = windowed_sum(code, 0, window, scale_by(weights, padded[:, near : 2 * near]))
+    conv = windowed_sum(spread(code), near, 0, window, scale_by(weights, padded[:, near : 2 * near]))
     extra_res[...] = (more + conv).astype(BF)
     full = jnp.concatenate([facts, jnp.zeros((EXTRA - LEAD, 128), F32)], axis=0)
     owner, slot, lead = (full[:, 2 * near + 8 * n : 2 * near + 8 * n + 1] for n in range(3))
@@ -360,14 +384,15 @@
     qs, ks, vs = (swap_halves(x) for x in (q, k, v))
     zero = jnp.zeros((half, 128), F32)
 
-    def dead_bias(x):
-        return jnp.where(x.astype(F32) < 0.1 * DEAD, DEAD, 0.0)
+    def key_rows(kk, flag):
+        kf = kk.astype(F32)
+        bias = jnp.where((lane == 64) & (flag.astype(F32) < 0.1 * DEAD), DEAD, zero)
+        return jnp.where((lane < 64) & (kf > 0.1 * DEAD), kf, bias).astype(BF)
 
     step = 128
     extra = jnp.where(lane == 64, 1.0, zero)
-    for part, (kk, flag) in enumerate(((k, qs), (ks, q))):
-        rows = slice(part * half, (part + 1) * half)
-        keys[rows, :] = jnp.where(lane < 64, kk.astype(F32), jnp.where(lane == 64, dead_bias(flag), 0.0)).astype(BF)
+    keys[:half, :] = key_rows(ks, k)
+    keys[half:, :] = key_rows(k, ks)
 
     def fill_values():
         for part, vv in enumerate((v, vs)):
@@ -443,9 +468,12 @@
     proj_weight,
     pool_weight,
     clusters,
+    block_hbm,
+    pooled_hbm,
+    block,
     block_out,
     pooled,
-    block,
+    sems,
 ):
     channels = gathered.shape[0]
     width = proj_weight.shape[1]
@@ -474,6 +502,11 @@
     channel = lax.axis_index("ch")
     pick = hot(iota((part, width), 1) == iota((part, width), 0) + channel * part)
     block_out[...] = dot_t(pick, full).astype(BF)
+    copies = [
+        pltpu.make_async_copy(block_out, block_hbm, sems.at[0]),
+        pltpu.make_async_copy(pooled, pooled_hbm, sems.at[1]),
+    ]
+    copies[0].start()
     count = pooled.shape[0]
     base = lax.axis_index("pts") * count
     member = jnp.where(iota((count, 2 * points), 0) == clusters[...] - base, 1.0, 0.0)
@@ -485,6 +518,9 @@
     weight = pool_weight[...]
     mean = (dot(upper, weight) + dot(lower, weight)) / number
     pooled[...] = (mean * (1.0 + lax.erf(mean * math.sqrt(0.5))) * 0.5).astype(BF)
+    copies[1].start()
+    for copy in copies:
+        copy.wait()
 
 
 def shape(dims, kind=BF):
@@ -531,7 +567,7 @@
     got_second = lax.ppermute(second, "pts", across)
     slots = nodes * HALF_SLOTS
     inner_rows = total - 2 * ROWS
-    inner_res, base, place, fetch, partial, top_scale, end_scale = call(
+    inner_res, base, place, fetch, partial, top_scale, end_scale, top_code, end_code = call(
         front_inner,
         (
             shape((inner_rows, width)),
@@ -539,8 +575,10 @@
             shape((2 * slots, 2 * ROWS)),
             shape((total, 2 * slots)),
             shape((2 * ROWS, width), F32),
-            shape((entries // GROUP, GROUP * ROWS, width)),
-            shape((entries // GROUP, GROUP * ROWS, width)),
+            shape((entries // GROUP, GROUP * ROWS, width), F32),
+            shape((entries // GROUP, GROUP * ROWS, width), F32),
+            shape((entries, ROWS, 128)),
+            shape((entries, ROWS, 128)),
         ),
         scratch=(pltpu.VMEM((inner_rows, width), BF), pltpu.VMEM((2 * slots, inner_rows), BF)),
         flops=10**9,
@@ -563,8 +601,6 @@
         got_first,
         got_second,
         points,
-        offsets,
-        kinds,
         conv_weight,
         gain,
         bias,
@@ -574,6 +610,8 @@
         partial,
         top_scale,
         end_scale,
+        top_code,
+        end_code,
     )
     arrived = lax.all_to_all(
         packed.reshape(nodes, HALF_SLOTS, 384), "pts", split_axis=0, concat_axis=0, tiled=True
@@ -600,10 +638,16 @@
     block_out, pooled = call(
         finish,
         (shape((width // channels, total)), shape((total // 4, pool_weight.shape[1]))),
-        scratch=(pltpu.VMEM((total, width), BF),),
+        scratch=(
+            pltpu.VMEM((total, width), BF),
+            pltpu.VMEM((width // channels, total), BF),
+            pltpu.VMEM((total // 4, pool_weight.shape[1]), BF),
+            pltpu.SemaphoreType.DMA((2,)),
+        ),
         flops=10**8,
         nbytes=10**6,
         name="finish",
+        out_space=pltpu.HBM,
     )(gathered, edge_res, inner_res, extra_res, extra_lead, proj_weight, pool_weight, clusters_here)
     return jnp.transpose(block_out), pooled
 

time: 83.5 us -> 83.2 us (level)
  no operation moved by 1% of the time
where the time goes in v7:
time: 83.2 us; the launch traced here: 83 us
  blocking collectives  59.4 us (71%)
  Pallas kernels  11.8 us (14%)
  starting transfers between devices  10.7 us (13%)
    all_to_all x1, blocking collectives, shards(): lax.all_to_all(packed.reshape(nodes, HALF_SLOTS, 384), 'pts', split_axis=...  30.3 us
    all_to_all x1, blocking collectives, shards(): lax.all_to_all(attended.reshape(nodes, 2, 384), 'pts', split_axis=0, conc...  19.1 us
    pallas_call x6, Pallas kernels, run(): pl.pallas_call(body, out_shape=outs, in_specs=[pl.BlockSpec(memory_space=...  11.8 us
    all_to_all x1, blocking collectives, shards(): lax.all_to_all(rows, 'ch', split_axis=0, concat_axis=0, tiled=True)  10.1 us
    ppermute x1, starting transfers between devices, shards(): got_first = lax.ppermute(first, 'pts', inside)  8.75 us
    ppermute x1, starting transfers between devices, shards(): got_second = lax.ppermute(second, 'pts', across)  1.92 us
  transfers between devices with their start and end apart: 2, of which 0 were waited for; matrix products, arithmetic and copies ran while one was open for 0% of the time, Pallas kernels for 5%

profile of v7, /device:TPU:1, one launch (start us, length us, event | category | flops | bytes accessed | tf_op | source)
XLA Modules:
  0.0 83.0 jit_solution(17286364436236460616)
XLA Ops:
  0.6 1.3 %stage.1 = (bf16[512,256]{1,0:T(8,128)(2,1)S(1)}, s32[16,512]{1,0:T(8,128)S(1)}, s32[16,512]{1,0:T(8,128)S(1)}, s32[1,512]{1,0:T(1,128)S(1)}, bf16[27,256]{1,0:T...) custom-call(bf16[512,256]{1,0:T(8,128)(2,1)} %refs_0_.1, ...), custom_call_target="tpu_custom_call" | custom-call | tf_op jit(solution)/shard_map/stage/pallas_call | solution.py:105
  1.9 8.7 %collective-permute-start = (bf16[144,256]{1,0:T(8,128)(2,1)S(1)}, bf16[144,256]{1,0:T(8,128)(2,1)S(1)}, u32[]{:S(2)}, u32[]{:S(2)}) collective-permute-start(bf16[144,256]{1,0:T(8,128)(2,1)S(1)} %get-tuple-element.31), channel_id=1, source_target_pairs={{0,4},{4,0},{8,12},{12,8},{16,20},{20,16},{24,28},{28,24},{32,36},... | collective-permute-start | bytes 221192 | tf_op jit(solution)/shard_map/ppermute | solution.py:566
  10.7 1.9 %collective-permute-start.1 = (bf16[144,256]{1,0:T(8,128)(2,1)S(1)}, bf16[144,256]{1,0:T(8,128)(2,1)S(1)}, u32[]{:S(2)}, u32[]{:S(2)}) collective-permute-start(bf16[144,256]{1,0:T(8,128)(2,1)S(1)} %get-tuple-element.32), channel_id=1, source_target_pairs={{4,8},{8,4},{12,16},{16,12},{20,24},{24,20},{28,32},{32,28},{36,40... | collective-permute-start | bytes 221192 | tf_op jit(solution)/shard_map/ppermute | solution.py:567
  12.6 3.9 %front_inner.1 = (bf16[256,256]{1,0:T(8,128)(2,1)S(1)}, bf16[1024,256]{1,0:T(8,128)(2,1)S(1)}, bf16[1024,256]{1,0:T(8,128)(2,1)S(1)}, bf16[512,1024]{1,0:T(8,128...) custom-call(bf16[512,256]{1,0:T(8,128)(2,1)S(1)} %get-tuple-element., ...), custom_call_target="tpu_custom_call" | custom-call | flops 1000000000 | bytes 4000000 | tf_op jit(solution)/shard_map/front_inner/pallas_call | solution.py:27
  16.5 0.0 collective-permute-done.got_first
  16.5 0.0 collective-permute-done.1.got_second
  16.5 1.7 %front_edges.1 = (bf16[256,256]{1,0:T(8,128)(2,1)S(1)}, bf16[512,384]{1,0:T(8,128)(2,1)S(1)}, bf16[16,256]{1,0:T(8,128)(2,1)S(1)}, bf16[16,512]{1,0:T(8,128)(2,1)S(1)}, f32[16,128]{1,0:T(8,128)S(1)}) custom-call(bf16[144,256]{1,0:T(8,128)(2,1)S(1)} %collective-permute-done.got_first, bf16[144,256]{1,0:T(8,128)(2,1)S(1)} %collective-permute-done.1.got_second, ...), custom_call_target="tpu_custom_call" | custom-call | flops 1000000000 | bytes 4000000 | tf_op jit(solution)/shard_map/front_edges/pallas_call | solution.py:27
  18.2 0.1 reshape.32
  18.3 30.3 %all_to_all.15 = bf16[128,4,384]{2,1,0:T(4,128)(2,1)S(1)} all-to-all(bf16[128,4,384]{2,1,0:T(4,128)(2,1)S(1)} %reshape.32), channel_id=1, replica_groups=mesh['pts'=128,'ch'=4] {'pts'}, dimensions={0} | all-to-all | bytes 786432 | tf_op jit(solution)/shard_map/all_to_all | solution.py:616
  48.6 0.1 reshape.33.packed
  48.7 3.1 %attend.1 = bf16[256,384]{1,0:T(8,128)(2,1)S(1)} custom-call(bf16[512,384]{1,0:T(8,128)(2,1)S(1)} %reshape.33.packed), custom_call_target="tpu_custom_call" | custom-call | flops 1000000000 | bytes 1000000 | tf_op jit(solution)/shard_map/attend/pallas_call | solution.py:27
  51.8 0.1 reshape.34
  51.9 19.1 %all_to_all.16 = bf16[128,2,384]{2,1,0:T(2,128)(2,1)S(1)} all-to-all(bf16[128,2,384]{2,1,0:T(2,128)(2,1)S(1)} %reshape.34), channel_id=1, replica_groups=mesh['pts'=128,'ch'=4] {'pts'}, dimensions={0} | all-to-all | bytes 393216 | tf_op jit(solution)/shard_map/all_to_all | solution.py:631
  71.0 0.1 reshape.35.returned
  71.0 0.5 fetch_rows.1
  71.6 10.1 %all_to_all.17.gathered = bf16[4,272,128]{2,1,0:T(8,128)(2,1)S(1)} all-to-all(bf16[4,272,128]{2,1,0:T(8,128)(2,1)S(1)} %fetch_rows.1), channel_id=1, replica_groups=mesh['pts'=128,'ch'=4] {'ch'}, dimensions={0} | all-to-all | bytes 557056 | tf_op jit(solution)/shard_map/all_to_all | solution.py:637
  81.6 1.3 %finish.1 = (bf16[64,512]{1,0:T(8,128)(2,1)}, bf16[128,128]{1,0:T(8,128)(2,1)}) custom-call(bf16[4,272,128]{2,1,0:T(8,128)(2,1)S(1)} %all_to_all.17.gathered, bf16[256,256]{1,0:T(8,128)(2,1)S(1)} %get-tuple-element.51.edge_res, bf16[256,256]{1,0:T(8,128)(2,1)S(1)} %get-tuple-element.52.inner_res, bf16[16,256]{1,0:T(8,128)(2,1)S(1)} %get-tuple-element.53.extra_res, ...), custom_call_target="tpu_custom_call" | custom-call | flops 100000000 | bytes 1000000 | tf_op jit(solution)/shard_map/finish/pallas_call | solution.py:27
Async XLA Ops:
  1.9 14.6 %collective-permute-start = (bf16[144,256]{1,0:T(8,128)(2,1)S(1)}, bf16[144,256]{1,0:T(8,128)(2,1)S(1)}, u32[]{:S(2)}, u32[]{:S(2)}) collective-permute-start(bf16[144,256]{1,0:T(8,128)(2,1)S(1)} %get-tuple-element.31), channel_id=1, source_target_pairs={{0,4},{4,0},{8,12},{12,8},{16,20},{20,16},{24,28},{28,24},{32,36},... | collective-permute-start | bytes 221192 | tf_op jit(solution)/shard_map/ppermute | solution.py:566
  10.7 5.8 %collective-permute-start.1 = (bf16[144,256]{1,0:T(8,128)(2,1)S(1)}, bf16[144,256]{1,0:T(8,128)(2,1)S(1)}, u32[]{:S(2)}, u32[]{:S(2)}) collective-permute-start(bf16[144,256]{1,0:T(8,128)(2,1)S(1)} %get-tuple-element.32), channel_id=1, source_target_pairs={{4,8},{8,4},{12,16},{16,12},{20,24},{24,20},{28,32},{32,28},{36,40... | collective-permute-start | bytes 221192 | tf_op jit(solution)/shard_map/ppermute | solution.py:567

commit v8 on v7

--- a/solution.py
+++ b/solution.py
@@ -377,39 +377,44 @@
 
 def attend(packed, out, keys, values, kept):
     half = packed.shape[0]
-    lane = iota((half, 128), 1)
+    step = 128
     q = packed[:, 0:128]
     k = packed[:, 128:256]
     v = packed[:, 256:384]
     qs, ks, vs = (swap_halves(x) for x in (q, k, v))
-    zero = jnp.zeros((half, 128), F32)
+
+    def lanes(rows):
+        return iota((rows, 128), 1).astype(F32).astype(BF)
+
+    def full(value, like):
+        return jnp.full(like.shape, value, BF)
+
+    lane = lanes(half)
+    zero = full(0.0, lane)
+    extra = jnp.where(lane == full(64, lane), full(1.0, lane), zero)
+    low = lane < full(64, lane)
 
     def key_rows(kk, flag):
-        kf = kk.astype(F32)
-        bias = jnp.where((lane == 64) & (flag.astype(F32) < 0.1 * DEAD), DEAD, zero)
-        return jnp.where((lane < 64) & (kf > 0.1 * DEAD), kf, bias).astype(BF)
-
-    step = 128
-    extra = jnp.where(lane == 64, 1.0, zero)
+        alive = jnp.where(kk > full(0.1 * DEAD, lane), kk, zero)
+        bias = jnp.where(flag < full(0.1 * DEAD, lane), full(DEAD, lane), zero)
+        return jnp.where(low, alive, jnp.where(lane == full(64, lane), bias, zero))
+
     keys[:half, :] = key_rows(ks, k)
     keys[half:, :] = key_rows(k, ks)
 
     def fill_values():
-        for part, vv in enumerate((v, vs)):
-            rows = slice(part * half, (part + 1) * half)
-            values[rows, :] = jnp.where(lane < 64, vv.astype(F32), extra).astype(BF)
+        values[:half, :] = jnp.where(low, v, extra)
+        values[half:, :] = jnp.where(low, vs, extra)
 
     factor = math.log2(math.e) / math.sqrt(HD)
     block_lane = iota((step, 128), 1)
 
     def scores_of(chunk):
         rows = slice((chunk // 2) * step, (chunk // 2 + 1) * step)
-        mine = (q, qs)[chunk % 2][rows].astype(F32)
-        pair = []
-        for head in range(2):
-            inside = (block_lane >= head * HD) & (block_lane < (head + 1) * HD)
-            pair.append(jnp.where(inside, mine, extra[:step]).astype(BF))
-        return dot_t(jnp.concatenate(pair, axis=0), keys[...])
+        mine, here = (q, qs)[chunk % 2][rows], lanes(step)
+        first = jnp.where(here < full(HD, here), mine, extra[:step])
+        second = jnp.where(here < full(HD, here), full(0.0, here), jnp.where(here < full(2 * HD, here), mine, extra[:step]))
+        return dot_t(jnp.concatenate([first, second], axis=0), keys[...])
 
     def attended_of(scores):
         top = jnp.max(scores, axis=1, keepdims=True)
@@ -417,6 +422,19 @@
         summed = dot(soft, values[...])
         result = summed / summed[:, 64:65]
         return jnp.where(block_lane < HD, result[:step], result[step:])
+
+    pairs = step // 2
+
+    def store_own(block):
+        rows = slice(block * pairs, (block + 1) * pairs)
+        out[rows, :128] = kept[pl.ds(block * step, pairs, stride=2), :].astype(BF)
+        out[rows, 128:256] = kept[pl.ds(block * step + 1, pairs, stride=2), :].astype(BF)
+
+    def store_next(block):
+        near = kept[pl.ds(block * step + HALF_SLOTS, pairs, stride=2), :]
+        far = kept[pl.ds(block * step + HALF_SLOTS + 1, pairs, stride=2), :]
+        rows = slice(block * pairs, (block + 1) * pairs)
+        out[rows, 256:] = jnp.where(iota((pairs, 128), 1) < 64, near, swap_halves(far)).astype(BF)
 
     chunks = 2 * half // step
     ahead = [scores_of(0)]
@@ -433,13 +451,11 @@
             rows = slice((chunk // 2) * step, (chunk // 2 + 1) * step)
             both = jnp.where(block_lane < 64, first, moved)
             kept[rows, :] = both
+            store_own(chunk // 2)
+            if chunk > 2:
+                store_next(chunk // 2 - 1)
     kept[half:, :] = jnp.zeros((8, 128), F32)
-    pairs = half // 2
-    lane = iota((pairs, 128), 1)
-    out[:, :128] = kept[pl.ds(0, pairs, stride=2), :].astype(BF)
-    out[:, 128:256] = kept[pl.ds(1, pairs, stride=2), :].astype(BF)
-    near, far = kept[pl.ds(HALF_SLOTS, pairs, stride=2), :], kept[pl.ds(HALF_SLOTS + 1, pairs, stride=2), :]
-    out[:, 256:] = jnp.where(lane < 64, near, swap_halves(far)).astype(BF)
+    store_next(half // step - 1)
 
 
 def fetch_rows(returned, fetch, extra_fetch, out):
@@ -563,8 +579,8 @@
     staged = stage(len(args))(*args)
     points, offsets, kinds, own, conv_weight, gain, bias, qkv_weight, proj_weight, pool_weight = staged[:10]
     clusters_here, first, second = staged[10:]
+    got_second = lax.ppermute(second, "pts", across)
     got_first = lax.ppermute(first, "pts", inside)
-    got_second = lax.ppermute(second, "pts", across)
     slots = nodes * HALF_SLOTS
     inner_rows = total - 2 * ROWS
     inner_res, base, place, fetch, partial, top_scale, end_scale, top_code, end_code = call(

time: 83.2 us -> 83.3 us (level)
  no operation moved by 1% of the time
where the time goes in v8:
time: 83.3 us; the launch traced here: 83 us
  blocking collectives  59.4 us (71%)
  Pallas kernels  11.8 us (14%)
  starting transfers between devices  10.7 us (13%)
    all_to_all x1, blocking collectives, shards(): lax.all_to_all(packed.reshape(nodes, HALF_SLOTS, 384), 'pts', split_axis=...  30.3 us
    all_to_all x1, blocking collectives, shards(): lax.all_to_all(attended.reshape(nodes, 2, 384), 'pts', split_axis=0, conc...  19.1 us
    pallas_call x6, Pallas kernels, run(): pl.pallas_call(body, out_shape=outs, in_specs=[pl.BlockSpec(memory_space=...  11.8 us
    all_to_all x1, blocking collectives, shards(): lax.all_to_all(rows, 'ch', split_axis=0, concat_axis=0, tiled=True)  10.1 us
    ppermute x1, starting transfers between devices, shards(): got_first = lax.ppermute(first, 'pts', inside)  8.75 us
    ppermute x1, starting transfers between devices, shards(): got_second = lax.ppermute(second, 'pts', across)  1.92 us
  transfers between devices with their start and end apart: 2, of which 0 were waited for; matrix products, arithmetic and copies ran while one was open for 0% of the time, Pallas kernels for 5%

profile of v8, /device:TPU:1, one launch (start us, length us, event | category | flops | bytes accessed | tf_op | source)
XLA Modules:
  0.0 83.0 jit_solution(4160669051081593103)
XLA Ops:
  0.6 1.3 %stage.1 = (bf16[512,256]{1,0:T(8,128)(2,1)S(1)}, s32[16,512]{1,0:T(8,128)S(1)}, s32[16,512]{1,0:T(8,128)S(1)}, s32[1,512]{1,0:T(1,128)S(1)}, bf16[27,256]{1,0:T...) custom-call(bf16[512,256]{1,0:T(8,128)(2,1)} %refs_0_.1, ...), custom_call_target="tpu_custom_call" | custom-call | tf_op jit(solution)/shard_map/stage/pallas_call | solution.py:105
  1.9 8.7 %collective-permute-start = (bf16[144,256]{1,0:T(8,128)(2,1)S(1)}, bf16[144,256]{1,0:T(8,128)(2,1)S(1)}, u32[]{:S(2)}, u32[]{:S(2)}) collective-permute-start(bf16[144,256]{1,0:T(8,128)(2,1)S(1)} %get-tuple-element.31), channel_id=1, source_target_pairs={{0,4},{4,0},{8,12},{12,8},{16,20},{20,16},{24,28},{28,24},{32,36},... | collective-permute-start | bytes 221192 | tf_op jit(solution)/shard_map/ppermute | solution.py:583
  10.7 1.9 %collective-permute-start.1 = (bf16[144,256]{1,0:T(8,128)(2,1)S(1)}, bf16[144,256]{1,0:T(8,128)(2,1)S(1)}, u32[]{:S(2)}, u32[]{:S(2)}) collective-permute-start(bf16[144,256]{1,0:T(8,128)(2,1)S(1)} %get-tuple-element.32), channel_id=1, source_target_pairs={{4,8},{8,4},{12,16},{16,12},{20,24},{24,20},{28,32},{32,28},{36,40... | collective-permute-start | bytes 221192 | tf_op jit(solution)/shard_map/ppermute | solution.py:582
  12.6 3.9 %front_inner.1 = (bf16[256,256]{1,0:T(8,128)(2,1)S(1)}, bf16[1024,256]{1,0:T(8,128)(2,1)S(1)}, bf16[1024,256]{1,0:T(8,128)(2,1)S(1)}, bf16[512,1024]{1,0:T(8,128...) custom-call(bf16[512,256]{1,0:T(8,128)(2,1)S(1)} %get-tuple-element., ...), custom_call_target="tpu_custom_call" | custom-call | flops 1000000000 | bytes 4000000 | tf_op jit(solution)/shard_map/front_inner/pallas_call | solution.py:27
  16.5 0.0 collective-permute-done.got_first
  16.5 0.0 collective-permute-done.1.got_second
  16.5 1.7 %front_edges.1 = (bf16[256,256]{1,0:T(8,128)(2,1)S(1)}, bf16[512,384]{1,0:T(8,128)(2,1)S(1)}, bf16[16,256]{1,0:T(8,128)(2,1)S(1)}, bf16[16,512]{1,0:T(8,128)(2,1)S(1)}, f32[16,128]{1,0:T(8,128)S(1)}) custom-call(bf16[144,256]{1,0:T(8,128)(2,1)S(1)} %collective-permute-done.got_first, bf16[144,256]{1,0:T(8,128)(2,1)S(1)} %collective-permute-done.1.got_second, ...), custom_call_target="tpu_custom_call" | custom-call | flops 1000000000 | bytes 4000000 | tf_op jit(solution)/shard_map/front_edges/pallas_call | solution.py:27
  18.2 0.1 reshape.32
  18.3 30.3 %all_to_all.15 = bf16[128,4,384]{2,1,0:T(4,128)(2,1)S(1)} all-to-all(bf16[128,4,384]{2,1,0:T(4,128)(2,1)S(1)} %reshape.32), channel_id=1, replica_groups=mesh['pts'=128,'ch'=4] {'pts'}, dimensions={0} | all-to-all | bytes 786432 | tf_op jit(solution)/shard_map/all_to_all | solution.py:632
  48.6 0.1 reshape.33.packed
  48.7 3.1 %attend.1 = bf16[256,384]{1,0:T(8,128)(2,1)S(1)} custom-call(bf16[512,384]{1,0:T(8,128)(2,1)S(1)} %reshape.33.packed), custom_call_target="tpu_custom_call" | custom-call | flops 1000000000 | bytes 1000000 | tf_op jit(solution)/shard_map/attend/pallas_call | solution.py:27
  51.8 0.1 reshape.34
  51.9 19.1 %all_to_all.16 = bf16[128,2,384]{2,1,0:T(2,128)(2,1)S(1)} all-to-all(bf16[128,2,384]{2,1,0:T(2,128)(2,1)S(1)} %reshape.34), channel_id=1, replica_groups=mesh['pts'=128,'ch'=4] {'pts'}, dimensions={0} | all-to-all | bytes 393216 | tf_op jit(solution)/shard_map/all_to_all | solution.py:647
  71.0 0.1 reshape.35.returned
  71.1 0.5 fetch_rows.1
  71.6 10.1 %all_to_all.17.gathered = bf16[4,272,128]{2,1,0:T(8,128)(2,1)S(1)} all-to-all(bf16[4,272,128]{2,1,0:T(8,128)(2,1)S(1)} %fetch_rows.1), channel_id=1, replica_groups=mesh['pts'=128,'ch'=4] {'ch'}, dimensions={0} | all-to-all | bytes 557056 | tf_op jit(solution)/shard_map/all_to_all | solution.py:653
  81.6 1.3 %finish.1 = (bf16[64,512]{1,0:T(8,128)(2,1)}, bf16[128,128]{1,0:T(8,128)(2,1)}) custom-call(bf16[4,272,128]{2,1,0:T(8,128)(2,1)S(1)} %all_to_all.17.gathered, bf16[256,256]{1,0:T(8,128)(2,1)S(1)} %get-tuple-element.51.edge_res, bf16[256,256]{1,0:T(8,128)(2,1)S(1)} %get-tuple-element.52.inner_res, bf16[16,256]{1,0:T(8,128)(2,1)S(1)} %get-tuple-element.53.extra_res, ...), custom_call_target="tpu_custom_call" | custom-call | flops 100000000 | bytes 1000000 | tf_op jit(solution)/shard_map/finish/pallas_call | solution.py:27
Async XLA Ops:
  1.9 14.6 %collective-permute-start = (bf16[144,256]{1,0:T(8,128)(2,1)S(1)}, bf16[144,256]{1,0:T(8,128)(2,1)S(1)}, u32[]{:S(2)}, u32[]{:S(2)}) collective-permute-start(bf16[144,256]{1,0:T(8,128)(2,1)S(1)} %get-tuple-element.31), channel_id=1, source_target_pairs={{0,4},{4,0},{8,12},{12,8},{16,20},{20,16},{24,28},{28,24},{32,36},... | collective-permute-start | bytes 221192 | tf_op jit(solution)/shard_map/ppermute | solution.py:583
  10.7 5.8 %collective-permute-start.1 = (bf16[144,256]{1,0:T(8,128)(2,1)S(1)}, bf16[144,256]{1,0:T(8,128)(2,1)S(1)}, u32[]{:S(2)}, u32[]{:S(2)}) collective-permute-start(bf16[144,256]{1,0:T(8,128)(2,1)S(1)} %get-tuple-element.32), channel_id=1, source_target_pairs={{4,8},{8,4},{12,16},{16,12},{20,24},{24,20},{28,32},{32,28},{36,40... | collective-permute-start | bytes 221192 | tf_op jit(solution)/shard_map/ppermute | solution.py:582

commit v9 on v8

--- a/solution.py
+++ b/solution.py
@@ -7,6 +7,7 @@
 from jax.experimental import pallas as pl
 from jax.experimental.pallas import tpu as pltpu
 from jax.sharding import PartitionSpec as P
+
 
 HD = 32
 G = 128
@@ -22,7 +23,7 @@
 VMEM_BYTES = 24 * 1024 * 1024
 
 
-def call(body, outs, scratch=(), flops=0, nbytes=0, name=None, out_space=pltpu.VMEM):
+def call(body, outs, scratch=(), flops=0, nbytes=0, out_space=pltpu.VMEM):
     def run(*args):
         return pl.pallas_call(
             body,
@@ -32,7 +33,6 @@
             scratch_shapes=list(scratch),
             compiler_params=pltpu.CompilerParams(vmem_limit_bytes=VMEM_BYTES),
             cost_estimate=pl.CostEstimate(flops=flops, bytes_accessed=nbytes, transcendentals=0),
-            name=name,
         )(*args)
 
     return run
@@ -599,7 +599,6 @@
         scratch=(pltpu.VMEM((inner_rows, width), BF), pltpu.VMEM((2 * slots, inner_rows), BF)),
         flops=10**9,
         nbytes=4 * 10**6,
-        name="front_inner",
     )(points, offsets, kinds, own, conv_weight, gain, bias, qkv_weight)
     edge_res, packed, extra_res, extra_fetch, extra_lead = call(
         front_edges,
@@ -612,7 +611,6 @@
         ),
         flops=10**9,
         nbytes=4 * 10**6,
-        name="front_edges",
     )(
         got_first,
         got_second,
@@ -642,13 +640,12 @@
         ),
         flops=10**9,
         nbytes=10**6,
-        name="attend",
     )(arrived)
     returned = lax.all_to_all(
         attended.reshape(nodes, 2, 384), "pts", split_axis=0, concat_axis=0, tiled=True
     ).reshape(slots // 2, 384)
     rows = call(
-        fetch_rows, shape((channels, total // 2 + EXTRA, 128)), flops=10**8, nbytes=10**6, name="fetch_rows"
+        fetch_rows, shape((channels, total // 2 + EXTRA, 128)), flops=10**8, nbytes=10**6
     )(returned, fetch, extra_fetch)
     gathered = lax.all_to_all(rows, "ch", split_axis=0, concat_axis=0, tiled=True)
     block_out, pooled = call(
@@ -662,7 +659,6 @@
         ),
         flops=10**8,
         nbytes=10**6,
-        name="finish",
         out_space=pltpu.HBM,
     )(gathered, edge_res, inner_res, extra_res, extra_lead, proj_weight, pool_weight, clusters_here)
     return jnp.transpose(block_out), pooled

time: 83.3 us -> 83.3 us (level)
  no operation moved by 1% of the time
where the time goes in v9:
time: 83.3 us; the launch traced here: 83 us
  blocking collectives  59.4 us (71%)
  Pallas kernels  11.8 us (14%)
  starting transfers between devices  10.7 us (13%)
    all_to_all x1, blocking collectives, shards(): lax.all_to_all(packed.reshape(nodes, HALF_SLOTS, 384), 'pts', split_axis=...  30.3 us
    all_to_all x1, blocking collectives, shards(): lax.all_to_all(attended.reshape(nodes, 2, 384), 'pts', split_axis=0, conc...  19.1 us
    pallas_call x6, Pallas kernels, run(): pl.pallas_call(body, out_shape=outs, in_specs=[pl.BlockSpec(memory_space=...  11.8 us
    all_to_all x1, blocking collectives, shards(): lax.all_to_all(rows, 'ch', split_axis=0, concat_axis=0, tiled=True)  10.1 us
    ppermute x1, starting transfers between devices, shards(): got_first = lax.ppermute(first, 'pts', inside)  8.75 us
    ppermute x1, starting transfers between devices, shards(): got_second = lax.ppermute(second, 'pts', across)  1.92 us
  transfers between devices with their start and end apart: 2, of which 0 were waited for; matrix products, arithmetic and copies ran while one was open for 0% of the time, Pallas kernels for 5%

profile of v9, /device:TPU:1, one launch (start us, length us, event | category | flops | bytes accessed | tf_op | source)
XLA Modules:
  0.0 83.0 jit_solution(4160669051081593103)
XLA Ops:
  0.6 1.3 %stage.1 = (bf16[512,256]{1,0:T(8,128)(2,1)S(1)}, s32[16,512]{1,0:T(8,128)S(1)}, s32[16,512]{1,0:T(8,128)S(1)}, s32[1,512]{1,0:T(1,128)S(1)}, bf16[27,256]{1,0:T...) custom-call(bf16[512,256]{1,0:T(8,128)(2,1)} %refs_0_.1, ...), custom_call_target="tpu_custom_call" | custom-call | tf_op jit(solution)/shard_map/stage/pallas_call | solution.py:105
  1.9 8.7 %collective-permute-start = (bf16[144,256]{1,0:T(8,128)(2,1)S(1)}, bf16[144,256]{1,0:T(8,128)(2,1)S(1)}, u32[]{:S(2)}, u32[]{:S(2)}) collective-permute-start(bf16[144,256]{1,0:T(8,128)(2,1)S(1)} %get-tuple-element.31), channel_id=1, source_target_pairs={{0,4},{4,0},{8,12},{12,8},{16,20},{20,16},{24,28},{28,24},{32,36},... | collective-permute-start | bytes 221192 | tf_op jit(solution)/shard_map/ppermute | solution.py:583
  10.7 1.9 %collective-permute-start.1 = (bf16[144,256]{1,0:T(8,128)(2,1)S(1)}, bf16[144,256]{1,0:T(8,128)(2,1)S(1)}, u32[]{:S(2)}, u32[]{:S(2)}) collective-permute-start(bf16[144,256]{1,0:T(8,128)(2,1)S(1)} %get-tuple-element.32), channel_id=1, source_target_pairs={{4,8},{8,4},{12,16},{16,12},{20,24},{24,20},{28,32},{32,28},{36,40... | collective-permute-start | bytes 221192 | tf_op jit(solution)/shard_map/ppermute | solution.py:582
  12.6 3.9 %shard_map.122 = (bf16[256,256]{1,0:T(8,128)(2,1)S(1)}, bf16[1024,256]{1,0:T(8,128)(2,1)S(1)}, bf16[1024,256]{1,0:T(8,128)(2,1)S(1)}, bf16[512,1024]{1,0:T(8,128...) custom-call(bf16[512,256]{1,0:T(8,128)(2,1)S(1)} %get-tuple-element., ...), custom_call_target="tpu_custom_call" | custom-call | flops 1000000000 | bytes 4000000 | tf_op jit(solution)/shard_map/pallas_call | solution.py:28
  16.5 0.0 collective-permute-done.got_first
  16.5 0.0 collective-permute-done.1.got_second
  16.5 1.7 %shard_map.123 = (bf16[256,256]{1,0:T(8,128)(2,1)S(1)}, bf16[512,384]{1,0:T(8,128)(2,1)S(1)}, bf16[16,256]{1,0:T(8,128)(2,1)S(1)}, bf16[16,512]{1,0:T(8,128)(2,1)S(1)}, f32[16,128]{1,0:T(8,128)S(1)}) custom-call(bf16[144,256]{1,0:T(8,128)(2,1)S(1)} %collective-permute-done.got_first, bf16[144,256]{1,0:T(8,128)(2,1)S(1)} %collective-permute-done.1.got_second, ...), custom_call_target="tpu_custom_call" | custom-call | flops 1000000000 | bytes 4000000 | tf_op jit(solution)/shard_map/pallas_call | solution.py:28
  18.2 0.1 reshape.32
  18.3 30.3 %all_to_all.15 = bf16[128,4,384]{2,1,0:T(4,128)(2,1)S(1)} all-to-all(bf16[128,4,384]{2,1,0:T(4,128)(2,1)S(1)} %reshape.32), channel_id=1, replica_groups=mesh['pts'=128,'ch'=4] {'pts'}, dimensions={0} | all-to-all | bytes 786432 | tf_op jit(solution)/shard_map/all_to_all | solution.py:630
  48.6 0.1 reshape.33.packed
  48.7 3.1 %shard_map.124 = bf16[256,384]{1,0:T(8,128)(2,1)S(1)} custom-call(bf16[512,384]{1,0:T(8,128)(2,1)S(1)} %reshape.33.packed), custom_call_target="tpu_custom_call" | custom-call | flops 1000000000 | bytes 1000000 | tf_op jit(solution)/shard_map/pallas_call | solution.py:28
  51.8 0.1 reshape.34
  51.9 19.1 %all_to_all.16 = bf16[128,2,384]{2,1,0:T(2,128)(2,1)S(1)} all-to-all(bf16[128,2,384]{2,1,0:T(2,128)(2,1)S(1)} %reshape.34), channel_id=1, replica_groups=mesh['pts'=128,'ch'=4] {'pts'}, dimensions={0} | all-to-all | bytes 393216 | tf_op jit(solution)/shard_map/all_to_all | solution.py:644
  71.0 0.1 reshape.35.returned
  71.1 0.5 shard_map.125
  71.6 10.1 %all_to_all.17.gathered = bf16[4,272,128]{2,1,0:T(8,128)(2,1)S(1)} all-to-all(bf16[4,272,128]{2,1,0:T(8,128)(2,1)S(1)} %shard_map.125), channel_id=1, replica_groups=mesh['pts'=128,'ch'=4] {'ch'}, dimensions={0} | all-to-all | bytes 557056 | tf_op jit(solution)/shard_map/all_to_all | solution.py:650
  81.6 1.3 %shard_map.126 = (bf16[64,512]{1,0:T(8,128)(2,1)}, bf16[128,128]{1,0:T(8,128)(2,1)}) custom-call(bf16[4,272,128]{2,1,0:T(8,128)(2,1)S(1)} %all_to_all.17.gathered, bf16[256,256]{1,0:T(8,128)(2,1)S(1)} %get-tuple-element.51.edge_res, bf16[256,256]{1,0:T(8,128)(2,1)S(1)} %get-tuple-element.52.inner_res, bf16[16,256]{1,0:T(8,128)(2,1)S(1)} %get-tuple-element.53.extra_res, ...), custom_call_target="tpu_custom_call" | custom-call | flops 100000000 | bytes 1000000 | tf_op jit(solution)/shard_map/pallas_call | solution.py:28
Async XLA Ops:
  1.9 14.6 %collective-permute-start = (bf16[144,256]{1,0:T(8,128)(2,1)S(1)}, bf16[144,256]{1,0:T(8,128)(2,1)S(1)}, u32[]{:S(2)}, u32[]{:S(2)}) collective-permute-start(bf16[144,256]{1,0:T(8,128)(2,1)S(1)} %get-tuple-element.31), channel_id=1, source_target_pairs={{0,4},{4,0},{8,12},{12,8},{16,20},{20,16},{24,28},{28,24},{32,36},... | collective-permute-start | bytes 221192 | tf_op jit(solution)/shard_map/ppermute | solution.py:583
  10.7 5.8 %collective-permute-start.1 = (bf16[144,256]{1,0:T(8,128)(2,1)S(1)}, bf16[144,256]{1,0:T(8,128)(2,1)S(1)}, u32[]{:S(2)}, u32[]{:S(2)}) collective-permute-start(bf16[144,256]{1,0:T(8,128)(2,1)S(1)} %get-tuple-element.32), channel_id=1, source_target_pairs={{4,8},{8,4},{12,16},{16,12},{20,24},{24,20},{28,32},{32,28},{36,40... | collective-permute-start | bytes 221192 | tf_op jit(solution)/shard_map/ppermute | solution.py:582
